TPU v7x, 32 devices: a whole 2x2x4 slice. The times are simulated.
32 devices in a mesh: dp: 8 (over y, x, core), tensor: 4 (over z).
Axes of the slice: x: 2, y: 2, z: 4, core: 2. Of those that a mesh axis runs over, the one named last changes fastest.
Arguments:
- inputs: bfloat16 [8, 1024, 768], P('dp', 'tensor'), may hold values from -6 to 6
- ln_gain: float32 [768], P(('dp', 'tensor')), may hold values from 0.25 to 1.75
- ln_bias: float32 [768], P(('dp', 'tensor')), may hold values from -1.5 to 1.5
- w_qkv: bfloat16 [768, 3, 768], P('dp', None, 'tensor'), may hold values from -1.5 to 1.5, as said below
- b_qkv: bfloat16 [3, 12, 64], P(None, 'tensor', 'dp'), may hold values from -2.5 to 2.5
- w_out: bfloat16 [768, 768], P('tensor', 'dp'), may hold values from -0.875 to 0.875
- w_in: bfloat16 [768, 3072], P('dp', 'tensor'), may hold values from -0.21875 to 0.21875
- b_in: bfloat16 [24, 128], P('tensor', 'dp'), may hold values from -2.5 to 2.5
- w_down: bfloat16 [3072, 768], P('tensor', 'dp'), may hold values from -0.109375 to 0.109375
- out_bias: float32 [2, 768], P(None, ('dp', 'tensor')), may hold values from -2.5 to 2.5
- cotangent: bfloat16 [8, 1024, 768], P('dp', 'tensor'), may hold values from -6 to 6
Outputs:
- outputs: bfloat16 [8, 1024, 768], P('dp', 'tensor')
- input_grad: bfloat16 [8, 1024, 768], P('dp', 'tensor')
- ln_gain_grad: float32 [768], P(('dp', 'tensor'))
- ln_bias_grad: float32 [768], P(('dp', 'tensor'))
- w_qkv_grad: float32 [768, 3, 768], P('dp', None, 'tensor')
- b_qkv_grad: float32 [3, 12, 64], P(None, 'tensor', 'dp')
- w_out_grad: float32 [768, 768], P('tensor', 'dp')
- w_in_grad: float32 [768, 3072], P('dp', 'tensor')
- b_in_grad: float32 [24, 128], P('tensor', 'dp')
- w_down_grad: float32 [3072, 768], P('tensor', 'dp')
- out_bias_grad: float32 [2, 768], P(None, ('dp', 'tensor'))
Inputs may be any that keep to these rules, and one draw needn't show every extreme that they name: `w_qkv`: projection weights of the queries, keys and values.
All inputs are finite; a program needn't handle non-finite values.
Results may differ from a plain program's by a relative error of at most 0.0082.
Values may be sent and summed in bfloat16 or wider, within the bound.
No kernel may reach another device: no remote copies, remote signals or barrier semaphores. Data moves between devices by JAX's collectives and lax.ppermute only.
A program may use at most 128 MiB of HBM per device.

v0:
```python
import functools
import math

import jax
import jax.numpy as jnp
from jax import lax
from jax.experimental import pallas as pl
from jax.experimental.pallas import tpu as pltpu
from jax.sharding import PartitionSpec as P

ROT = 16
EPS = 1e-05
ROOT_HALF = 0.7071067811865476
INV_ROOT_TAU = 0.3989422804014327
NEG_BIG = -1e30
F32 = jnp.float32
BF16 = jnp.bfloat16


def dot(a, b, contract, out=F32):
    return lax.dot_general(
        a, b, (((contract[0],), (contract[1],)), ((), ())), preferred_element_type=out
    )


def swap(x, axis_name, size, step):
    return lax.ppermute(x, axis_name, [(i, i ^ step) for i in range(size)])


def bit_of(axis_name, step):
    return (lax.axis_index(axis_name) // step) % 2


def gather_bits(x, size, axis, steps):
    done = []
    for step in steps:
        other = swap(x, "dp", size, step)
        mine_first = bit_of("dp", step) == 0
        low = jnp.where(mine_first, x, other)
        high = jnp.where(mine_first, other, x)
        place = axis + sum(1 for s in done if s > step)
        x = jnp.stack([low, high], axis=place)
        done.append(step)
    shape = x.shape
    levels = len(steps)
    return x.reshape(shape[:axis] + (size,) + shape[axis + levels :])


def scatter_bits(x, axis, steps, wire, size, unit):
    shape = x.shape
    levels = len(steps)
    x = x.reshape(shape[:axis] + (2,) * levels + shape[axis + 1 :])
    left = sorted(steps, reverse=True)
    for step in steps:
        place = axis + left.index(step)
        bit = bit_of("dp", step * unit)
        keep = lax.dynamic_index_in_dim(x, bit, place, keepdims=False)
        send = lax.dynamic_index_in_dim(x, 1 - bit, place, keepdims=False)
        got = swap(send.astype(wire), "dp", size, step * unit)
        x = keep + got.astype(F32)
        left.remove(step)
    return x


def rotate_rows(x, cosine, sine):
    half = ROT // 2
    first, second = x[:half], x[half:ROT]
    return jnp.concatenate(
        [first * cosine - second * sine, second * cosine + first * sine, x[ROT:]], axis=0
    )


def normalize(x):
    wide = x.astype(F32)
    centred = wide - jnp.mean(wide, axis=-1, keepdims=True)
    inv_sigma = lax.rsqrt(jnp.mean(centred * centred, axis=-1, keepdims=True) + EPS)
    return centred * inv_sigma, inv_sigma


def enter_kernel(
    heads, head_dim, x_ref, vec_ref, in_bias_ref, qkv_bias_ref, first_ref, second_ref,
    cos_ref, sin_ref, normed_t_ref, proj_t_ref, hidden_ref, slope_ref,
):
    width = heads * head_dim
    hidden_units = hidden_ref.shape[1]
    unit, _ = normalize(x_ref[...])
    wide = unit * vec_ref[0:1] + vec_ref[1:2]
    normed = wide.astype(BF16)
    normed_t_ref[...] = jnp.transpose(normed)
    projected = dot(normed, second_ref[:, hidden_units:], (1, 0)) + qkv_bias_ref[...]
    projected = jnp.transpose(projected)
    cosine, sine = cos_ref[...], sin_ref[...]
    for place in range(2 * heads):
        rows = slice(place * head_dim, (place + 1) * head_dim)
        proj_t_ref[rows] = rotate_rows(projected[rows], cosine, sine).astype(BF16)
    proj_t_ref[2 * width :] = projected[2 * width :].astype(BF16)
    pre_act = dot(normed, first_ref[:, :hidden_units], (1, 0)) + in_bias_ref[...]
    normal_cdf = 0.5 * (1.0 + lax.erf(pre_act * ROOT_HALF))
    normal_pdf = jnp.exp(-0.5 * pre_act * pre_act) * INV_ROOT_TAU
    hidden_ref[...] = (pre_act * normal_cdf).astype(BF16)
    slope_ref[...] = normal_cdf + pre_act * normal_pdf


def causal(block):
    key_pos = lax.broadcasted_iota(jnp.int32, (block, block), 0)
    query_pos = lax.broadcasted_iota(jnp.int32, (block, block), 1)
    return key_pos <= query_pos


def forward_kernel(scale, block, q_ref, k_ref, v_ref, ctx_ref, lse_ref):
    length = q_ref.shape[1]
    queries = q_ref[...] * jnp.asarray(scale, BF16)
    keys = jnp.transpose(k_ref[...])
    values = v_ref[...]
    allowed = causal(block)
    for step in range(length // block):
        here = slice(step * block, (step + 1) * block)
        q_cols = queries[:, here]
        near = jnp.where(allowed, dot(keys[here], q_cols, (1, 0)), NEG_BIG)
        top = jnp.max(near, axis=0, keepdims=True)
        if step:
            far = dot(keys[: step * block], q_cols, (1, 0))
            top = jnp.maximum(top, jnp.max(far, axis=0, keepdims=True))
        near = jnp.exp(near - top)
        total = jnp.sum(near, axis=0, keepdims=True)
        context = dot(values[:, here], near.astype(BF16), (1, 0))
        if step:
            far = jnp.exp(far - top)
            total = total + jnp.sum(far, axis=0, keepdims=True)
            context = context + dot(values[:, : step * block], far.astype(BF16), (1, 0))
        ctx_ref[:, here] = (context / total).astype(BF16)
        lse_ref[0, :, here] = jnp.broadcast_to(top + jnp.log(total), (8, block))


def backward_kernel(
    scale, block, q_ref, k_ref, v_ref, cos_ref, sin_ref, lse_ref, grad_ref,
    dq_ref, dk_ref, dv_ref, sum_ref, keys_acc, values_acc,
):
    length = q_ref.shape[1]
    cosine, sine = cos_ref[...], sin_ref[...]
    queries = q_ref[...] * jnp.asarray(scale, BF16)
    query_rows = jnp.transpose(q_ref[...])
    keys_t = k_ref[...]
    keys = jnp.transpose(keys_t)
    values = jnp.transpose(v_ref[...])
    grad_t = grad_ref[...]
    grad_rows = jnp.transpose(grad_t)
    allowed = causal(block)
    keys_acc[...] = jnp.zeros_like(keys_acc)
    values_acc[...] = jnp.zeros_like(values_acc)
    query_sum = 0.0
    for step in range(length // block):
        here = slice(step * block, (step + 1) * block)
        upto = slice(0, (step + 1) * block)
        lse = lse_ref[0, 0:1, here]
        scores = dot(keys[upto], queries[:, here], (1, 0))
        probs = jnp.exp(scores - lse)
        low = jnp.where(allowed, probs[step * block :], 0.0)
        probs = jnp.concatenate([probs[: step * block], low], axis=0) if step else low
        values_acc[upto, :] += dot(probs.astype(BF16), grad_rows[here], (1, 0))
        prob_grad = dot(values[upto], grad_t[:, here], (1, 0))
        row_dot = jnp.sum(probs * prob_grad, axis=0, keepdims=True)
        score_grad = (probs * (prob_grad - row_dot) * scale).astype(BF16)
        keys_acc[upto, :] += dot(score_grad, query_rows[here], (1, 0))
        dq = dot(keys_t[:, upto], score_grad, (1, 0))
        dq = rotate_rows(dq, cosine[:, here], -sine[:, here])
        dq_ref[:, here] = dq.astype(BF16)
        query_sum = query_sum + jnp.sum(dq, axis=1, keepdims=True)
    dk = rotate_rows(jnp.transpose(keys_acc[...]), cosine, -sine)
    dv = jnp.transpose(values_acc[...])
    dk_ref[...] = dk.astype(BF16)
    dv_ref[...] = dv.astype(BF16)
    sums = [query_sum, jnp.sum(dk, axis=1, keepdims=True), jnp.sum(dv, axis=1, keepdims=True)]
    for place, part in enumerate(sums):
        sum_ref[0, 0, place] = jnp.broadcast_to(part, (part.shape[0], 128))


def branch_kernel(ctx_t_ref, hidden_ref, first_ref, second_ref, branch_ref, ctx_ref):
    hidden_units = hidden_ref.shape[1]
    context = jnp.transpose(ctx_t_ref[...])
    ctx_ref[...] = context
    total = dot(context, first_ref[:, hidden_units:], (1, 1))
    total = total + dot(hidden_ref[...], second_ref[:, :hidden_units], (1, 1))
    branch_ref[...] = total.astype(BF16)


def row_sums(x):
    return jnp.sum(x.reshape(x.shape[0] // 8, 8, x.shape[1]), axis=0)


def return_kernel(
    after_ref, cot_ref, slope_ref, first_ref, second_ref,
    cot_t_ref, ctx_grad_t_ref, pre_low_ref, in_sum_ref, cot_sum_ref,
):
    hidden_units = slope_ref.shape[1]
    cot = cot_ref[...]
    cot_t_ref[...] = jnp.transpose(cot)
    ctx_grad = dot(cot, first_ref[:, hidden_units:], (1, 0))
    ctx_grad_t_ref[...] = jnp.transpose(ctx_grad).astype(BF16)
    pre_grad = dot(cot, second_ref[:, :hidden_units], (1, 0)) * slope_ref[...]
    pre_low_ref[...] = pre_grad.astype(BF16)

    @pl.when(pl.program_id(0) == 0)
    def _():
        in_sum_ref[...] = jnp.zeros_like(in_sum_ref)
        cot_sum_ref[...] = jnp.zeros_like(cot_sum_ref)

    in_sum_ref[...] += row_sums(pre_grad)
    cot_sum_ref[...] += row_sums(cot.astype(F32))


def norm_kernel(
    x_ref, dq_ref, dk_ref, dv_ref, pre_low_ref, first_ref, second_ref,
    proj_low_ref, norm_grad_ref, gain_sum_ref, shift_sum_ref,
):
    hidden_units = pre_low_ref.shape[1]
    proj_low = jnp.transpose(
        jnp.concatenate([dq_ref[...], dk_ref[...], dv_ref[...]], axis=0)
    )
    proj_low_ref[...] = proj_low
    norm_grad = dot(proj_low, second_ref[:, hidden_units:], (1, 1))
    norm_grad = norm_grad + dot(pre_low_ref[...], first_ref[:, :hidden_units], (1, 1))
    norm_grad_ref[...] = norm_grad.astype(BF16)
    unit, _ = normalize(x_ref[...])

    @pl.when(pl.program_id(0) == 0)
    def _():
        gain_sum_ref[...] = jnp.zeros_like(gain_sum_ref)
        shift_sum_ref[...] = jnp.zeros_like(shift_sum_ref)

    gain_sum_ref[...] += row_sums(norm_grad * unit)
    shift_sum_ref[...] += row_sums(norm_grad)


def weight_kernel(
    bit_ref, normed_t_ref, cot_t_ref, pre_low_ref, ctx_ref, hidden_ref, proj_low_ref,
    first_ref, second_ref,
):
    blocks, part, _ = first_ref.shape
    hidden_units = hidden_ref.shape[1]
    starts = [pl.multiple_of((2 * j + bit_ref[0]) * part, part) for j in range(blocks)]

    def rows(ref):
        return jnp.concatenate([ref[pl.ds(start, part), :] for start in starts], axis=0)

    def put(ref, columns, value):
        ref[:, :, columns] = value.reshape(blocks, part, -1).astype(ref.dtype)

    left = rows(normed_t_ref)
    put(first_ref, slice(0, hidden_units), dot(left, pre_low_ref[...], (1, 0)))
    put(second_ref, slice(hidden_units, None), dot(left, proj_low_ref[...], (1, 0)))
    left = rows(cot_t_ref)
    put(first_ref, slice(hidden_units, None), dot(left, ctx_ref[...], (1, 0)))
    put(second_ref, slice(0, hidden_units), dot(left, hidden_ref[...], (1, 0)))


def whole(x):
    return pl.BlockSpec(x.shape, lambda *_: (0,) * x.ndim)


def tokens(block, columns):
    return pl.BlockSpec((block, columns), lambda t: (t, 0))


def tokens_t(rows, block):
    return pl.BlockSpec((rows, block), lambda t: (0, t))


def cost(flops, nbytes, trans=0):
    return pl.CostEstimate(flops=flops, bytes_accessed=nbytes, transcendentals=trans)


def struct(*shape, dtype=BF16):
    return jax.ShapeDtypeStruct(shape, dtype)


def enter(x, vectors, in_bias, qkv_bias, first, second, cosine, sine, heads, head_dim):
    rows, model = x.shape
    hidden_units = in_bias.shape[1]
    proj = 3 * heads * head_dim
    block = min(256, rows)
    per_seq = cosine.shape[1] // block
    table = pl.BlockSpec((ROT // 2, block), lambda t: (0, lax.rem(t, per_seq)))
    return pl.pallas_call(
        functools.partial(enter_kernel, heads, head_dim),
        grid=(rows // block,),
        in_specs=[
            tokens(block, model), whole(vectors), whole(in_bias), whole(qkv_bias),
            whole(first), whole(second), table, table,
        ],
        out_specs=[
            tokens_t(model, block), tokens_t(proj, block),
            tokens(block, hidden_units), tokens(block, hidden_units),
        ],
        out_shape=[
            struct(model, rows), struct(proj, rows),
            struct(rows, hidden_units), struct(rows, hidden_units, dtype=F32),
        ],
        cost_estimate=cost(
            2 * rows * model * (proj + hidden_units), 2 * (first.size + second.size) + 12 * x.size,
            2 * rows * hidden_units,
        ),
        name="enter",
    )(x, vectors, in_bias, qkv_bias, first, second, cosine, sine)


def attend(proj_t, seqs, heads, head_dim, length):
    block = min(256, length)
    scale = 1.0 / math.sqrt(head_dim)

    def part(which):
        return pl.BlockSpec((head_dim, length), lambda s, h: (which * heads + h, s))

    lse_spec = pl.BlockSpec((1, 8, length), lambda s, h: (h, 0, s))
    work = seqs * heads * length * length
    return pl.pallas_call(
        functools.partial(forward_kernel, scale, block),
        grid=(seqs, heads),
        in_specs=[part(0), part(1), part(2)],
        out_specs=[part(0), lse_spec],
        out_shape=[
            struct(heads * head_dim, seqs * length),
            struct(heads, 8, seqs * length, dtype=F32),
        ],
        cost_estimate=cost(4 * work * head_dim, proj_t.size * 4, work),
        name="attend_forward",
    )(proj_t, proj_t, proj_t)


def attend_back(proj_t, cosine, sine, lse, ctx_grad_t, seqs, heads, head_dim, length):
    block = min(256, length)
    scale = 1.0 / math.sqrt(head_dim)

    def part(which):
        return pl.BlockSpec((head_dim, length), lambda s, h: (which * heads + h, s))

    table = pl.BlockSpec((ROT // 2, length), lambda s, h: (0, 0))
    lse_spec = pl.BlockSpec((1, 8, length), lambda s, h: (h, 0, s))
    sum_spec = pl.BlockSpec((1, 1, 3, head_dim, 128), lambda s, h: (s, h, 0, 0, 0))
    flat = struct(heads * head_dim, seqs * length)
    work = seqs * heads * length * length
    return pl.pallas_call(
        functools.partial(backward_kernel, scale, block),
        grid=(seqs, heads),
        in_specs=[part(0), part(1), part(2), table, table, lse_spec, part(0)],
        out_specs=[part(0), part(0), part(0), sum_spec],
        out_shape=[flat, flat, flat, struct(seqs, heads, 3, head_dim, 128, dtype=F32)],
        scratch_shapes=[pltpu.VMEM((length, head_dim), F32)] * 2,
        cost_estimate=cost(10 * work * head_dim, proj_t.size * 6, work),
        name="attend_backward",
    )(proj_t, proj_t, proj_t, cosine, sine, lse, ctx_grad_t)


def branch_sum(ctx_t, hidden, first, second):
    width, rows = ctx_t.shape
    hidden_units = hidden.shape[1]
    model = first.shape[0]
    block = min(256, rows)
    return pl.pallas_call(
        branch_kernel,
        grid=(rows // block,),
        in_specs=[
            tokens_t(width, block), tokens(block, hidden_units), whole(first), whole(second),
        ],
        out_specs=[tokens(block, model), tokens(block, width)],
        out_shape=[struct(rows, model), struct(rows, width)],
        cost_estimate=cost(2 * rows * model * (width + hidden_units), 8 * rows * model),
        name="branch",
    )(ctx_t, hidden, first, second)


def return_grads(after, cot, slopes, first, second, width):
    rows, model = cot.shape
    hidden_units = slopes.shape[1]
    block = min(256, rows)
    return pl.pallas_call(
        return_kernel,
        grid=(rows // block,),
        in_specs=[
            pl.BlockSpec(memory_space=pl.ANY), tokens(block, model), tokens(block, hidden_units), whole(first), whole(second),
        ],
        out_specs=[
            tokens_t(model, block), tokens_t(width, block), tokens(block, hidden_units),
            pl.BlockSpec((8, hidden_units), lambda t: (0, 0)),
            pl.BlockSpec((8, model), lambda t: (0, 0)),
        ],
        out_shape=[
            struct(model, rows), struct(width, rows), struct(rows, hidden_units),
            struct(8, hidden_units, dtype=F32), struct(8, model, dtype=F32),
        ],
        cost_estimate=cost(2 * rows * model * (width + hidden_units), 10 * rows * model),
        name="return_grads",
    )(after, cot, slopes, first, second)


def norm_sum(x, dq_t, dk_t, dv_t, pre_low, first, second):
    rows, model = x.shape
    width = dq_t.shape[0]
    hidden_units = pre_low.shape[1]
    block = min(256, rows)
    return pl.pallas_call(
        norm_kernel,
        grid=(rows // block,),
        in_specs=[
            tokens(block, model), tokens_t(width, block), tokens_t(width, block),
            tokens_t(width, block), tokens(block, hidden_units), whole(first), whole(second),
        ],
        out_specs=[
            tokens(block, 3 * width), tokens(block, model),
            pl.BlockSpec((8, model), lambda t: (0, 0)),
            pl.BlockSpec((8, model), lambda t: (0, 0)),
        ],
        out_shape=[
            struct(rows, 3 * width), struct(rows, model),
            struct(8, model, dtype=F32), struct(8, model, dtype=F32),
        ],
        cost_estimate=cost(2 * rows * model * (3 * width + hidden_units), 8 * rows * model),
        name="norm_grads",
    )(x, dq_t, dk_t, dv_t, pre_low, first, second)


def weight_half(bit, normed_t, cot_t, pre_low, ctx, hidden, proj_low, dp, dtype):
    model, rows = normed_t.shape
    operands = (normed_t, cot_t, pre_low, ctx, hidden, proj_low)
    columns = (hidden.shape[1] + ctx.shape[1], hidden.shape[1] + proj_low.shape[1])
    shapes = [struct(dp // 2, model // dp, c, dtype=dtype) for c in columns]
    return pl.pallas_call(
        weight_kernel,
        grid_spec=pltpu.PrefetchScalarGridSpec(
            num_scalar_prefetch=1,
            grid=(1,),
            in_specs=[whole(x) for x in operands],
            out_specs=[whole(x) for x in shapes],
        ),
        out_shape=shapes,
        cost_estimate=cost(rows * model * sum(columns), 8 * rows * model),
        name="weight_grads",
    )(bit.reshape(1).astype(jnp.int32), *operands)


def rotary_tables(length):
    half_rot = ROT // 2
    position = jnp.arange(length).astype(F32)
    inv_freq = jnp.exp(jnp.arange(half_rot).astype(F32) * (-2.0 * math.log(10000.0) / ROT))
    angles = inv_freq[:, None] * position[None, :]
    return jnp.cos(angles), jnp.sin(angles)


def body(
    dp, tensor, inputs, ln_gain, ln_bias, w_qkv, b_qkv, w_out, w_in, b_in, w_down, out_bias,
    cotangent,
):
    model = inputs.shape[-1]
    heads, head_dim = b_qkv.shape[1], b_qkv.shape[2] * dp
    width = heads * head_dim
    hidden_units = w_in.shape[1]
    seqs, length = inputs.shape[0], inputs.shape[1] * tensor
    rows = seqs * length
    own = ln_gain.shape[0]
    share = own * tensor
    slow = [1 << b for b in range(1, dp.bit_length() - 1)]
    ways = (slow + [1], slow[::-1] + [1])
    me_z = lax.axis_index("tensor")

    full_in = lax.all_gather(inputs, "tensor", axis=1, tiled=True).reshape(rows, model)
    full_cot = lax.all_gather(cotangent, "tensor", axis=1, tiled=True).reshape(rows, model)

    vector = jnp.stack([ln_gain, ln_bias, out_bias[0] + out_bias[1]])
    by_z = [vector]
    for k in range(1, tensor):
        by_z.append(
            lax.ppermute(vector, "tensor", [(i, (i + k) % tensor) for i in range(tensor)])
        )
    by_z = jnp.stack(by_z)
    order = (me_z - jnp.arange(tensor)) % tensor
    by_z = jnp.take(by_z, order, axis=0).transpose(1, 0, 2)
    small = jnp.concatenate(
        [by_z.reshape(-1), b_qkv.astype(F32).reshape(-1), b_in.astype(F32).reshape(-1)]
    )
    used = small.shape[0]
    padded = -(-used // 1024) * 1024
    small = jnp.pad(small, (0, padded - used)).reshape(-1, 128)
    small = gather_bits(small, dp, 0, ways[0]).reshape(dp, padded)
    norm_rows = small[:, : 3 * share].reshape(dp, 3, share).transpose(1, 0, 2).reshape(3, model)
    gain, out_shift = norm_rows[0], norm_rows[2]
    at = 3 * share
    qkv_count = b_qkv.size
    qkv_bias = (
        small[:, at : at + qkv_count]
        .reshape(dp, 3, heads, head_dim // dp)
        .transpose(1, 2, 0, 3)
        .reshape(3 * width)
    )
    at += qkv_count
    in_groups, in_each = b_in.shape
    in_bias = (
        small[:, at : at + b_in.size]
        .reshape(dp, in_groups, in_each)
        .transpose(1, 0, 2)
        .reshape(hidden_units)
    )

    first = gather_bits(jnp.concatenate([w_in, w_out.T], axis=1), dp, 0, ways[0])
    second = gather_bits(
        jnp.concatenate([w_down.T, w_qkv.reshape(w_qkv.shape[0], -1)], axis=1), dp, 0, ways[1]
    )
    first = first.reshape(model, -1)
    second = second.reshape(model, -1)

    cosine, sine = rotary_tables(length)
    normed_t, proj_t, hidden, slopes = enter(
        full_in, norm_rows, in_bias.reshape(1, -1), qkv_bias.reshape(1, -1), first, second,
        cosine, sine, heads, head_dim,
    )
    ctx_t, lse = attend(proj_t, seqs, heads, head_dim, length)
    branch, context = branch_sum(ctx_t, hidden, first, second)
    summed = lax.psum_scatter(
        branch.reshape(seqs, length, model), "tensor", scatter_dimension=1, tiled=True
    )
    outputs = (inputs.astype(F32) + summed.astype(F32) + out_shift).astype(BF16)

    cot_t, ctx_grad_t, pre_low, in_sum, cot_sum = return_grads(
        context, full_cot, slopes, first, second, width
    )
    dq_t, dk_t, dv_t, sums = attend_back(
        proj_t, cosine, sine, lse, ctx_grad_t, seqs, heads, head_dim, length
    )
    proj_low, norm_grad, gain_sum, shift_sum = norm_sum(
        full_in, dq_t, dk_t, dv_t, pre_low, first, second
    )
    own_grad = lax.psum_scatter(
        norm_grad.reshape(seqs, length, model), "tensor", scatter_dimension=1, tiled=True
    ).astype(F32)
    grad_qkv_bias = jnp.sum(sums[..., 0], axis=0).transpose(1, 0, 2)
    grad_in_bias = jnp.sum(in_sum, axis=0)
    gain_part, shift_part, bias_part = (
        jnp.sum(gain_sum, axis=0), jnp.sum(shift_sum, axis=0), jnp.sum(cot_sum, axis=0),
    )

    part = model // dp
    back = (slow[::-1], slow)
    core = bit_of("dp", 1)
    if dp > 1 and part % 16 == 0:
        halves = (normed_t, cot_t, pre_low, context, hidden, proj_low, dp)
        sent = weight_half(1 - core, *halves, BF16)
        got = [swap(x, "dp", dp, 1) for x in sent]
        kept = weight_half(core, *halves, F32)
    else:
        grads = (
            jnp.concatenate([dot(normed_t, pre_low, (1, 0)), dot(cot_t, context, (1, 0))], 1),
            jnp.concatenate([dot(cot_t, hidden, (1, 0)), dot(normed_t, proj_low, (1, 0))], 1),
        )
        grads = [g.reshape(dp // 2, 2, part, -1) for g in grads]
        kept = [lax.dynamic_index_in_dim(g, core, 1, keepdims=False) for g in grads]
        sent = [lax.dynamic_index_in_dim(g, 1 - core, 1, keepdims=False) for g in grads]
        got = [swap(x.astype(BF16), "dp", dp, 1) for x in sent]
    first_grad, second_grad = (
        scatter_bits(k + g.astype(F32), 0, [s // 2 for s in way], BF16, dp, 2)
        for k, g, way in zip(kept, got, back)
    )
    in_out, out_out = first_grad[:, :hidden_units], first_grad[:, hidden_units:].T
    down_out = second_grad[:, :hidden_units].T
    qkv_out = second_grad[:, hidden_units:].reshape(part, 3, width)

    small = jnp.concatenate(
        [
            jnp.stack([gain_part, shift_part, bias_part])
            .reshape(3, dp, share)
            .transpose(1, 0, 2)
            .reshape(dp, -1),
            grad_qkv_bias.reshape(3, heads, dp, head_dim // dp)
            .transpose(2, 0, 1, 3)
            .reshape(dp, -1),
            grad_in_bias.reshape(in_groups, dp, in_each).transpose(1, 0, 2).reshape(dp, -1),
        ],
        axis=1,
    )
    small = jnp.pad(small, ((0, 0), (0, padded - used))).reshape(dp, -1, 128)
    small = scatter_bits(small, 0, [1] + slow, F32, dp, 1).reshape(-1)
    vector = small[: 3 * share].reshape(3, tensor, own)
    mine = lax.dynamic_index_in_dim(vector, me_z, 1, keepdims=False)
    pair = mine[:2]
    for k in range(1, tensor):
        piece = lax.dynamic_index_in_dim(vector[:2], (me_z + k) % tensor, 1, keepdims=False)
        pair = pair + lax.ppermute(
            piece, "tensor", [(i, (i + k) % tensor) for i in range(tensor)]
        )
    bias_grad = jnp.stack([mine[2], mine[2]])
    at = 3 * share
    qkv_bias_out = small[at : at + qkv_count].reshape(b_qkv.shape)
    at += qkv_count
    in_bias_out = small[at : at + b_in.size].reshape(b_in.shape)

    local = inputs.astype(F32)
    local = local - jnp.mean(local, axis=-1, keepdims=True)
    local_inv = lax.rsqrt(jnp.mean(local * local, axis=-1, keepdims=True) + EPS)
    local = local * local_inv
    unit_grad = own_grad * gain
    input_grad = cotangent.astype(F32) + local_inv * (
        unit_grad
        - jnp.mean(unit_grad, axis=-1, keepdims=True)
        - local * jnp.mean(unit_grad * local, axis=-1, keepdims=True)
    )
    return (
        outputs,
        input_grad.astype(BF16),
        pair[0],
        pair[1],
        qkv_out,
        qkv_bias_out,
        out_out,
        in_out,
        in_bias_out,
        down_out,
        bias_grad,
    )


def solution(mesh):
    spread = P("dp", "tensor", None)
    vector = P(("dp", "tensor"))
    qkv, qkv_bias = P("dp", None, "tensor"), P(None, "tensor", "dp")
    by_out, by_in, pair = P("tensor", "dp"), P("dp", "tensor"), P(None, ("dp", "tensor"))

    def layer(*arrays):
        return body(mesh.shape["dp"], mesh.shape["tensor"], *arrays)

    return jax.shard_map(
        layer,
        mesh=mesh,
        in_specs=(
            spread, vector, vector, qkv, qkv_bias, by_out, by_in, by_out, by_out, pair, spread,
        ),
        out_specs=(
            spread, spread, vector, vector, qkv, qkv_bias, by_out, by_in, by_out, by_out, pair,
        ),
        check_vma=False,
    )
```

profile of v0, /device:TPU:0, one launch (start us, length us, event | category | flops | bytes accessed | tf_op | source)
XLA Modules:
  0.0 194.2 jit_solution(10705141909077250884)
XLA Ops:
  9.4 4.1 %collective-permute-start.1 = (f32[3,24]{1,0:T(4,128)S(1)}, f32[3,24]{1,0:T(4,128)S(1)}, u32[]{:S(2)}, u32[]{:S(2)}) collective-permute-start(f32[3,24]{1,0:T(4,128)S(1)} %get-tuple-element.124), channel_id=1, source_target_pairs={{0,2},{1,3},{2,0},{3,1},{4,6},{5,7},{6,4},{7,5},{8,10},{9,11},{10,... | collective-permute-start | bytes 872 | tf_op jit(solution)/shard_map/ppermute | solution.py:472
  15.1 2.2 %collective-permute-start.2 = (f32[3,24]{1,0:T(4,128)S(1)}, f32[3,24]{1,0:T(4,128)S(1)}, u32[]{:S(2)}, u32[]{:S(2)}) collective-permute-start(f32[3,24]{1,0:T(4,128)S(1)} %get-tuple-element.124), channel_id=1, source_target_pairs={{0,3},{1,0},{2,1},{3,2},{4,7},{5,4},{6,5},{7,6},{8,11},{9,8},{10,9... | collective-permute-start | bytes 872 | tf_op jit(solution)/shard_map/ppermute | solution.py:472
  22.0 1.6 collective-permute-start.9
  25.4 3.1 %collective-permute-done.3 = f32[8,128]{1,0:T(8,128)S(1)} collective-permute-done((f32[8,128]{1,0:T(8,128)S(1)}, f32[8,128]{1,0:T(8,128)S(1)}, u32[]{:S(2)}, u32[]{:S(2)}) %collective-permute-start.3) | collective-permute-done | bytes 4128 | tf_op jit(solution)/shard_map/ppermute | solution.py:27
  29.2 1.6 collective-permute-start.7
  32.3 5.5 %collective-permute-done.7 = bf16[2,96,960]{2,1,0:T(8,128)(2,1)S(1)} collective-permute-done((bf16[2,96,960]{2,1,0:T(8,128)(2,1)S(1)}, bf16[2,96,960]{2,1,0:T(8,128)(2,1)S(1)}, u32[]{:S(2)}, u32[]{:S(2)}) %collective-permute-start.7) | collective-permute-done | bytes 368672 | tf_op jit(solution)/shard_map/ppermute | solution.py:27
  38.9 3.5 %collective-permute-done.10 = bf16[2,96,1344]{2,1,0:T(8,128)(2,1)S(1)} collective-permute-done((bf16[2,96,1344]{2,1,0:T(8,128)(2,1)S(1)}, bf16[2,96,1344]{2,1,0:T(8,128)(2,1)S(1)}, u32[]{:S(2)}, u32[]{:S(2)}) %collective-permute-start.10) | collective-permute-done | bytes 516128 | tf_op jit(solution)/shard_map/ppermute | solution.py:27
  54.0 8.6 %enter.1 = (bf16[768,1024]{1,0:T(8,128)(2,1)}, bf16[576,1024]{1,0:T(8,128)(2,1)}, bf16[1024,768]{1,0:T(8,128)(2,1)}, f32[1024,768]{1,0:T(8,128)}) custom-call(bf16[1024,768]{1,0:T(8,128)(2,1)} %bitcast.158, f32[3,768]{1,0:T(4,128)} %reshape.247.vec_ref, f32[1,768]{1,0:T(1,128)} %reshape_reshape.19.in_bias_ref, f32[1,576]{1,0:T(1,128)} %reshape_reshape.20.qkv_bias_ref, ...), custom_call_target="tpu_custom_call" | custom-call | flops 2113929216 | bytes 12976128 | tf_op jit(solution)/shard_map/enter/pallas_call | solution.py:284
  62.5 6.8 %attend_forward.1 = (bf16[192,1024]{1,0:T(8,128)(2,1)}, f32[3,8,1024]{2,1,0:T(8,128)}) custom-call(bf16[576,1024]{1,0:T(8,128)(2,1)} %get-tuple-element.36.q_ref.k_ref.v_ref, bf16[576,1024]{1,0:T(8,128)(2,1)} %get-tuple-element.36.q_ref.k_ref.v_ref, bf16[576,1024]{1,0:T(8,128)(2,1)} %get-tuple-element.36.q_ref.k_ref.v_ref), custom_call_target="tpu_custom_call" | custom-call | flops 805306368 | bytes 2359296 | tf_op jit(solution)/shard_map/attend_forward/pallas_call | solution.py:316
  69.4 6.1 %branch.1 = (bf16[1024,768]{1,0:T(8,128)(2,1)}, bf16[1024,192]{1,0:T(8,128)(2,1)}) custom-call(bf16[192,1024]{1,0:T(8,128)(2,1)} %get-tuple-element.37.ctx_t_ref, bf16[1024,768]{1,0:T(8,128)(2,1)} %get-tuple-element.38.hidden_ref, bf16[768,960]{1,0:T(8,128)(2,1)} %bitcast.149, bf16[768,1344]{1,0:T(8,128)(2,1)} %bitcast.145), custom_call_target="tpu_custom_call" | custom-call | flops 1509949440 | bytes 6291456 | tf_op jit(solution)/shard_map/branch/pallas_call | solution.py:359
  75.5 11.4 %all-gather.5.cloned.1.call-done = bf16[1,1024,768]{2,1,0:T(8,128)(2,1)} async-done(((bf16[1,256,768]{2,1,0:T(8,128)(2,1)}), bf16[1,1024,768]{2,1,0:T(8,128)(2,1)}) %all-gather.5.cloned.1.call-update) | async-done | bytes 1572880 | tf_op jit(solution)/shard_map/all_gather | solution.py:466
  86.9 6.9 %return_grads.1 = (bf16[768,1024]{1,0:T(8,128)(2,1)}, bf16[192,1024]{1,0:T(8,128)(2,1)}, bf16[1024,768]{1,0:T(8,128)(2,1)}, f32[8,768]{1,0:T(8,128)}, f32[8,768]{1,0:T(8,128)}) custom-call(bf16[1024,192]{1,0:T(8,128)(2,1)} %get-tuple-element.41.after_ref.ctx_ref, bf16[1024,768]{1,0:T(8,128)(2,1)} %bitcast.160, f32[1024,768]{1,0:T(8,128)} %get-tuple-element.42.slope_ref, ...), custom_call_target="tpu_custom_call" | custom-call | flops 1509949440 | bytes 7864320 | tf_op jit(solution)/shard_map/return_grads/pallas_call | solution.py:376
  93.8 12.6 %attend_backward.1 = (bf16[192,1024]{1,0:T(8,128)(2,1)}, bf16[192,1024]{1,0:T(8,128)(2,1)}, bf16[192,1024]{1,0:T(8,128)(2,1)}, f32[1,3,3,64,128]{4,3,2,1,0:T(8,128)}) custom-call(bf16[576,1024]{1,0:T(8,128)(2,1)} %get-tuple-element.36.q_ref.k_ref.v_ref, bf16[576,1024]{1,0:T(8,128)(2,1)} %get-tuple-element.36.q_ref.k_ref.v_ref, ...), custom_call_target="tpu_custom_call" | custom-call | flops 2013265920 | bytes 3538944 | tf_op jit(solution)/shard_map/attend_backward/pallas_call | solution.py:342
  106.4 7.7 %norm_grads.1 = (bf16[1024,576]{1,0:T(8,128)(2,1)}, bf16[1024,768]{1,0:T(8,128)(2,1)}, f32[8,768]{1,0:T(8,128)}, f32[8,768]{1,0:T(8,128)}) custom-call(bf16[1024,768]{1,0:T(8,128)(2,1)} %bitcast.159, bf16[192,1024]{1,0:T(8,128)(2,1)} %get-tuple-element.44.dq_ref, bf16[192,1024]{1,0:T(8,128)(2,1)} %get-tuple-element.45.dk_ref, ...), custom_call_target="tpu_custom_call" | custom-call | flops 2113929216 | bytes 6291456 | tf_op jit(solution)/shard_map/norm_grads/pallas_call | solution.py:401
  119.4 6.5 %weight_grads.3 = (bf16[4,96,960]{2,1,0:T(8,128)(2,1)}, bf16[4,96,1344]{2,1,0:T(8,128)(2,1)}) custom-call(s32[1]{0:T(128)} %bitcast.58.bit_ref, bf16[768,1024]{1,0:T(8,128)(2,1)} %get-tuple-element.54.normed_t_ref, bf16[768,1024]{1,0:T(8,128)(2,1)} %get-tuple-element.55.cot_t_ref, bf16[1024,768]{1,0:T(8,128)(2,1)} %get-tuple-element.47.pre_low_ref, ...), custom_call_target="tpu_custom_call" | custom-call | flops 1811939328 | bytes 6291456 | tf_op jit(solution)/shard_map/weight_grads/pallas_call | solution.py:427
  127.5 7.1 %weight_grads.2 = (f32[4,96,960]{2,1,0:T(8,128)}, f32[4,96,1344]{2,1,0:T(8,128)}) custom-call(s32[1]{0:T(128)} %bitcast.57.bit_ref, bf16[768,1024]{1,0:T(8,128)(2,1)} %get-tuple-element.54.normed_t_ref, bf16[768,1024]{1,0:T(8,128)(2,1)} %get-tuple-element.55.cot_t_ref, bf16[1024,768]{1,0:T(8,128)(2,1)} %get-tuple-element.47.pre_low_ref, ...), custom_call_target="tpu_custom_call" | custom-call | flops 1811939328 | bytes 6291456 | tf_op jit(solution)/shard_map/weight_grads/pallas_call | solution.py:427
  141.1 2.2 %collective-permute-done.15 = f32[2,24]{1,0:T(2,128)S(1)} collective-permute-done((f32[2,24]{1,0:T(2,128)S(1)}, f32[2,24]{1,0:T(2,128)S(1)}, u32[]{:S(2)}, u32[]{:S(2)}) %collective-permute-start.15) | collective-permute-done | bytes 224 | tf_op jit(solution)/shard_map/ppermute | solution.py:585
  151.4 1.7 copy.57
  153.1 3.3 %collective-permute-done.22 = bf16[2,96,960]{2,1,0:T(8,128)(2,1)} collective-permute-done((bf16[2,96,960]{2,1,0:T(8,128)(2,1)}, bf16[2,96,960]{2,1,0:T(8,128)(2,1)}, u32[]{:S(2)}, u32[]{:S(2)}) %collective-permute-start.22) | collective-permute-done | bytes 368672 | tf_op jit(solution)/shard_map/ppermute | solution.py:27
  160.0 4.6 %collective-permute-done.19 = bf16[2,96,1344]{2,1,0:T(8,128)(2,1)} collective-permute-done((bf16[2,96,1344]{2,1,0:T(8,128)(2,1)}, bf16[2,96,1344]{2,1,0:T(8,128)(2,1)}, u32[]{:S(2)}, u32[]{:S(2)}) %collective-permute-start.19) | collective-permute-done | bytes 516128 | tf_op jit(solution)/shard_map/ppermute | solution.py:27
  164.6 2.2 %copy.59 = bf16[2,96,1344]{1,2,0:T(8,128)(2,1)} copy(bf16[2,96,1344]{2,1,0:T(8,128)(2,1)} %collective-permute-done.19) | data formatting | bytes 1032192 | tf_op jit(solution)/shard_map/ppermute | solution.py:27
  170.9 4.6 %collective-permute-done.20 = bf16[96,1344]{0,1:T(8,128)(2,1)S(1)} collective-permute-done((bf16[96,1344]{0,1:T(8,128)(2,1)S(1)}, bf16[96,1344]{0,1:T(8,128)(2,1)S(1)}, u32[]{:S(2)}, u32[]{:S(2)}) %collective-permute-start.20) | collective-permute-done | bytes 258080 | tf_op jit(solution)/shard_map/ppermute | solution.py:27
  178.7 6.6 %reduce-scatter.3.cloned.1.call-done = bf16[1,256,768]{2,1,0:T(8,128)(2,1)} async-done(((bf16[1,1024,768]{2,1,0:T(8,128)(2,1)}), bf16[1,256,768]{2,1,0:T(8,128)(2,1)}) %reduce-scatter.3.cloned.1.call-update) | async-done | bytes 393232 | tf_op jit(solution)/shard_map/reduce_scatter | solution.py:517
  185.3 2.4 %fusion.8 = (bf16[1,256,768]{2,1,0:T(8,128)(2,1)}, bf16[1,256,768]{2,1,0:T(8,128)(2,1)}) fusion(bf16[1,256,768]{2,1,0:T(8,128)(2,1)S(1)} %copy-done, bf16[1,256,768]{2,1,0:T(8,128)(2,1)} %reduce-scatter.5.cloned.1.call-done, bf16[1,256,768]{2,1,0:T(8,128)(2,1)S(1)} %copy-done.4, f32[256]{0:T(256)S(1)} %get-tuple-element.127, f32[256]{0:T(256)S(1)} %get-tuple-element.128, ...), kind=kLoop, calls=%fused_computation.21 | loop fusion | flops 3145728 | bytes 2369536 | tf_op jit(solution)/shard_map/convert_element_type | solution.py:606
  (198 shorter events, 56.7 us)
Async XLA Ops:
  7.2 46.7 %all-gather.3.cloned.1.call-start = ((), (), s32[]{:S(2)}) async-start(), calls=%async_computation.2 | async-start | bytes 1966080 | tf_op jit(solution)/shard_map/all_gather | solution.py:465
  8.0 79.0 %all-gather.5.cloned.1.call-start = ((), (), s32[]{:S(2)}) async-start(), calls=%async_computation.4 | async-start | bytes 1966080 | tf_op jit(solution)/shard_map/all_gather | solution.py:466
  9.4 14.5 %collective-permute-start.1 = (f32[3,24]{1,0:T(4,128)S(1)}, f32[3,24]{1,0:T(4,128)S(1)}, u32[]{:S(2)}, u32[]{:S(2)}) collective-permute-start(f32[3,24]{1,0:T(4,128)S(1)} %get-tuple-element.124), channel_id=1, source_target_pairs={{0,2},{1,3},{2,0},{3,1},{4,6},{5,7},{6,4},{7,5},{8,10},{9,11},{10,... | collective-permute-start | bytes 872 | tf_op jit(solution)/shard_map/ppermute | solution.py:472
  13.6 10.4 %collective-permute-start = (f32[3,24]{1,0:T(4,128)S(1)}, f32[3,24]{1,0:T(4,128)S(1)}, u32[]{:S(2)}, u32[]{:S(2)}) collective-permute-start(f32[3,24]{1,0:T(4,128)S(1)} %get-tuple-element.124), channel_id=1, source_target_pairs={{0,1},{1,2},{2,3},{3,0},{4,5},{5,6},{6,7},{7,4},{8,9},{9,10},{10,1... | collective-permute-start | bytes 872 | tf_op jit(solution)/shard_map/ppermute | solution.py:472
  15.1 8.9 %collective-permute-start.2 = (f32[3,24]{1,0:T(4,128)S(1)}, f32[3,24]{1,0:T(4,128)S(1)}, u32[]{:S(2)}, u32[]{:S(2)}) collective-permute-start(f32[3,24]{1,0:T(4,128)S(1)} %get-tuple-element.124), channel_id=1, source_target_pairs={{0,3},{1,0},{2,1},{3,2},{4,7},{5,4},{6,5},{7,6},{8,11},{9,8},{10,9... | collective-permute-start | bytes 872 | tf_op jit(solution)/shard_map/ppermute | solution.py:472
  19.2 9.8 %collective-permute-start.6 = (bf16[96,960]{1,0:T(8,128)(2,1)S(1)}, bf16[96,960]{1,0:T(8,128)(2,1)S(1)}, u32[]{:S(2)}, u32[]{:S(2)}) collective-permute-start(bf16[96,960]{1,0:T(8,128)(2,1)S(1)} %pad_maximum_fusion.7), channel_id=1, source_target_pairs={{0,8},{4,12},{8,0},{12,4},{16,24},{20,28},{24,16},{28,20},{1,9},{5... | collective-permute-start | bytes 552968 | tf_op jit(solution)/shard_map/ppermute | solution.py:27
  22.0 8.7 %collective-permute-start.9 = (bf16[96,1344]{1,0:T(8,128)(2,1)S(1)}, bf16[96,1344]{1,0:T(8,128)(2,1)S(1)}, u32[]{:S(2)}, u32[]{:S(2)}) collective-permute-start(bf16[96,1344]{1,0:T(8,128)(2,1)S(1)} %pad_maximum_fusion.6), channel_id=1, source_target_pairs={{0,16},{4,20},{8,24},{12,28},{16,0},{20,4},{24,8},{28,12},{1,17},{... | collective-permute-start | bytes 774152 | tf_op jit(solution)/shard_map/ppermute | solution.py:27
  23.7 153.7 %reduce-scatter.5.cloned.1.call-start = ((), (), s32[]{:S(2)}) async-start(), calls=%async_computation.5 | async-start | bytes 1966080 | tf_op jit(solution)/shard_map/reduce_scatter | solution.py:531
  29.2 8.7 %collective-permute-start.7 = (bf16[2,96,960]{2,1,0:T(8,128)(2,1)S(1)}, bf16[2,96,960]{2,1,0:T(8,128)(2,1)S(1)}, u32[]{:S(2)}, u32[]{:S(2)}) collective-permute-start(bf16[2,96,960]{2,1,0:T(8,128)(2,1)S(1)} %pad_maximum_fusion.5), channel_id=1, source_target_pairs={{0,16},{4,20},{8,24},{12,28},{16,0},{20,4},{24,8},{28,12},{1,17},{... | collective-permute-start | bytes 1105928 | tf_op jit(solution)/shard_map/ppermute | solution.py:27
  30.9 11.4 %collective-permute-start.10 = (bf16[2,96,1344]{2,1,0:T(8,128)(2,1)S(1)}, bf16[2,96,1344]{2,1,0:T(8,128)(2,1)S(1)}, u32[]{:S(2)}, u32[]{:S(2)}) collective-permute-start(bf16[2,96,1344]{2,1,0:T(8,128)(2,1)S(1)} %pad_maximum_fusion.4), channel_id=1, source_target_pairs={{0,8},{4,12},{8,0},{12,4},{16,24},{20,28},{24,16},{28,20},{1,9},{5... | collective-permute-start | bytes 1548296 | tf_op jit(solution)/shard_map/ppermute | solution.py:27
  38.9 9.1 %collective-permute-start.8 = (bf16[2,2,96,960]{3,2,1,0:T(8,128)(2,1)}, bf16[2,2,96,960]{3,2,1,0:T(8,128)(2,1)}, u32[]{:S(2)}, u32[]{:S(2)}) collective-permute-start(bf16[2,2,96,960]{3,2,1,0:T(8,128)(2,1)} %pad_maximum_fusion.3), channel_id=1, source_target_pairs={{0,4},{4,0},{8,12},{12,8},{16,20},{20,16},{24,28},{28,24},{1,5},{5... | collective-permute-start | bytes 2211848 | tf_op jit(solution)/shard_map/ppermute | solution.py:27
  42.6 8.1 %collective-permute-start.11 = (bf16[2,2,96,1344]{3,2,0,1:T(8,128)(2,1)S(1)}, bf16[2,2,96,1344]{3,2,0,1:T(8,128)(2,1)}, u32[]{:S(2)}, u32[]{:S(2)}) collective-permute-start(bf16[2,2,96,1344]{3,2,0,1:T(8,128)(2,1)S(1)} %pad_maximum_fusion.2), channel_id=1, source_target_pairs={{0,4},{4,0},{8,12},{12,8},{16,20},{20,16},{24,28},{28,24},{1,5},{5... | collective-permute-start | bytes 3096584 | tf_op jit(solution)/shard_map/ppermute | solution.py:27
  114.3 71.0 %reduce-scatter.3.cloned.1.call-start = ((), (), s32[]{:S(2)}) async-start(), calls=%async_computation.3 | async-start | bytes 1966080 | tf_op jit(solution)/shard_map/reduce_scatter | solution.py:517
  117.9 8.0 %collective-permute-start.13 = (f32[2,8,128]{2,1,0:T(8,128)S(1)}, f32[2,8,128]{2,1,0:T(8,128)S(1)}, u32[]{:S(2)}, u32[]{:S(2)}) collective-permute-start(f32[2,8,128]{2,1,0:T(8,128)S(1)} %dynamic-slice_bitcast_fusion.1), channel_id=1, source_target_pairs={{0,8},{4,12},{8,0},{12,4},{16,24},{20,28},{24,16},{28,20},{1,9},{5... | collective-permute-start | bytes 24584 | tf_op jit(solution)/shard_map/ppermute | solution.py:27
  126.0 9.2 %collective-permute-start.14 = (f32[8,128]{1,0:T(8,128)S(1)}, f32[8,128]{1,0:T(8,128)S(1)}, u32[]{:S(2)}, u32[]{:S(2)}) collective-permute-start(f32[8,128]{1,0:T(8,128)S(1)} %fusion.21), channel_id=1, source_target_pairs={{0,16},{4,20},{8,24},{12,28},{16,0},{20,4},{24,8},{28,12},{1,17},{... | collective-permute-start | bytes 12296 | tf_op jit(solution)/shard_map/ppermute | solution.py:27
  134.7 9.4 %collective-permute-start.21 = (bf16[4,96,960]{2,1,0:T(8,128)(2,1)S(1)}, bf16[4,96,960]{2,1,0:T(8,128)(2,1)}, u32[]{:S(2)}, u32[]{:S(2)}) collective-permute-start(bf16[4,96,960]{2,1,0:T(8,128)(2,1)S(1)} %copy-done.15), channel_id=1, source_target_pairs={{0,4},{4,0},{8,12},{12,8},{16,20},{20,16},{24,28},{28,24},{1,5},{5... | collective-permute-start | bytes 2211848 | tf_op jit(solution)/shard_map/ppermute | solution.py:27
  134.7 12.8 %collective-permute-start.18 = (bf16[4,96,1344]{2,1,0:T(8,128)(2,1)}, bf16[4,96,1344]{2,1,0:T(8,128)(2,1)}, u32[]{:S(2)}, u32[]{:S(2)}) collective-permute-start(bf16[4,96,1344]{2,1,0:T(8,128)(2,1)} %get-tuple-element.58), channel_id=1, source_target_pairs={{0,4},{4,0},{8,12},{12,8},{16,20},{20,16},{24,28},{28,24},{1,5},{5... | collective-permute-start | bytes 3096584 | tf_op jit(solution)/shard_map/ppermute | solution.py:27
  136.3 4.8 %collective-permute-start.17 = (f32[2,24]{1,0:T(2,128)S(1)}, f32[2,24]{1,0:T(2,128)S(1)}, u32[]{:S(2)}, u32[]{:S(2)}) collective-permute-start(f32[2,24]{1,0:T(2,128)S(1)} %bitcast.186), channel_id=1, source_target_pairs={{0,3},{1,0},{2,1},{3,2},{4,7},{5,4},{6,5},{7,6},{8,11},{9,8},{10,9... | collective-permute-start | bytes 584 | tf_op jit(solution)/shard_map/ppermute | solution.py:585
  137.8 5.5 %collective-permute-start.15 = (f32[2,24]{1,0:T(2,128)S(1)}, f32[2,24]{1,0:T(2,128)S(1)}, u32[]{:S(2)}, u32[]{:S(2)}) collective-permute-start(f32[2,24]{1,0:T(2,128)S(1)} %bitcast.185), channel_id=1, source_target_pairs={{0,1},{1,2},{2,3},{3,0},{4,5},{5,6},{6,7},{7,4},{8,9},{9,10},{10,1... | collective-permute-start | bytes 584 | tf_op jit(solution)/shard_map/ppermute | solution.py:585
  138.9 4.7 %collective-permute-start.16 = (f32[2,24]{1,0:T(2,128)S(1)}, f32[2,24]{1,0:T(2,128)S(1)}, u32[]{:S(2)}, u32[]{:S(2)}) collective-permute-start(f32[2,24]{1,0:T(2,128)S(1)} %bitcast.184), channel_id=1, source_target_pairs={{0,2},{1,3},{2,0},{3,1},{4,6},{5,7},{6,4},{7,5},{8,10},{9,11},{10,... | collective-permute-start | bytes 584 | tf_op jit(solution)/shard_map/ppermute | solution.py:585
  146.5 9.8 %collective-permute-start.22 = (bf16[2,96,960]{2,1,0:T(8,128)(2,1)}, bf16[2,96,960]{2,1,0:T(8,128)(2,1)}, u32[]{:S(2)}, u32[]{:S(2)}) collective-permute-start(bf16[2,96,960]{2,1,0:T(8,128)(2,1)} %fusion.14), channel_id=1, source_target_pairs={{0,16},{4,20},{8,24},{12,28},{16,0},{20,4},{24,8},{28,12},{1,17},{... | collective-permute-start | bytes 1105928 | tf_op jit(solution)/shard_map/ppermute | solution.py:27
  149.9 14.7 %collective-permute-start.19 = (bf16[2,96,1344]{2,1,0:T(8,128)(2,1)}, bf16[2,96,1344]{2,1,0:T(8,128)(2,1)}, u32[]{:S(2)}, u32[]{:S(2)}) collective-permute-start(bf16[2,96,1344]{2,1,0:T(8,128)(2,1)} %fusion.13), channel_id=1, source_target_pairs={{0,8},{4,12},{8,0},{12,4},{16,24},{20,28},{24,16},{28,20},{1,9},{5... | collective-permute-start | bytes 1548296 | tf_op jit(solution)/shard_map/ppermute | solution.py:27
  159.0 10.3 %collective-permute-start.23 = (bf16[96,960]{1,0:T(8,128)(2,1)}, bf16[96,960]{1,0:T(8,128)(2,1)S(1)}, u32[]{:S(2)}, u32[]{:S(2)}) collective-permute-start(bf16[96,960]{1,0:T(8,128)(2,1)} %fusion.16), channel_id=1, source_target_pairs={{0,8},{4,12},{8,0},{12,4},{16,24},{20,28},{24,16},{28,20},{1,9},{5... | collective-permute-start | bytes 552968 | tf_op jit(solution)/shard_map/ppermute | solution.py:27
  168.1 7.3 %collective-permute-start.20 = (bf16[96,1344]{0,1:T(8,128)(2,1)S(1)}, bf16[96,1344]{0,1:T(8,128)(2,1)S(1)}, u32[]{:S(2)}, u32[]{:S(2)}) collective-permute-start(bf16[96,1344]{0,1:T(8,128)(2,1)S(1)} %fusion.15), channel_id=1, source_target_pairs={{0,16},{4,20},{8,24},{12,28},{16,0},{20,4},{24,8},{28,12},{1,17},{... | collective-permute-start | bytes 774152 | tf_op jit(solution)/shard_map/ppermute | solution.py:27
  (20 other events, 123.6 us)
Sparse Core Ops, SparseCore 0:
  9.6 39.7 all-gather.2
  50.9 35.9 all-gather.4
  114.4 34.3 reduce-scatter.4
  150.9 34.2 reduce-scatter.2
where the time goes:
time: 195 us; the launch traced here: 194 us
  Pallas kernels  62.5 us (32%)
  waiting for transfers between devices  48.9 us (25%)
  starting transfers between devices  26 us (13%)
  local copies, waits for them, and re-layouts  23.6 us (12%)
  other arithmetic  18.6 us (10%)
  between operations  14.5 us (7%)
    ppermute x18, waiting for transfers between devices, swap(): return lax.ppermute(x, axis_name, [(i, i ^ step) for i in range(size)])  27.7 us
    ppermute x18, starting transfers between devices, swap(): return lax.ppermute(x, axis_name, [(i, i ^ step) for i in range(size)])  14.2 us
    pallas_call x2, Pallas kernels, weight_half(): pl.pallas_call(weight_kernel, grid_spec=pltpu.PrefetchScalarGridSpec(num_...  13.7 us
    pallas_call x1, Pallas kernels, attend_back(): pl.pallas_call(functools.partial(backward_kernel, scale, block), grid=(se...  12.6 us
    all_gather x1, waiting for transfers between devices, body(): lax.all_gather(cotangent, 'tensor', axis=1, tiled=True).reshape(rows, model)  11.4 us
    pallas_call x1, Pallas kernels, enter(): pl.pallas_call(functools.partial(enter_kernel, heads, head_dim), grid=(ro...  8.58 us
    ppermute x3, starting transfers between devices, body(): lax.ppermute(vector, 'tensor', [(i, (i + k) % tensor) for i in range(tens...  7.94 us
    pallas_call x1, Pallas kernels, norm_sum(): pl.pallas_call(norm_kernel, grid=(rows // block,), in_specs=[tokens(block...  7.75 us
  transfers between devices with their start and end apart: 28, of which 13 were waited for; matrix products, arithmetic and copies ran while one was open for 20% of the time, Pallas kernels for 18%

commit v1 on v0

--- a/solution.py
+++ b/solution.py
@@ -13,6 +13,7 @@
 ROOT_HALF = 0.7071067811865476
 INV_ROOT_TAU = 0.3989422804014327
 NEG_BIG = -1e30
+SMALL_ROWS = 16
 F32 = jnp.float32
 BF16 = jnp.bfloat16
 
@@ -232,26 +233,36 @@
     shift_sum_ref[...] += row_sums(norm_grad)
 
 
-def weight_kernel(
-    bit_ref, normed_t_ref, cot_t_ref, pre_low_ref, ctx_ref, hidden_ref, proj_low_ref,
-    first_ref, second_ref,
+def half_rows(ref, bit, blocks, part):
+    starts = [pl.multiple_of((2 * j + bit) * part, part) for j in range(blocks)]
+    return jnp.concatenate([ref[pl.ds(start, part), :] for start in starts], axis=0)
+
+
+def put(ref, columns, value):
+    blocks, part, _ = ref.shape
+    ref[:, :, columns] = value.reshape(blocks, part, -1).astype(ref.dtype)
+
+
+def early_kernel(
+    bit_ref, normed_t_ref, cot_t_ref, pre_low_ref, ctx_ref, hidden_ref, early_ref
 ):
-    blocks, part, _ = first_ref.shape
+    blocks, part, _ = early_ref.shape
     hidden_units = hidden_ref.shape[1]
-    starts = [pl.multiple_of((2 * j + bit_ref[0]) * part, part) for j in range(blocks)]
-
-    def rows(ref):
-        return jnp.concatenate([ref[pl.ds(start, part), :] for start in starts], axis=0)
-
-    def put(ref, columns, value):
-        ref[:, :, columns] = value.reshape(blocks, part, -1).astype(ref.dtype)
-
-    left = rows(normed_t_ref)
-    put(first_ref, slice(0, hidden_units), dot(left, pre_low_ref[...], (1, 0)))
-    put(second_ref, slice(hidden_units, None), dot(left, proj_low_ref[...], (1, 0)))
-    left = rows(cot_t_ref)
-    put(first_ref, slice(hidden_units, None), dot(left, ctx_ref[...], (1, 0)))
-    put(second_ref, slice(0, hidden_units), dot(left, hidden_ref[...], (1, 0)))
+    left = half_rows(normed_t_ref, bit_ref[0], blocks, part)
+    put(early_ref, slice(0, hidden_units), dot(left, pre_low_ref[...], (1, 0)))
+    left = half_rows(cot_t_ref, bit_ref[0], blocks, part)
+    put(early_ref, slice(hidden_units, 2 * hidden_units), dot(left, hidden_ref[...], (1, 0)))
+    put(early_ref, slice(2 * hidden_units, None), dot(left, ctx_ref[...], (1, 0)))
+
+
+def late_kernel(bit_ref, normed_t_ref, proj_low_ref, small_ref, late_ref):
+    blocks, total, columns = late_ref.shape
+    part = total - SMALL_ROWS
+    left = half_rows(normed_t_ref, bit_ref[0], blocks, part)
+    value = dot(left, proj_low_ref[...], (1, 0)).reshape(blocks, part, columns)
+    late_ref[:, :part] = value.astype(late_ref.dtype)
+    for block in range(blocks):
+        late_ref[block, part:] = small_ref[2 * block + bit_ref[0]].astype(late_ref.dtype)
 
 
 def whole(x):
@@ -419,22 +430,42 @@
     )(x, dq_t, dk_t, dv_t, pre_low, first, second)
 
 
-def weight_half(bit, normed_t, cot_t, pre_low, ctx, hidden, proj_low, dp, dtype):
-    model, rows = normed_t.shape
-    operands = (normed_t, cot_t, pre_low, ctx, hidden, proj_low)
-    columns = (hidden.shape[1] + ctx.shape[1], hidden.shape[1] + proj_low.shape[1])
-    shapes = [struct(dp // 2, model // dp, c, dtype=dtype) for c in columns]
-    return pl.pallas_call(
-        weight_kernel,
+def finish_kernel(x_ref, cot_ref, own_ref, gain_ref, grad_ref):
+    unit, inv_sigma = normalize(x_ref[0])
+    unit_grad = own_ref[0].astype(F32) * gain_ref[...]
+    grad = cot_ref[0].astype(F32) + inv_sigma * (
+        unit_grad
+        - jnp.mean(unit_grad, axis=-1, keepdims=True)
+        - unit * jnp.mean(unit_grad * unit, axis=-1, keepdims=True)
+    )
+    grad_ref[0] = grad.astype(BF16)
+
+
+def finish(x, cot, own, gain):
+    rows = pl.BlockSpec((1, x.shape[1] // 2, x.shape[2]), lambda s, t: (s, t, 0))
+    return pl.pallas_call(
+        finish_kernel,
+        grid=(x.shape[0], 2),
+        in_specs=[rows, rows, rows, pl.BlockSpec(gain.shape, lambda *_: (0, 0))],
+        out_specs=rows,
+        out_shape=struct(*x.shape),
+        cost_estimate=cost(20 * x.size, 8 * x.size),
+        name="finish",
+    )(x, cot, own, gain)
+
+
+def weight_half(kernel, bit, operands, shape, flops, dtype):
+    out = struct(*shape, dtype=dtype)
+    return pl.pallas_call(
+        kernel,
         grid_spec=pltpu.PrefetchScalarGridSpec(
             num_scalar_prefetch=1,
             grid=(1,),
             in_specs=[whole(x) for x in operands],
-            out_specs=[whole(x) for x in shapes],
+            out_specs=whole(out),
         ),
-        out_shape=shapes,
-        cost_estimate=cost(rows * model * sum(columns), 8 * rows * model),
-        name="weight_grads",
+        out_shape=out,
+        cost_estimate=cost(flops, 4 * operands[0].size),
     )(bit.reshape(1).astype(jnp.int32), *operands)
 
 
@@ -444,6 +475,30 @@
     inv_freq = jnp.exp(jnp.arange(half_rot).astype(F32) * (-2.0 * math.log(10000.0) / ROT))
     angles = inv_freq[:, None] * position[None, :]
     return jnp.cos(angles), jnp.sin(angles)
+
+
+def split_core(grad, dp):
+    core = bit_of("dp", 1)
+    grad = grad.reshape(dp // 2, 2, -1, grad.shape[-1])
+    kept = lax.dynamic_index_in_dim(grad, core, 1, keepdims=False)
+    sent = lax.dynamic_index_in_dim(grad, 1 - core, 1, keepdims=False)
+    return kept, sent.astype(BF16)
+
+
+def exchange(kept, sent, dp):
+    got = swap(sent, "dp", dp, 1)
+    x = kept + got.astype(F32)
+    count = dp // 2
+    if count > 4:
+        steps = [1 << b for b in range(count.bit_length() - 1)]
+        return scatter_bits(x, 0, steps[::-1], BF16, dp, 2)
+    chip = lax.axis_index("dp") // 2
+    total = lax.dynamic_index_in_dim(x, chip, 0, keepdims=False)
+    for k in range(1, count):
+        piece = lax.dynamic_index_in_dim(x, chip ^ k, 0, keepdims=False).astype(BF16)
+        got = swap(piece, "dp", dp, 2 * k)
+        total = total + got.astype(F32)
+    return total
 
 
 def body(
@@ -502,7 +557,7 @@
 
     first = gather_bits(jnp.concatenate([w_in, w_out.T], axis=1), dp, 0, ways[0])
     second = gather_bits(
-        jnp.concatenate([w_down.T, w_qkv.reshape(w_qkv.shape[0], -1)], axis=1), dp, 0, ways[1]
+        jnp.concatenate([w_down.T, w_qkv.reshape(w_qkv.shape[0], -1)], axis=1), dp, 0, ways[1],
     )
     first = first.reshape(model, -1)
     second = second.reshape(model, -1)
@@ -522,6 +577,27 @@
     cot_t, ctx_grad_t, pre_low, in_sum, cot_sum = return_grads(
         context, full_cot, slopes, first, second, width
     )
+    part = model // dp
+    core = bit_of("dp", 1)
+    aligned = dp > 1 and part % 16 == 0
+    if aligned:
+        operands = (normed_t, cot_t, pre_low, context, hidden)
+        shape = (dp // 2, part, 2 * hidden_units + width)
+        flops = rows * model * shape[2]
+        early_sent = weight_half(early_kernel, 1 - core, operands, shape, flops, BF16)
+        early_kept = weight_half(early_kernel, core, operands, shape, flops, F32)
+    else:
+        early_kept, early_sent = split_core(
+            jnp.concatenate(
+                [
+                    dot(normed_t, pre_low, (1, 0)),
+                    dot(cot_t, hidden, (1, 0)),
+                    dot(cot_t, context, (1, 0)),
+                ],
+                axis=1,
+            ),
+            dp,
+        )
     dq_t, dk_t, dv_t, sums = attend_back(
         proj_t, cosine, sine, lse, ctx_grad_t, seqs, heads, head_dim, length
     )
@@ -530,44 +606,22 @@
     )
     own_grad = lax.psum_scatter(
         norm_grad.reshape(seqs, length, model), "tensor", scatter_dimension=1, tiled=True
-    ).astype(F32)
+    )
     grad_qkv_bias = jnp.sum(sums[..., 0], axis=0).transpose(1, 0, 2)
     grad_in_bias = jnp.sum(in_sum, axis=0)
-    gain_part, shift_part, bias_part = (
-        jnp.sum(gain_sum, axis=0), jnp.sum(shift_sum, axis=0), jnp.sum(cot_sum, axis=0),
-    )
-
-    part = model // dp
-    back = (slow[::-1], slow)
-    core = bit_of("dp", 1)
-    if dp > 1 and part % 16 == 0:
-        halves = (normed_t, cot_t, pre_low, context, hidden, proj_low, dp)
-        sent = weight_half(1 - core, *halves, BF16)
-        got = [swap(x, "dp", dp, 1) for x in sent]
-        kept = weight_half(core, *halves, F32)
-    else:
-        grads = (
-            jnp.concatenate([dot(normed_t, pre_low, (1, 0)), dot(cot_t, context, (1, 0))], 1),
-            jnp.concatenate([dot(cot_t, hidden, (1, 0)), dot(normed_t, proj_low, (1, 0))], 1),
+    bias_part = jnp.sum(cot_sum, axis=0).reshape(dp, tensor, own)
+    pair = jnp.stack([gain_sum, shift_sum]).sum(axis=1).reshape(2, dp, tensor, own)
+    pair_total = lax.dynamic_index_in_dim(pair, me_z, 2, keepdims=False)
+    for k in range(1, tensor):
+        piece = lax.dynamic_index_in_dim(pair, (me_z + k) % tensor, 2, keepdims=False)
+        got = lax.ppermute(
+            piece, "tensor", [(i, (i + k) % tensor) for i in range(tensor)]
         )
-        grads = [g.reshape(dp // 2, 2, part, -1) for g in grads]
-        kept = [lax.dynamic_index_in_dim(g, core, 1, keepdims=False) for g in grads]
-        sent = [lax.dynamic_index_in_dim(g, 1 - core, 1, keepdims=False) for g in grads]
-        got = [swap(x.astype(BF16), "dp", dp, 1) for x in sent]
-    first_grad, second_grad = (
-        scatter_bits(k + g.astype(F32), 0, [s // 2 for s in way], BF16, dp, 2)
-        for k, g, way in zip(kept, got, back)
-    )
-    in_out, out_out = first_grad[:, :hidden_units], first_grad[:, hidden_units:].T
-    down_out = second_grad[:, :hidden_units].T
-    qkv_out = second_grad[:, hidden_units:].reshape(part, 3, width)
-
+        pair_total = pair_total + got
+    bias_total = lax.dynamic_index_in_dim(bias_part, me_z, 1, keepdims=False)
     small = jnp.concatenate(
         [
-            jnp.stack([gain_part, shift_part, bias_part])
-            .reshape(3, dp, share)
-            .transpose(1, 0, 2)
-            .reshape(dp, -1),
+            pair_total[0], pair_total[1], bias_total,
             grad_qkv_bias.reshape(3, heads, dp, head_dim // dp)
             .transpose(2, 0, 1, 3)
             .reshape(dp, -1),
@@ -575,37 +629,40 @@
         ],
         axis=1,
     )
-    small = jnp.pad(small, ((0, 0), (0, padded - used))).reshape(dp, -1, 128)
-    small = scatter_bits(small, 0, [1] + slow, F32, dp, 1).reshape(-1)
-    vector = small[: 3 * share].reshape(3, tensor, own)
-    mine = lax.dynamic_index_in_dim(vector, me_z, 1, keepdims=False)
-    pair = mine[:2]
-    for k in range(1, tensor):
-        piece = lax.dynamic_index_in_dim(vector[:2], (me_z + k) % tensor, 1, keepdims=False)
-        pair = pair + lax.ppermute(
-            piece, "tensor", [(i, (i + k) % tensor) for i in range(tensor)]
-        )
-    bias_grad = jnp.stack([mine[2], mine[2]])
-    at = 3 * share
+    columns = 3 * width
+    small = jnp.pad(
+        small[:, None, :], ((0, 0), (0, SMALL_ROWS - 1), (0, columns - small.shape[1]))
+    )
+    if aligned:
+        operands = (normed_t, proj_low, small)
+        shape = (dp // 2, part + SMALL_ROWS, columns)
+        flops = rows * model * columns
+        late_sent = weight_half(late_kernel, 1 - core, operands, shape, flops, BF16)
+        late_kept = weight_half(late_kernel, core, operands, shape, flops, F32)
+    else:
+        late = dot(normed_t, proj_low, (1, 0)).reshape(dp, part, columns)
+        late_kept, late_sent = split_core(jnp.concatenate([late, small], axis=1), dp)
+
+    early = exchange(early_kept, early_sent, dp)
+    late = exchange(late_kept, late_sent, dp)
+    in_out = early[:, :hidden_units]
+    down_out = early[:, hidden_units : 2 * hidden_units].T
+    out_out = early[:, 2 * hidden_units :].T
+    qkv_out = late[:part].reshape(part, 3, width)
+    small = late[part]
+    gain_out, shift_out, bias_out = (small[k * own : (k + 1) * own] for k in range(3))
+    bias_grad = jnp.stack([bias_out, bias_out])
+    at = 3 * own
     qkv_bias_out = small[at : at + qkv_count].reshape(b_qkv.shape)
     at += qkv_count
     in_bias_out = small[at : at + b_in.size].reshape(b_in.shape)
 
-    local = inputs.astype(F32)
-    local = local - jnp.mean(local, axis=-1, keepdims=True)
-    local_inv = lax.rsqrt(jnp.mean(local * local, axis=-1, keepdims=True) + EPS)
-    local = local * local_inv
-    unit_grad = own_grad * gain
-    input_grad = cotangent.astype(F32) + local_inv * (
-        unit_grad
-        - jnp.mean(unit_grad, axis=-1, keepdims=True)
-        - local * jnp.mean(unit_grad * local, axis=-1, keepdims=True)
-    )
+    input_grad = finish(inputs, cotangent, own_grad, gain.reshape(1, model))
     return (
         outputs,
-        input_grad.astype(BF16),
-        pair[0],
-        pair[1],
+        input_grad,
+        gain_out,
+        shift_out,
         qkv_out,
         qkv_bias_out,
         out_out,

time: 195 us -> 185 us (0.949)
  local copies, waits for them, and re-layouts: 23.6 us -> 15.6 us
  Pallas kernels: 62.5 us -> 70.2 us
  waiting for transfers between devices: 48.9 us -> 44.7 us
  other arithmetic: 18.6 us -> 15.1 us
    pallas_call x2 -> x5, Pallas kernels: 13.7 us -> 21.4 us  [the longest x4 18.9 us: weight_half(): pl.pallas_call(kernel, grid_spec=pltpu.PrefetchScalarGridSpec(num_scalar_...]
    reduce_scatter x1, waiting for transfers between devices: 6.61 us -> 0.01 us  [body(): lax.psum_scatter(branch.reshape(seqs, length, model), 'tensor', scatter_d...]
    dynamic_slice x3 -> x2, local copies, waits for them, and re-layouts: 2.73 us -> 0.05 us  [the longest x1 0.04 us: body(): lax.dynamic_index_in_dim(pair, (me_z + k) % tensor, 2, keepdims=False)]
    unnamed x39 -> x21, local copies, waits for them, and re-layouts: 6 us -> 3.64 us
    convert_element_type x4 -> x2, local copies, waits for them, and re-layouts: 2.42 us -> 0.18 us  [exchange(): lax.dynamic_index_in_dim(x, chip ^ k, 0, keepdims=False).astype(BF16)]
    ppermute x1 -> x0, local copies, waits for them, and re-layouts: 2.19 us -> none  [swap(): return lax.ppermute(x, axis_name, [(i, i ^ step) for i in range(size)])]
    add x9 -> x5, other arithmetic: 5.56 us -> 3.64 us  [the longest x2 3.41 us: exchange(): x = kept + got.astype(F32)]
    ppermute x18 -> x17, waiting for transfers between devices: 27.7 us -> 27.3 us  [swap(): return lax.ppermute(x, axis_name, [(i, i ^ step) for i in range(size)])]
  transfers between devices with their start and end apart: 28 -> 27, of which waited for: 13 -> 11; matrix products, arithmetic and copies ran while one was open for 20% -> 17% of each run, Pallas kernels for 18% -> 37%
where the time goes in v1:
time: 185 us; the launch traced here: 184 us
  Pallas kernels  70.2 us (38%)
  waiting for transfers between devices  44.7 us (24%)
  starting transfers between devices  24.4 us (13%)
  local copies, waits for them, and re-layouts  15.6 us (8%)
  other arithmetic  15.1 us (8%)
  between operations  14.3 us (8%)
    ppermute x17, waiting for transfers between devices, swap(): return lax.ppermute(x, axis_name, [(i, i ^ step) for i in range(size)])  27.3 us
    pallas_call x4, Pallas kernels, weight_half(): pl.pallas_call(kernel, grid_spec=pltpu.PrefetchScalarGridSpec(num_scalar_...  18.9 us
    ppermute x17, starting transfers between devices, swap(): return lax.ppermute(x, axis_name, [(i, i ^ step) for i in range(size)])  14.6 us
    all_gather x1, waiting for transfers between devices, body(): lax.all_gather(cotangent, 'tensor', axis=1, tiled=True).reshape(rows, model)  12.9 us
    pallas_call x1, Pallas kernels, attend_back(): pl.pallas_call(functools.partial(backward_kernel, scale, block), grid=(se...  12.6 us
    pallas_call x1, Pallas kernels, enter(): pl.pallas_call(functools.partial(enter_kernel, heads, head_dim), grid=(ro...  8.56 us
    pallas_call x1, Pallas kernels, norm_sum(): pl.pallas_call(norm_kernel, grid=(rows // block,), in_specs=[tokens(block...  7.79 us
    pallas_call x1, Pallas kernels, return_grads(): pl.pallas_call(return_kernel, grid=(rows // block,), in_specs=[pl.BlockSp...  6.9 us
  transfers between devices with their start and end apart: 27, of which 11 were waited for; matrix products, arithmetic and copies ran while one was open for 17% of the time, Pallas kernels for 37%

profile of v1, /device:TPU:0, one launch (start us, length us, event | category | flops | bytes accessed | tf_op | source)
XLA Modules:
  0.0 184.2 jit_solution(8919462881656580673)
XLA Ops:
  9.4 5.1 %collective-permute-start.2 = (f32[3,24]{1,0:T(4,128)S(1)}, f32[3,24]{1,0:T(4,128)S(1)}, u32[]{:S(2)}, u32[]{:S(2)}) collective-permute-start(f32[3,24]{1,0:T(4,128)S(1)} %get-tuple-element.115), channel_id=1, source_target_pairs={{0,3},{1,0},{2,1},{3,2},{4,7},{5,4},{6,5},{7,6},{8,11},{9,8},{10,9... | collective-permute-start | bytes 872 | tf_op jit(solution)/shard_map/ppermute | solution.py:527
  20.2 1.6 collective-permute-start.9
  23.6 3.1 %collective-permute-done.3 = f32[8,128]{1,0:T(8,128)S(1)} collective-permute-done((f32[8,128]{1,0:T(8,128)S(1)}, f32[8,128]{1,0:T(8,128)S(1)}, u32[]{:S(2)}, u32[]{:S(2)}) %collective-permute-start.3) | collective-permute-done | bytes 4128 | tf_op jit(solution)/shard_map/ppermute | solution.py:28
  30.5 5.5 %collective-permute-done.7 = bf16[2,96,960]{2,1,0:T(8,128)(2,1)S(1)} collective-permute-done((bf16[2,96,960]{2,1,0:T(8,128)(2,1)S(1)}, bf16[2,96,960]{2,1,0:T(8,128)(2,1)S(1)}, u32[]{:S(2)}, u32[]{:S(2)}) %collective-permute-start.7) | collective-permute-done | bytes 368672 | tf_op jit(solution)/shard_map/ppermute | solution.py:28
  37.0 3.4 %collective-permute-done.10 = bf16[2,96,1344]{2,1,0:T(8,128)(2,1)S(1)} collective-permute-done((bf16[2,96,1344]{2,1,0:T(8,128)(2,1)S(1)}, bf16[2,96,1344]{2,1,0:T(8,128)(2,1)S(1)}, u32[]{:S(2)}, u32[]{:S(2)}) %collective-permute-start.10) | collective-permute-done | bytes 516128 | tf_op jit(solution)/shard_map/ppermute | solution.py:28
  52.1 8.6 %enter.1 = (bf16[768,1024]{1,0:T(8,128)(2,1)}, bf16[576,1024]{1,0:T(8,128)(2,1)}, bf16[1024,768]{1,0:T(8,128)(2,1)}, f32[1024,768]{1,0:T(8,128)}) custom-call(bf16[1024,768]{1,0:T(8,128)(2,1)} %bitcast.137, f32[3,768]{1,0:T(4,128)} %reshape.196.vec_ref, f32[1,768]{1,0:T(1,128)} %reshape_reshape.16.in_bias_ref, f32[1,576]{1,0:T(1,128)} %reshape_reshape.17.qkv_bias_ref, ...), custom_call_target="tpu_custom_call" | custom-call | flops 2113929216 | bytes 12976128 | tf_op jit(solution)/shard_map/enter/pallas_call | solution.py:295
  60.7 6.8 %attend_forward.1 = (bf16[192,1024]{1,0:T(8,128)(2,1)}, f32[3,8,1024]{2,1,0:T(8,128)}) custom-call(bf16[576,1024]{1,0:T(8,128)(2,1)} %get-tuple-element.32.q_ref.k_ref.v_ref, bf16[576,1024]{1,0:T(8,128)(2,1)} %get-tuple-element.32.q_ref.k_ref.v_ref, bf16[576,1024]{1,0:T(8,128)(2,1)} %get-tuple-element.32.q_ref.k_ref.v_ref), custom_call_target="tpu_custom_call" | custom-call | flops 805306368 | bytes 2359296 | tf_op jit(solution)/shard_map/attend_forward/pallas_call | solution.py:327
  67.6 6.1 %branch.1 = (bf16[1024,768]{1,0:T(8,128)(2,1)}, bf16[1024,192]{1,0:T(8,128)(2,1)}) custom-call(bf16[192,1024]{1,0:T(8,128)(2,1)} %get-tuple-element.33.ctx_t_ref, bf16[1024,768]{1,0:T(8,128)(2,1)} %get-tuple-element.34.hidden_ref, bf16[768,960]{1,0:T(8,128)(2,1)} %bitcast.132, bf16[768,1344]{1,0:T(8,128)(2,1)} %bitcast.128), custom_call_target="tpu_custom_call" | custom-call | flops 1509949440 | bytes 6291456 | tf_op jit(solution)/shard_map/branch/pallas_call | solution.py:370
  74.0 12.9 %all-gather.5.cloned.1.call-done = bf16[1,1024,768]{2,1,0:T(8,128)(2,1)} async-done(((bf16[1,256,768]{2,1,0:T(8,128)(2,1)}), bf16[1,1024,768]{2,1,0:T(8,128)(2,1)}) %all-gather.5.cloned.1.call-update) | async-done | bytes 1572880 | tf_op jit(solution)/shard_map/all_gather | solution.py:521
  86.9 6.9 %return_grads.1 = (bf16[768,1024]{1,0:T(8,128)(2,1)}, bf16[192,1024]{1,0:T(8,128)(2,1)}, bf16[1024,768]{1,0:T(8,128)(2,1)}, f32[8,768]{1,0:T(8,128)}, f32[8,768]{1,0:T(8,128)}) custom-call(bf16[1024,192]{1,0:T(8,128)(2,1)} %get-tuple-element.37.after_ref.ctx_ref, bf16[1024,768]{1,0:T(8,128)(2,1)} %bitcast.139, f32[1024,768]{1,0:T(8,128)} %get-tuple-element.38.slope_ref, ...), custom_call_target="tpu_custom_call" | custom-call | flops 1509949440 | bytes 7864320 | tf_op jit(solution)/shard_map/return_grads/pallas_call | solution.py:387
  93.8 12.6 %attend_backward.1 = (bf16[192,1024]{1,0:T(8,128)(2,1)}, bf16[192,1024]{1,0:T(8,128)(2,1)}, bf16[192,1024]{1,0:T(8,128)(2,1)}, f32[1,3,3,64,128]{4,3,2,1,0:T(8,128)}) custom-call(bf16[576,1024]{1,0:T(8,128)(2,1)} %get-tuple-element.32.q_ref.k_ref.v_ref, bf16[576,1024]{1,0:T(8,128)(2,1)} %get-tuple-element.32.q_ref.k_ref.v_ref, ...), custom_call_target="tpu_custom_call" | custom-call | flops 2013265920 | bytes 3538944 | tf_op jit(solution)/shard_map/attend_backward/pallas_call | solution.py:353
  106.4 7.8 %norm_grads.1 = (bf16[1024,576]{1,0:T(8,128)(2,1)}, bf16[1024,768]{1,0:T(8,128)(2,1)}, f32[8,768]{1,0:T(8,128)}, f32[8,768]{1,0:T(8,128)}) custom-call(bf16[1024,768]{1,0:T(8,128)(2,1)} %bitcast.138, bf16[192,1024]{1,0:T(8,128)(2,1)} %get-tuple-element.40.dq_ref, bf16[192,1024]{1,0:T(8,128)(2,1)} %get-tuple-element.41.dk_ref, ...), custom_call_target="tpu_custom_call" | custom-call | flops 2113929216 | bytes 6291456 | tf_op jit(solution)/shard_map/norm_grads/pallas_call | solution.py:412
  119.4 2.4 %collective-permute-done.13 = f32[2,8,24]{2,1,0:T(8,128)S(1)} collective-permute-done((f32[2,8,24]{2,1,0:T(8,128)S(1)}, f32[2,8,24]{2,1,0:T(8,128)S(1)}, u32[]{:S(2)}, u32[]{:S(2)}) %collective-permute-start.13) | collective-permute-done | bytes 1568 | tf_op jit(solution)/shard_map/ppermute | solution.py:617
  123.8 3.4 %shard_map.195 = bf16[4,112,576]{2,1,0:T(8,128)(2,1)} custom-call(s32[1]{0:T(128)} %bitcast.53.bit_ref, bf16[768,1024]{1,0:T(8,128)(2,1)} %get-tuple-element.45.normed_t_ref, bf16[1024,576]{1,0:T(8,128)(2,1)} %get-tuple-element.46.proj_low_ref, f32[8,16,576]{2,1,0:T(8,128)} %pad.9.small_ref), custom_call_target="tpu_custom_call" | custom-call | flops 452984832 | bytes 3145728 | tf_op jit(solution)/shard_map/pallas_call | solution.py:459
  127.3 5.7 %shard_map.197 = bf16[4,96,1728]{2,1,0:T(8,128)(2,1)} custom-call(s32[1]{0:T(128)} %bitcast.53.bit_ref, bf16[768,1024]{1,0:T(8,128)(2,1)} %get-tuple-element.45.normed_t_ref, bf16[768,1024]{1,0:T(8,128)(2,1)} %get-tuple-element.52.cot_t_ref, bf16[1024,768]{1,0:T(8,128)(2,1)} %get-tuple-element.43.pre_low_ref, ...), custom_call_target="tpu_custom_call" | custom-call | flops 1358954496 | bytes 3145728 | tf_op jit(solution)/shard_map/pallas_call | solution.py:459
  133.5 3.6 %shard_map.194 = f32[4,112,576]{2,1,0:T(8,128)} custom-call(s32[1]{0:T(128)} %bitcast.40.bit_ref, bf16[768,1024]{1,0:T(8,128)(2,1)} %get-tuple-element.45.normed_t_ref, bf16[1024,576]{1,0:T(8,128)(2,1)} %get-tuple-element.46.proj_low_ref, f32[8,16,576]{2,1,0:T(8,128)} %pad.9.small_ref), custom_call_target="tpu_custom_call" | custom-call | flops 452984832 | bytes 3145728 | tf_op jit(solution)/shard_map/pallas_call | solution.py:459
  138.6 2.4 %collective-permute-start.18 = (bf16[112,576]{1,0:T(8,128)(2,1)S(1)}, bf16[112,576]{1,0:T(8,128)(2,1)S(1)}, u32[]{:S(2)}, u32[]{:S(2)}) collective-permute-start(bf16[112,576]{1,0:T(8,128)(2,1)S(1)} %get-tuple-element.85), channel_id=1, source_target_pairs={{0,24},{4,28},{8,16},{12,20},{16,8},{20,12},{24,0},{28,4},{1,25},{... | collective-permute-start | bytes 387080 | tf_op jit(solution)/shard_map/ppermute | solution.py:28
  142.9 6.1 %shard_map.196 = f32[4,96,1728]{2,1,0:T(8,128)} custom-call(s32[1]{0:T(128)} %bitcast.40.bit_ref, bf16[768,1024]{1,0:T(8,128)(2,1)} %get-tuple-element.45.normed_t_ref, bf16[768,1024]{1,0:T(8,128)(2,1)} %get-tuple-element.52.cot_t_ref, bf16[1024,768]{1,0:T(8,128)(2,1)} %get-tuple-element.43.pre_low_ref, ...), custom_call_target="tpu_custom_call" | custom-call | flops 1358954496 | bytes 3145728 | tf_op jit(solution)/shard_map/pallas_call | solution.py:459
  151.7 2.0 %convert_add_fusion = f32[4,96,1728]{2,1,0:T(8,128)S(1)} fusion(f32[4,96,1728]{2,1,0:T(8,128)} %shard_map.196, bf16[4,96,1728]{2,1,0:T(8,128)(2,1)S(1)} %collective-permute-done.19), kind=kLoop, calls=%fused_computation.1 | loop fusion | flops 1327104 | bytes 6635520 | tf_op jit(solution)/shard_map/add | solution.py:490
  153.9 2.4 %collective-permute-start.22 = (bf16[96,1728]{1,0:T(8,128)(2,1)S(1)}, bf16[96,1728]{1,0:T(8,128)(2,1)S(1)}, u32[]{:S(2)}, u32[]{:S(2)}) collective-permute-start(bf16[96,1728]{1,0:T(8,128)(2,1)S(1)} %get-tuple-element.78), channel_id=1, source_target_pairs={{0,24},{4,28},{8,16},{12,20},{16,8},{20,12},{24,0},{28,4},{1,25},{... | collective-permute-start | bytes 995336 | tf_op jit(solution)/shard_map/ppermute | solution.py:28
  158.6 7.2 %collective-permute-done.22 = bf16[96,1728]{1,0:T(8,128)(2,1)S(1)} collective-permute-done((bf16[96,1728]{1,0:T(8,128)(2,1)S(1)}, bf16[96,1728]{1,0:T(8,128)(2,1)S(1)}, u32[]{:S(2)}, u32[]{:S(2)}) %collective-permute-start.22) | collective-permute-done | bytes 331808 | tf_op jit(solution)/shard_map/ppermute | solution.py:28
  165.8 5.7 %collective-permute-done.21 = bf16[96,1728]{1,0:T(8,128)(2,1)S(1)} collective-permute-done((bf16[96,1728]{1,0:T(8,128)(2,1)S(1)}, bf16[96,1728]{1,0:T(8,128)(2,1)S(1)}, u32[]{:S(2)}, u32[]{:S(2)}) %collective-permute-start.21) | collective-permute-done | bytes 331808 | tf_op jit(solution)/shard_map/ppermute | solution.py:28
  173.3 1.9 %add_convert_fusion = bf16[1,256,768]{2,1,0:T(8,128)(2,1)} fusion(bf16[1,256,768]{2,1,0:T(8,128)(2,1)} %reduce-scatter.3.cloned.1.call-done, bf16[1,256,768]{2,1,0:T(8,128)(2,1)S(1)} %copy-done, f32[768]{0:T(1024)S(1)} %add.170), kind=kLoop, calls=%fused_computation.9 | loop fusion | flops 983040 | bytes 1182720 | tf_op jit(solution)/shard_map/convert_element_type | solution.py:575
  175.2 2.5 %finish.1 = bf16[1,256,768]{2,1,0:T(8,128)(2,1)} custom-call(bf16[1,256,768]{2,1,0:T(8,128)(2,1)} %x_ref.1, bf16[1,256,768]{2,1,0:T(8,128)(2,1)} %cot_ref.1, bf16[1,256,768]{2,1,0:T(8,128)(2,1)} %reduce-scatter.5.cloned.1.call-done.own_ref, f32[1,768]{1,0:T(1,128)} %slice.83.gain_ref), custom_call_target="tpu_custom_call" | custom-call | flops 3932160 | bytes 1572864 | tf_op jit(solution)/shard_map/finish/pallas_call | solution.py:446
  (156 shorter events, 44.1 us)
Async XLA Ops:
  7.2 44.9 %all-gather.3.cloned.1.call-start = ((), (), s32[]{:S(2)}) async-start(), calls=%async_computation.2 | async-start | bytes 1966080 | tf_op jit(solution)/shard_map/all_gather | solution.py:520
  8.0 78.9 %all-gather.5.cloned.1.call-start = ((), (), s32[]{:S(2)}) async-start(), calls=%async_computation.4 | async-start | bytes 1966080 | tf_op jit(solution)/shard_map/all_gather | solution.py:521
  9.4 12.7 %collective-permute-start.2 = (f32[3,24]{1,0:T(4,128)S(1)}, f32[3,24]{1,0:T(4,128)S(1)}, u32[]{:S(2)}, u32[]{:S(2)}) collective-permute-start(f32[3,24]{1,0:T(4,128)S(1)} %get-tuple-element.115), channel_id=1, source_target_pairs={{0,3},{1,0},{2,1},{3,2},{4,7},{5,4},{6,5},{7,6},{8,11},{9,8},{10,9... | collective-permute-start | bytes 872 | tf_op jit(solution)/shard_map/ppermute | solution.py:527
  14.6 7.6 %collective-permute-start.1 = (f32[3,24]{1,0:T(4,128)S(1)}, f32[3,24]{1,0:T(4,128)S(1)}, u32[]{:S(2)}, u32[]{:S(2)}) collective-permute-start(f32[3,24]{1,0:T(4,128)S(1)} %get-tuple-element.115), channel_id=1, source_target_pairs={{0,2},{1,3},{2,0},{3,1},{4,6},{5,7},{6,4},{7,5},{8,10},{9,11},{10,... | collective-permute-start | bytes 872 | tf_op jit(solution)/shard_map/ppermute | solution.py:527
  14.6 7.6 %collective-permute-start = (f32[3,24]{1,0:T(4,128)S(1)}, f32[3,24]{1,0:T(4,128)S(1)}, u32[]{:S(2)}, u32[]{:S(2)}) collective-permute-start(f32[3,24]{1,0:T(4,128)S(1)} %get-tuple-element.115), channel_id=1, source_target_pairs={{0,1},{1,2},{2,3},{3,0},{4,5},{5,6},{6,7},{7,4},{8,9},{9,10},{10,1... | collective-permute-start | bytes 872 | tf_op jit(solution)/shard_map/ppermute | solution.py:527
  17.4 9.8 %collective-permute-start.6 = (bf16[96,960]{1,0:T(8,128)(2,1)S(1)}, bf16[96,960]{1,0:T(8,128)(2,1)S(1)}, u32[]{:S(2)}, u32[]{:S(2)}) collective-permute-start(bf16[96,960]{1,0:T(8,128)(2,1)S(1)} %pad_maximum_fusion.7), channel_id=1, source_target_pairs={{0,8},{4,12},{8,0},{12,4},{16,24},{20,28},{24,16},{28,20},{1,9},{5... | collective-permute-start | bytes 552968 | tf_op jit(solution)/shard_map/ppermute | solution.py:28
  20.2 8.7 %collective-permute-start.9 = (bf16[96,1344]{1,0:T(8,128)(2,1)S(1)}, bf16[96,1344]{1,0:T(8,128)(2,1)S(1)}, u32[]{:S(2)}, u32[]{:S(2)}) collective-permute-start(bf16[96,1344]{1,0:T(8,128)(2,1)S(1)} %pad_maximum_fusion.6), channel_id=1, source_target_pairs={{0,16},{4,20},{8,24},{12,28},{16,0},{20,4},{24,8},{28,12},{1,17},{... | collective-permute-start | bytes 774152 | tf_op jit(solution)/shard_map/ppermute | solution.py:28
  21.8 151.5 %reduce-scatter.3.cloned.1.call-start = ((), (), s32[]{:S(2)}) async-start(), calls=%async_computation.3 | async-start | bytes 1966080 | tf_op jit(solution)/shard_map/reduce_scatter | solution.py:572
  27.4 8.6 %collective-permute-start.7 = (bf16[2,96,960]{2,1,0:T(8,128)(2,1)S(1)}, bf16[2,96,960]{2,1,0:T(8,128)(2,1)S(1)}, u32[]{:S(2)}, u32[]{:S(2)}) collective-permute-start(bf16[2,96,960]{2,1,0:T(8,128)(2,1)S(1)} %pad_maximum_fusion.5), channel_id=1, source_target_pairs={{0,16},{4,20},{8,24},{12,28},{16,0},{20,4},{24,8},{28,12},{1,17},{... | collective-permute-start | bytes 1105928 | tf_op jit(solution)/shard_map/ppermute | solution.py:28
  29.1 11.4 %collective-permute-start.10 = (bf16[2,96,1344]{2,1,0:T(8,128)(2,1)S(1)}, bf16[2,96,1344]{2,1,0:T(8,128)(2,1)S(1)}, u32[]{:S(2)}, u32[]{:S(2)}) collective-permute-start(bf16[2,96,1344]{2,1,0:T(8,128)(2,1)S(1)} %pad_maximum_fusion.4), channel_id=1, source_target_pairs={{0,8},{4,12},{8,0},{12,4},{16,24},{20,28},{24,16},{28,20},{1,9},{5... | collective-permute-start | bytes 1548296 | tf_op jit(solution)/shard_map/ppermute | solution.py:28
  37.0 9.1 %collective-permute-start.8 = (bf16[2,2,96,960]{3,2,1,0:T(8,128)(2,1)}, bf16[2,2,96,960]{3,2,1,0:T(8,128)(2,1)}, u32[]{:S(2)}, u32[]{:S(2)}) collective-permute-start(bf16[2,2,96,960]{3,2,1,0:T(8,128)(2,1)} %pad_maximum_fusion.3), channel_id=1, source_target_pairs={{0,4},{4,0},{8,12},{12,8},{16,20},{20,16},{24,28},{28,24},{1,5},{5... | collective-permute-start | bytes 2211848 | tf_op jit(solution)/shard_map/ppermute | solution.py:28
  40.8 8.1 %collective-permute-start.11 = (bf16[2,2,96,1344]{3,2,0,1:T(8,128)(2,1)S(1)}, bf16[2,2,96,1344]{3,2,0,1:T(8,128)(2,1)}, u32[]{:S(2)}, u32[]{:S(2)}) collective-permute-start(bf16[2,2,96,1344]{3,2,0,1:T(8,128)(2,1)S(1)} %pad_maximum_fusion.2), channel_id=1, source_target_pairs={{0,4},{4,0},{8,12},{12,8},{16,20},{20,16},{24,28},{28,24},{1,5},{5... | collective-permute-start | bytes 3096584 | tf_op jit(solution)/shard_map/ppermute | solution.py:28
  73.7 101.5 %reduce-scatter.5.cloned.1.call-start = ((), (), s32[]{:S(2)}) async-start(), calls=%async_computation.5 | async-start | bytes 1966080 | tf_op jit(solution)/shard_map/reduce_scatter | solution.py:607
  115.2 4.2 %collective-permute-start.14 = (f32[2,8,24]{2,1,0:T(8,128)S(1)}, f32[2,8,24]{2,1,0:T(8,128)S(1)}, u32[]{:S(2)}, u32[]{:S(2)}) collective-permute-start(f32[2,8,24]{2,1,0:T(8,128)S(1)} %bitcast.163), channel_id=1, source_target_pairs={{0,3},{1,0},{2,1},{3,2},{4,7},{5,4},{6,5},{7,6},{8,11},{9,8},{10,9... | collective-permute-start | bytes 4616 | tf_op jit(solution)/shard_map/ppermute | solution.py:617
  116.5 5.2 %collective-permute-start.13 = (f32[2,8,24]{2,1,0:T(8,128)S(1)}, f32[2,8,24]{2,1,0:T(8,128)S(1)}, u32[]{:S(2)}, u32[]{:S(2)}) collective-permute-start(f32[2,8,24]{2,1,0:T(8,128)S(1)} %bitcast.162), channel_id=1, source_target_pairs={{0,2},{1,3},{2,0},{3,1},{4,6},{5,7},{6,4},{7,5},{8,10},{9,11},{10,... | collective-permute-start | bytes 4616 | tf_op jit(solution)/shard_map/ppermute | solution.py:617
  117.2 5.7 %collective-permute-start.12 = (f32[2,8,24]{2,1,0:T(8,128)S(1)}, f32[2,8,24]{2,1,0:T(8,128)S(1)}, u32[]{:S(2)}, u32[]{:S(2)}) collective-permute-start(f32[2,8,24]{2,1,0:T(8,128)S(1)} %bitcast.161), channel_id=1, source_target_pairs={{0,1},{1,2},{2,3},{3,0},{4,5},{5,6},{6,7},{7,4},{8,9},{9,10},{10,1... | collective-permute-start | bytes 4616 | tf_op jit(solution)/shard_map/ppermute | solution.py:617
  127.3 9.8 %collective-permute-start.15 = (bf16[4,112,576]{2,1,0:T(8,128)(2,1)}, bf16[4,112,576]{2,1,0:T(8,128)(2,1)S(1)}, u32[]{:S(2)}, u32[]{:S(2)}) collective-permute-start(bf16[4,112,576]{2,1,0:T(8,128)(2,1)} %shard_map.195), channel_id=1, source_target_pairs={{0,4},{4,0},{8,12},{12,8},{16,20},{20,16},{24,28},{28,24},{1,5},{5... | collective-permute-start | bytes 1548296 | tf_op jit(solution)/shard_map/ppermute | solution.py:28
  132.9 18.8 %collective-permute-start.19 = (bf16[4,96,1728]{2,1,0:T(8,128)(2,1)}, bf16[4,96,1728]{2,1,0:T(8,128)(2,1)S(1)}, u32[]{:S(2)}, u32[]{:S(2)}) collective-permute-start(bf16[4,96,1728]{2,1,0:T(8,128)(2,1)} %shard_map.197), channel_id=1, source_target_pairs={{0,4},{4,0},{8,12},{12,8},{16,20},{20,16},{24,28},{28,24},{1,5},{5... | collective-permute-start | bytes 3981320 | tf_op jit(solution)/shard_map/ppermute | solution.py:28
  138.6 10.5 %collective-permute-start.18 = (bf16[112,576]{1,0:T(8,128)(2,1)S(1)}, bf16[112,576]{1,0:T(8,128)(2,1)S(1)}, u32[]{:S(2)}, u32[]{:S(2)}) collective-permute-start(bf16[112,576]{1,0:T(8,128)(2,1)S(1)} %get-tuple-element.85), channel_id=1, source_target_pairs={{0,24},{4,28},{8,16},{12,20},{16,8},{20,12},{24,0},{28,4},{1,25},{... | collective-permute-start | bytes 387080 | tf_op jit(solution)/shard_map/ppermute | solution.py:28
  141.0 8.0 %collective-permute-start.17 = (bf16[112,576]{1,0:T(8,128)(2,1)S(1)}, bf16[112,576]{1,0:T(8,128)(2,1)S(1)}, u32[]{:S(2)}, u32[]{:S(2)}) collective-permute-start(bf16[112,576]{1,0:T(8,128)(2,1)S(1)} %get-tuple-element.86), channel_id=1, source_target_pairs={{0,16},{4,20},{8,24},{12,28},{16,0},{20,4},{24,8},{28,12},{1,17},{... | collective-permute-start | bytes 387080 | tf_op jit(solution)/shard_map/ppermute | solution.py:28
  141.5 7.5 %collective-permute-start.16 = (bf16[112,576]{1,0:T(8,128)(2,1)S(1)}, bf16[112,576]{1,0:T(8,128)(2,1)S(1)}, u32[]{:S(2)}, u32[]{:S(2)}) collective-permute-start(bf16[112,576]{1,0:T(8,128)(2,1)S(1)} %get-tuple-element.84), channel_id=1, source_target_pairs={{0,8},{4,12},{8,0},{12,4},{16,24},{20,28},{24,16},{28,20},{1,9},{5... | collective-permute-start | bytes 387080 | tf_op jit(solution)/shard_map/ppermute | solution.py:28
  153.9 11.9 %collective-permute-start.22 = (bf16[96,1728]{1,0:T(8,128)(2,1)S(1)}, bf16[96,1728]{1,0:T(8,128)(2,1)S(1)}, u32[]{:S(2)}, u32[]{:S(2)}) collective-permute-start(bf16[96,1728]{1,0:T(8,128)(2,1)S(1)} %get-tuple-element.78), channel_id=1, source_target_pairs={{0,24},{4,28},{8,16},{12,20},{16,8},{20,12},{24,0},{28,4},{1,25},{... | collective-permute-start | bytes 995336 | tf_op jit(solution)/shard_map/ppermute | solution.py:28
  156.3 15.2 %collective-permute-start.21 = (bf16[96,1728]{1,0:T(8,128)(2,1)S(1)}, bf16[96,1728]{1,0:T(8,128)(2,1)S(1)}, u32[]{:S(2)}, u32[]{:S(2)}) collective-permute-start(bf16[96,1728]{1,0:T(8,128)(2,1)S(1)} %get-tuple-element.79), channel_id=1, source_target_pairs={{0,16},{4,20},{8,24},{12,28},{16,0},{20,4},{24,8},{28,12},{1,17},{... | collective-permute-start | bytes 995336 | tf_op jit(solution)/shard_map/ppermute | solution.py:28
  156.8 14.7 %collective-permute-start.20 = (bf16[96,1728]{1,0:T(8,128)(2,1)S(1)}, bf16[96,1728]{1,0:T(8,128)(2,1)S(1)}, u32[]{:S(2)}, u32[]{:S(2)}) collective-permute-start(bf16[96,1728]{1,0:T(8,128)(2,1)S(1)} %get-tuple-element.77), channel_id=1, source_target_pairs={{0,8},{4,12},{8,0},{12,4},{16,24},{20,28},{24,16},{28,20},{1,9},{5... | collective-permute-start | bytes 995336 | tf_op jit(solution)/shard_map/ppermute | solution.py:28
  (11 other events, 111.3 us)
Sparse Core Ops, SparseCore 0:
  9.6 39.7 all-gather.2
  50.9 35.8 all-gather.4
  89.2 34.8 reduce-scatter.2
  133.6 34.2 reduce-scatter.4

commit v2 on v1

--- a/solution.py
+++ b/solution.py
@@ -233,36 +233,41 @@
     shift_sum_ref[...] += row_sums(norm_grad)
 
 
-def half_rows(ref, bit, blocks, part):
-    starts = [pl.multiple_of((2 * j + bit) * part, part) for j in range(blocks)]
+def half_rows(ref, at_ref, blocks, part):
+    chips = [lax.bitwise_xor(at_ref[1], k) for k in range(blocks)]
+    starts = [pl.multiple_of((2 * chip + at_ref[0]) * part, part) for chip in chips]
     return jnp.concatenate([ref[pl.ds(start, part), :] for start in starts], axis=0)
 
 
-def put(ref, columns, value):
-    blocks, part, _ = ref.shape
-    ref[:, :, columns] = value.reshape(blocks, part, -1).astype(ref.dtype)
-
-
-def early_kernel(
-    bit_ref, normed_t_ref, cot_t_ref, pre_low_ref, ctx_ref, hidden_ref, early_ref
-):
-    blocks, part, _ = early_ref.shape
-    hidden_units = hidden_ref.shape[1]
-    left = half_rows(normed_t_ref, bit_ref[0], blocks, part)
-    put(early_ref, slice(0, hidden_units), dot(left, pre_low_ref[...], (1, 0)))
-    left = half_rows(cot_t_ref, bit_ref[0], blocks, part)
-    put(early_ref, slice(hidden_units, 2 * hidden_units), dot(left, hidden_ref[...], (1, 0)))
-    put(early_ref, slice(2 * hidden_units, None), dot(left, ctx_ref[...], (1, 0)))
-
-
-def late_kernel(bit_ref, normed_t_ref, proj_low_ref, small_ref, late_ref):
-    blocks, total, columns = late_ref.shape
-    part = total - SMALL_ROWS
-    left = half_rows(normed_t_ref, bit_ref[0], blocks, part)
-    value = dot(left, proj_low_ref[...], (1, 0)).reshape(blocks, part, columns)
-    late_ref[:, :part] = value.astype(late_ref.dtype)
-    for block in range(blocks):
-        late_ref[block, part:] = small_ref[2 * block + bit_ref[0]].astype(late_ref.dtype)
+def put(outs, got_ref, rows, columns, value):
+    blocks = value.shape[0] // (rows.stop - rows.start)
+    value = value.reshape(blocks, rows.stop - rows.start, -1)
+    if got_ref is None:
+        outs[0][:, rows, columns] = value.astype(BF16)
+        return
+    value = value + got_ref[:, rows, columns].astype(F32)
+    for k in range(blocks):
+        outs[k][rows, columns] = value[k].astype(outs[k].dtype)
+
+
+def early_kernel(blocks, part, at_ref, normed_t_ref, cot_t_ref, pre_low_ref, ctx_ref, hidden_ref, *refs):
+    got_ref, outs = (None, refs) if len(refs) == 1 else (refs[0], refs[1:])
+    units = hidden_ref.shape[1]
+    rows = slice(0, part)
+    left = half_rows(normed_t_ref, at_ref, blocks, part)
+    put(outs, got_ref, rows, slice(0, units), dot(left, pre_low_ref[...], (1, 0)))
+    left = half_rows(cot_t_ref, at_ref, blocks, part)
+    put(outs, got_ref, rows, slice(units, 2 * units), dot(left, hidden_ref[...], (1, 0)))
+    put(outs, got_ref, rows, slice(2 * units, None), dot(left, ctx_ref[...], (1, 0)))
+
+
+def late_kernel(blocks, part, at_ref, normed_t_ref, proj_low_ref, small_ref, *refs):
+    got_ref, outs = (None, refs) if len(refs) == 1 else (refs[0], refs[1:])
+    left = half_rows(normed_t_ref, at_ref, blocks, part)
+    put(outs, got_ref, slice(0, part), slice(None), dot(left, proj_low_ref[...], (1, 0)))
+    members = [2 * lax.bitwise_xor(at_ref[1], k) + at_ref[0] for k in range(blocks)]
+    extra = jnp.concatenate([small_ref[member] for member in members], axis=0)
+    put(outs, got_ref, slice(part, part + SMALL_ROWS), slice(None), extra)
 
 
 def whole(x):
@@ -454,19 +459,23 @@
     )(x, cot, own, gain)
 
 
-def weight_half(kernel, bit, operands, shape, flops, dtype):
-    out = struct(*shape, dtype=dtype)
+def weight_half(kernel, at, operands, got, blocks, part, shape, flops):
+    if got is None:
+        outs = [struct(blocks, *shape)]
+    else:
+        operands = operands + (got,)
+        outs = [struct(*shape, dtype=F32)] + [struct(*shape)] * (blocks - 1)
     return pl.pallas_call(
-        kernel,
+        functools.partial(kernel, blocks, part),
         grid_spec=pltpu.PrefetchScalarGridSpec(
             num_scalar_prefetch=1,
             grid=(1,),
             in_specs=[whole(x) for x in operands],
-            out_specs=whole(out),
+            out_specs=[whole(x) for x in outs],
         ),
-        out_shape=out,
+        out_shape=outs,
         cost_estimate=cost(flops, 4 * operands[0].size),
-    )(bit.reshape(1).astype(jnp.int32), *operands)
+    )(jnp.stack(at).astype(jnp.int32), *operands)
 
 
 def rotary_tables(length):
@@ -485,20 +494,23 @@
     return kept, sent.astype(BF16)
 
 
-def exchange(kept, sent, dp):
-    got = swap(sent, "dp", dp, 1)
-    x = kept + got.astype(F32)
-    count = dp // 2
-    if count > 4:
-        steps = [1 << b for b in range(count.bit_length() - 1)]
-        return scatter_bits(x, 0, steps[::-1], BF16, dp, 2)
-    chip = lax.axis_index("dp") // 2
-    total = lax.dynamic_index_in_dim(x, chip, 0, keepdims=False)
-    for k in range(1, count):
-        piece = lax.dynamic_index_in_dim(x, chip ^ k, 0, keepdims=False).astype(BF16)
-        got = swap(piece, "dp", dp, 2 * k)
+def swap_core(sent, dp):
+    return swap(sent, "dp", dp, 1)
+
+
+def add_pieces(pieces, dp):
+    total = pieces[0]
+    for k in range(1, len(pieces)):
+        got = swap(pieces[k], "dp", dp, 2 * k)
         total = total + got.astype(F32)
     return total
+
+
+def exchange(grad, dp):
+    kept, sent = split_core(grad, dp)
+    x = kept + swap_core(sent, dp).astype(F32)
+    steps = [1 << b for b in range((dp // 2).bit_length() - 1)]
+    return scatter_bits(x, 0, steps[::-1], BF16, dp, 2)
 
 
 def body(
@@ -579,25 +591,32 @@
     )
     part = model // dp
     core = bit_of("dp", 1)
-    aligned = dp > 1 and part % 16 == 0
+    aligned = 2 <= dp <= 8 and part % 16 == 0
+    chip = lax.axis_index("dp") // 2
+    blocks = dp // 2
     if aligned:
         operands = (normed_t, cot_t, pre_low, context, hidden)
-        shape = (dp // 2, part, 2 * hidden_units + width)
-        flops = rows * model * shape[2]
-        early_sent = weight_half(early_kernel, 1 - core, operands, shape, flops, BF16)
-        early_kept = weight_half(early_kernel, core, operands, shape, flops, F32)
+        shape = (part, 2 * hidden_units + width)
+        flops = rows * model * shape[1]
+        (early_sent,) = weight_half(
+            early_kernel, (1 - core, chip), operands, None, blocks, part, shape, flops
+        )
+        early_got = swap_core(early_sent, dp)
+        early_pieces = weight_half(
+            early_kernel, (core, chip), operands, early_got, blocks, part,
+            shape, flops,
+        )
+        early = add_pieces(early_pieces, dp)
     else:
-        early_kept, early_sent = split_core(
-            jnp.concatenate(
-                [
-                    dot(normed_t, pre_low, (1, 0)),
-                    dot(cot_t, hidden, (1, 0)),
-                    dot(cot_t, context, (1, 0)),
-                ],
-                axis=1,
-            ),
-            dp,
+        early = jnp.concatenate(
+            [
+                dot(normed_t, pre_low, (1, 0)),
+                dot(cot_t, hidden, (1, 0)),
+                dot(cot_t, context, (1, 0)),
+            ],
+            axis=1,
         )
+        early = exchange(early, dp)
     dq_t, dk_t, dv_t, sums = attend_back(
         proj_t, cosine, sine, lse, ctx_grad_t, seqs, heads, head_dim, length
     )
@@ -635,16 +654,21 @@
     )
     if aligned:
         operands = (normed_t, proj_low, small)
-        shape = (dp // 2, part + SMALL_ROWS, columns)
+        shape = (part + SMALL_ROWS, columns)
         flops = rows * model * columns
-        late_sent = weight_half(late_kernel, 1 - core, operands, shape, flops, BF16)
-        late_kept = weight_half(late_kernel, core, operands, shape, flops, F32)
+        (late_sent,) = weight_half(
+            late_kernel, (1 - core, chip), operands, None, blocks, part, shape,
+            flops,
+        )
+        late_got = swap_core(late_sent, dp)
+        late_pieces = weight_half(
+            late_kernel, (core, chip), operands, late_got, blocks, part, shape,
+            flops,
+        )
+        late = add_pieces(late_pieces, dp)
     else:
         late = dot(normed_t, proj_low, (1, 0)).reshape(dp, part, columns)
-        late_kept, late_sent = split_core(jnp.concatenate([late, small], axis=1), dp)
-
-    early = exchange(early_kept, early_sent, dp)
-    late = exchange(late_kept, late_sent, dp)
+        late = exchange(jnp.concatenate([late, small], axis=1), dp)
     in_out = early[:, :hidden_units]
     down_out = early[:, hidden_units : 2 * hidden_units].T
     out_out = early[:, 2 * hidden_units :].T

time: 185 us -> 193 us (1.043)
  waiting for transfers between devices: 44.7 us -> 48.6 us
  Pallas kernels: 70.2 us -> 73 us
    ppermute x17, waiting for transfers between devices: 27.3 us -> 35.5 us  [swap(): return lax.ppermute(x, axis_name, [(i, i ^ step) for i in range(size)])]
    ppermute x3, waiting for transfers between devices: 3.81 us -> 0.01 us  [body(): lax.ppermute(piece, 'tensor', [(i, (i + k) % tensor) for i in range(tenso...]
    pallas_call x4, Pallas kernels: 18.9 us -> 21.6 us  [weight_half(): pl.pallas_call(functools.partial(kernel, blocks, part), grid_spec=pltpu.P...]
    unnamed x21 -> x25, local copies, waits for them, and re-layouts: 3.64 us -> 5.55 us
  transfers between devices with their start and end apart: 27 -> 27, of which waited for: 11 -> 13; matrix products, arithmetic and copies ran while one was open for 17% -> 16% of each run, Pallas kernels for 37% -> 37%
where the time goes in v2:
time: 193 us; the launch traced here: 192 us
  Pallas kernels  73 us (38%)
  waiting for transfers between devices  48.6 us (25%)
  starting transfers between devices  24.3 us (13%)
  local copies, waits for them, and re-layouts  17.3 us (9%)
  other arithmetic  15 us (8%)
  between operations  14.3 us (7%)
    ppermute x17, waiting for transfers between devices, swap(): return lax.ppermute(x, axis_name, [(i, i ^ step) for i in range(size)])  35.5 us
    pallas_call x4, Pallas kernels, weight_half(): pl.pallas_call(functools.partial(kernel, blocks, part), grid_spec=pltpu.P...  21.6 us
    ppermute x17, starting transfers between devices, swap(): return lax.ppermute(x, axis_name, [(i, i ^ step) for i in range(size)])  14.4 us
    pallas_call x1, Pallas kernels, attend_back(): pl.pallas_call(functools.partial(backward_kernel, scale, block), grid=(se...  12.6 us
    all_gather x1, waiting for transfers between devices, body(): lax.all_gather(cotangent, 'tensor', axis=1, tiled=True).reshape(rows, model)  12.3 us
    pallas_call x1, Pallas kernels, enter(): pl.pallas_call(functools.partial(enter_kernel, heads, head_dim), grid=(ro...  8.55 us
    pallas_call x1, Pallas kernels, norm_sum(): pl.pallas_call(norm_kernel, grid=(rows // block,), in_specs=[tokens(block...  7.79 us
    pallas_call x1, Pallas kernels, return_grads(): pl.pallas_call(return_kernel, grid=(rows // block,), in_specs=[pl.BlockSp...  6.92 us
  transfers between devices with their start and end apart: 27, of which 13 were waited for; matrix products, arithmetic and copies ran while one was open for 16% of the time, Pallas kernels for 37%

profile of v2, /device:TPU:0, one launch (start us, length us, event | category | flops | bytes accessed | tf_op | source)
XLA Modules:
  0.0 192.3 jit_solution(17058865665358853191)
XLA Ops:
  9.4 5.1 %collective-permute-start.2 = (f32[3,24]{1,0:T(4,128)S(1)}, f32[3,24]{1,0:T(4,128)S(1)}, u32[]{:S(2)}, u32[]{:S(2)}) collective-permute-start(f32[3,24]{1,0:T(4,128)S(1)} %get-tuple-element.125), channel_id=1, source_target_pairs={{0,3},{1,0},{2,1},{3,2},{4,7},{5,4},{6,5},{7,6},{8,11},{9,8},{10,9... | collective-permute-start | bytes 872 | tf_op jit(solution)/shard_map/ppermute | solution.py:539
  20.2 1.6 collective-permute-start.9
  23.6 3.1 %collective-permute-done.3 = f32[8,128]{1,0:T(8,128)S(1)} collective-permute-done((f32[8,128]{1,0:T(8,128)S(1)}, f32[8,128]{1,0:T(8,128)S(1)}, u32[]{:S(2)}, u32[]{:S(2)}) %collective-permute-start.3) | collective-permute-done | bytes 4128 | tf_op jit(solution)/shard_map/ppermute | solution.py:28
  30.5 5.5 %collective-permute-done.7 = bf16[2,96,960]{2,1,0:T(8,128)(2,1)S(1)} collective-permute-done((bf16[2,96,960]{2,1,0:T(8,128)(2,1)S(1)}, bf16[2,96,960]{2,1,0:T(8,128)(2,1)S(1)}, u32[]{:S(2)}, u32[]{:S(2)}) %collective-permute-start.7) | collective-permute-done | bytes 368672 | tf_op jit(solution)/shard_map/ppermute | solution.py:28
  37.0 3.4 %collective-permute-done.10 = bf16[2,96,1344]{2,1,0:T(8,128)(2,1)S(1)} collective-permute-done((bf16[2,96,1344]{2,1,0:T(8,128)(2,1)S(1)}, bf16[2,96,1344]{2,1,0:T(8,128)(2,1)S(1)}, u32[]{:S(2)}, u32[]{:S(2)}) %collective-permute-start.10) | collective-permute-done | bytes 516128 | tf_op jit(solution)/shard_map/ppermute | solution.py:28
  52.1 8.6 %enter.1 = (bf16[768,1024]{1,0:T(8,128)(2,1)}, bf16[576,1024]{1,0:T(8,128)(2,1)}, bf16[1024,768]{1,0:T(8,128)(2,1)}, f32[1024,768]{1,0:T(8,128)}) custom-call(bf16[1024,768]{1,0:T(8,128)(2,1)} %bitcast.114, f32[3,768]{1,0:T(4,128)} %reshape.182.vec_ref, f32[1,768]{1,0:T(1,128)} %reshape_reshape.16.in_bias_ref, f32[1,576]{1,0:T(1,128)} %reshape_reshape.17.qkv_bias_ref, ...), custom_call_target="tpu_custom_call" | custom-call | flops 2113929216 | bytes 12976128 | tf_op jit(solution)/shard_map/enter/pallas_call | solution.py:300
  60.7 6.8 %attend_forward.1 = (bf16[192,1024]{1,0:T(8,128)(2,1)}, f32[3,8,1024]{2,1,0:T(8,128)}) custom-call(bf16[576,1024]{1,0:T(8,128)(2,1)} %get-tuple-element.40.q_ref.k_ref.v_ref, bf16[576,1024]{1,0:T(8,128)(2,1)} %get-tuple-element.40.q_ref.k_ref.v_ref, bf16[576,1024]{1,0:T(8,128)(2,1)} %get-tuple-element.40.q_ref.k_ref.v_ref), custom_call_target="tpu_custom_call" | custom-call | flops 805306368 | bytes 2359296 | tf_op jit(solution)/shard_map/attend_forward/pallas_call | solution.py:332
  67.5 6.1 %branch.1 = (bf16[1024,768]{1,0:T(8,128)(2,1)}, bf16[1024,192]{1,0:T(8,128)(2,1)}) custom-call(bf16[192,1024]{1,0:T(8,128)(2,1)} %get-tuple-element.41.ctx_t_ref, bf16[1024,768]{1,0:T(8,128)(2,1)} %get-tuple-element.42.hidden_ref, bf16[768,960]{1,0:T(8,128)(2,1)} %bitcast.109, bf16[768,1344]{1,0:T(8,128)(2,1)} %bitcast.105), custom_call_target="tpu_custom_call" | custom-call | flops 1509949440 | bytes 6291456 | tf_op jit(solution)/shard_map/branch/pallas_call | solution.py:375
  74.5 12.3 %all-gather.5.cloned.1.call-done = bf16[1,1024,768]{2,1,0:T(8,128)(2,1)} async-done(((bf16[1,256,768]{2,1,0:T(8,128)(2,1)}), bf16[1,1024,768]{2,1,0:T(8,128)(2,1)}) %all-gather.5.cloned.1.call-update) | async-done | bytes 1572880 | tf_op jit(solution)/shard_map/all_gather | solution.py:533
  86.9 6.9 %return_grads.1 = (bf16[768,1024]{1,0:T(8,128)(2,1)}, bf16[192,1024]{1,0:T(8,128)(2,1)}, bf16[1024,768]{1,0:T(8,128)(2,1)}, f32[8,768]{1,0:T(8,128)}, f32[8,768]{1,0:T(8,128)}) custom-call(bf16[1024,192]{1,0:T(8,128)(2,1)} %get-tuple-element.45.after_ref.ctx_ref, bf16[1024,768]{1,0:T(8,128)(2,1)} %bitcast.116, f32[1024,768]{1,0:T(8,128)} %get-tuple-element.46.slope_ref, ...), custom_call_target="tpu_custom_call" | custom-call | flops 1509949440 | bytes 7864320 | tf_op jit(solution)/shard_map/return_grads/pallas_call | solution.py:392
  93.8 12.6 %attend_backward.1 = (bf16[192,1024]{1,0:T(8,128)(2,1)}, bf16[192,1024]{1,0:T(8,128)(2,1)}, bf16[192,1024]{1,0:T(8,128)(2,1)}, f32[1,3,3,64,128]{4,3,2,1,0:T(8,128)}) custom-call(bf16[576,1024]{1,0:T(8,128)(2,1)} %get-tuple-element.40.q_ref.k_ref.v_ref, bf16[576,1024]{1,0:T(8,128)(2,1)} %get-tuple-element.40.q_ref.k_ref.v_ref, ...), custom_call_target="tpu_custom_call" | custom-call | flops 2013265920 | bytes 3538944 | tf_op jit(solution)/shard_map/attend_backward/pallas_call | solution.py:358
  106.4 7.8 %norm_grads.1 = (bf16[1024,576]{1,0:T(8,128)(2,1)}, bf16[1024,768]{1,0:T(8,128)(2,1)}, f32[8,768]{1,0:T(8,128)}, f32[8,768]{1,0:T(8,128)}) custom-call(bf16[1024,768]{1,0:T(8,128)(2,1)} %bitcast.115, bf16[192,1024]{1,0:T(8,128)(2,1)} %get-tuple-element.48.dq_ref, bf16[192,1024]{1,0:T(8,128)(2,1)} %get-tuple-element.49.dk_ref, ...), custom_call_target="tpu_custom_call" | custom-call | flops 2113929216 | bytes 6291456 | tf_op jit(solution)/shard_map/norm_grads/pallas_call | solution.py:417
  118.8 6.5 %shard_map.196 = bf16[4,96,1728]{2,1,0:T(8,128)(2,1)} custom-call(s32[2]{0:T(128)} %pad_add_fusion.1.at_ref, bf16[768,1024]{1,0:T(8,128)(2,1)} %get-tuple-element.53.normed_t_ref, bf16[768,1024]{1,0:T(8,128)(2,1)} %get-tuple-element.64.cot_t_ref, bf16[1024,768]{1,0:T(8,128)(2,1)} %get-tuple-element.51.pre_low_ref, ...), custom_call_target="tpu_custom_call" | custom-call | flops 1358954496 | bytes 3145728 | tf_op jit(solution)/shard_map/pallas_call | solution.py:468
  126.6 4.1 %shard_map.194 = bf16[4,112,576]{2,1,0:T(8,128)(2,1)} custom-call(s32[2]{0:T(128)} %pad_add_fusion.1.at_ref, bf16[768,1024]{1,0:T(8,128)(2,1)} %get-tuple-element.53.normed_t_ref, bf16[1024,576]{1,0:T(8,128)(2,1)} %get-tuple-element.54.proj_low_ref, f32[8,16,576]{2,1,0:T(8,128)} %pad.9.small_ref), custom_call_target="tpu_custom_call" | custom-call | flops 452984832 | bytes 3145728 | tf_op jit(solution)/shard_map/pallas_call | solution.py:468
  133.9 4.2 %shard_map.195 = (f32[112,576]{1,0:T(8,128)}, bf16[112,576]{1,0:T(8,128)(2,1)}, bf16[112,576]{1,0:T(8,128)(2,1)}, bf16[112,576]{1,0:T(8,128)(2,1)}) custom-call(s32[2]{0:T(128)} %pad_add_fusion.at_ref, bf16[768,1024]{1,0:T(8,128)(2,1)} %get-tuple-element.53.normed_t_ref, bf16[1024,576]{1,0:T(8,128)(2,1)} %get-tuple-element.54.proj_low_ref, ...), custom_call_target="tpu_custom_call" | custom-call | flops 452984832 | bytes 3145728 | tf_op jit(solution)/shard_map/pallas_call | solution.py:468
  138.1 2.4 %collective-permute-start.18 = (bf16[112,576]{1,0:T(8,128)(2,1)}, bf16[112,576]{1,0:T(8,128)(2,1)S(1)}, u32[]{:S(2)}, u32[]{:S(2)}) collective-permute-start(bf16[112,576]{1,0:T(8,128)(2,1)} %get-tuple-element.63), channel_id=1, source_target_pairs={{0,24},{4,28},{8,16},{12,20},{16,8},{20,12},{24,0},{28,4},{1,25},{... | collective-permute-start | bytes 387080 | tf_op jit(solution)/shard_map/ppermute | solution.py:28
  142.4 3.5 %collective-permute-done.18 = bf16[112,576]{1,0:T(8,128)(2,1)S(1)} collective-permute-done((bf16[112,576]{1,0:T(8,128)(2,1)}, bf16[112,576]{1,0:T(8,128)(2,1)S(1)}, u32[]{:S(2)}, u32[]{:S(2)}) %collective-permute-start.18) | collective-permute-done | bytes 129056 | tf_op jit(solution)/shard_map/ppermute | solution.py:28
  145.9 2.5 %collective-permute-done.17 = bf16[112,576]{1,0:T(8,128)(2,1)S(1)} collective-permute-done((bf16[112,576]{1,0:T(8,128)(2,1)}, bf16[112,576]{1,0:T(8,128)(2,1)S(1)}, u32[]{:S(2)}, u32[]{:S(2)}) %collective-permute-start.17) | collective-permute-done | bytes 129056 | tf_op jit(solution)/shard_map/ppermute | solution.py:28
  153.1 6.8 %shard_map.197 = (f32[96,1728]{1,0:T(8,128)}, bf16[96,1728]{1,0:T(8,128)(2,1)}, bf16[96,1728]{1,0:T(8,128)(2,1)}, bf16[96,1728]{1,0:T(8,128)(2,1)}) custom-call(s32[2]{0:T(128)} %pad_add_fusion.at_ref, bf16[768,1024]{1,0:T(8,128)(2,1)} %get-tuple-element.53.normed_t_ref, bf16[768,1024]{1,0:T(8,128)(2,1)} %get-tuple-element.64.cot_t_ref, ...), custom_call_target="tpu_custom_call" | custom-call | flops 1358954496 | bytes 3145728 | tf_op jit(solution)/shard_map/pallas_call | solution.py:468
  159.9 1.7 collective-permute-start.22
  164.6 7.4 %collective-permute-done.22 = bf16[96,1728]{1,0:T(8,128)(2,1)S(1)} collective-permute-done((bf16[96,1728]{1,0:T(8,128)(2,1)}, bf16[96,1728]{1,0:T(8,128)(2,1)S(1)}, u32[]{:S(2)}, u32[]{:S(2)}) %collective-permute-start.22) | collective-permute-done | bytes 331808 | tf_op jit(solution)/shard_map/ppermute | solution.py:28
  172.0 6.5 %collective-permute-done.21 = bf16[96,1728]{1,0:T(8,128)(2,1)S(1)} collective-permute-done((bf16[96,1728]{1,0:T(8,128)(2,1)}, bf16[96,1728]{1,0:T(8,128)(2,1)S(1)}, u32[]{:S(2)}, u32[]{:S(2)}) %collective-permute-start.21) | collective-permute-done | bytes 331808 | tf_op jit(solution)/shard_map/ppermute | solution.py:28
  181.4 1.9 add_convert_fusion
  183.3 2.5 %finish.1 = bf16[1,256,768]{2,1,0:T(8,128)(2,1)} custom-call(bf16[1,256,768]{2,1,0:T(8,128)(2,1)} %x_ref.1, bf16[1,256,768]{2,1,0:T(8,128)(2,1)} %cot_ref.1, bf16[1,256,768]{2,1,0:T(8,128)(2,1)} %reduce-scatter.5.cloned.1.call-done.own_ref, f32[1,768]{1,0:T(1,128)} %slice.83.gain_ref), custom_call_target="tpu_custom_call" | custom-call | flops 3932160 | bytes 1572864 | tf_op jit(solution)/shard_map/finish/pallas_call | solution.py:451
  (158 shorter events, 48.2 us)
Async XLA Ops:
  7.2 44.9 %all-gather.3.cloned.1.call-start = ((), (), s32[]{:S(2)}) async-start(), calls=%async_computation.2 | async-start | bytes 1966080 | tf_op jit(solution)/shard_map/all_gather | solution.py:532
  8.0 78.9 %all-gather.5.cloned.1.call-start = ((), (), s32[]{:S(2)}) async-start(), calls=%async_computation.4 | async-start | bytes 1966080 | tf_op jit(solution)/shard_map/all_gather | solution.py:533
  9.4 12.7 %collective-permute-start.2 = (f32[3,24]{1,0:T(4,128)S(1)}, f32[3,24]{1,0:T(4,128)S(1)}, u32[]{:S(2)}, u32[]{:S(2)}) collective-permute-start(f32[3,24]{1,0:T(4,128)S(1)} %get-tuple-element.125), channel_id=1, source_target_pairs={{0,3},{1,0},{2,1},{3,2},{4,7},{5,4},{6,5},{7,6},{8,11},{9,8},{10,9... | collective-permute-start | bytes 872 | tf_op jit(solution)/shard_map/ppermute | solution.py:539
  14.6 7.6 %collective-permute-start.1 = (f32[3,24]{1,0:T(4,128)S(1)}, f32[3,24]{1,0:T(4,128)S(1)}, u32[]{:S(2)}, u32[]{:S(2)}) collective-permute-start(f32[3,24]{1,0:T(4,128)S(1)} %get-tuple-element.125), channel_id=1, source_target_pairs={{0,2},{1,3},{2,0},{3,1},{4,6},{5,7},{6,4},{7,5},{8,10},{9,11},{10,... | collective-permute-start | bytes 872 | tf_op jit(solution)/shard_map/ppermute | solution.py:539
  14.6 7.6 %collective-permute-start = (f32[3,24]{1,0:T(4,128)S(1)}, f32[3,24]{1,0:T(4,128)S(1)}, u32[]{:S(2)}, u32[]{:S(2)}) collective-permute-start(f32[3,24]{1,0:T(4,128)S(1)} %get-tuple-element.125), channel_id=1, source_target_pairs={{0,1},{1,2},{2,3},{3,0},{4,5},{5,6},{6,7},{7,4},{8,9},{9,10},{10,1... | collective-permute-start | bytes 872 | tf_op jit(solution)/shard_map/ppermute | solution.py:539
  17.4 9.8 %collective-permute-start.6 = (bf16[96,960]{1,0:T(8,128)(2,1)S(1)}, bf16[96,960]{1,0:T(8,128)(2,1)S(1)}, u32[]{:S(2)}, u32[]{:S(2)}) collective-permute-start(bf16[96,960]{1,0:T(8,128)(2,1)S(1)} %pad_maximum_fusion.7), channel_id=1, source_target_pairs={{0,8},{4,12},{8,0},{12,4},{16,24},{20,28},{24,16},{28,20},{1,9},{5... | collective-permute-start | bytes 552968 | tf_op jit(solution)/shard_map/ppermute | solution.py:28
  20.2 8.7 %collective-permute-start.9 = (bf16[96,1344]{1,0:T(8,128)(2,1)S(1)}, bf16[96,1344]{1,0:T(8,128)(2,1)S(1)}, u32[]{:S(2)}, u32[]{:S(2)}) collective-permute-start(bf16[96,1344]{1,0:T(8,128)(2,1)S(1)} %pad_maximum_fusion.6), channel_id=1, source_target_pairs={{0,16},{4,20},{8,24},{12,28},{16,0},{20,4},{24,8},{28,12},{1,17},{... | collective-permute-start | bytes 774152 | tf_op jit(solution)/shard_map/ppermute | solution.py:28
  21.8 159.6 %reduce-scatter.3.cloned.1.call-start = ((), (), s32[]{:S(2)}) async-start(), calls=%async_computation.3 | async-start | bytes 1966080 | tf_op jit(solution)/shard_map/reduce_scatter | solution.py:584
  26.7 3.7 %collective-permute-start.4 = (f32[2,8,128]{2,1,0:T(8,128)S(1)}, f32[2,8,128]{2,1,0:T(8,128)S(1)}, u32[]{:S(2)}, u32[]{:S(2)}) collective-permute-start(f32[2,8,128]{2,1,0:T(8,128)S(1)} %pad_maximum_fusion.11), channel_id=1, source_target_pairs={{0,16},{4,20},{8,24},{12,28},{16,0},{20,4},{24,8},{28,12},{1,17},{... | collective-permute-start | bytes 24584 | tf_op jit(solution)/shard_map/ppermute | solution.py:28
  27.4 8.6 %collective-permute-start.7 = (bf16[2,96,960]{2,1,0:T(8,128)(2,1)S(1)}, bf16[2,96,960]{2,1,0:T(8,128)(2,1)S(1)}, u32[]{:S(2)}, u32[]{:S(2)}) collective-permute-start(bf16[2,96,960]{2,1,0:T(8,128)(2,1)S(1)} %pad_maximum_fusion.5), channel_id=1, source_target_pairs={{0,16},{4,20},{8,24},{12,28},{16,0},{20,4},{24,8},{28,12},{1,17},{... | collective-permute-start | bytes 1105928 | tf_op jit(solution)/shard_map/ppermute | solution.py:28
  29.1 11.4 %collective-permute-start.10 = (bf16[2,96,1344]{2,1,0:T(8,128)(2,1)S(1)}, bf16[2,96,1344]{2,1,0:T(8,128)(2,1)S(1)}, u32[]{:S(2)}, u32[]{:S(2)}) collective-permute-start(bf16[2,96,1344]{2,1,0:T(8,128)(2,1)S(1)} %pad_maximum_fusion.4), channel_id=1, source_target_pairs={{0,8},{4,12},{8,0},{12,4},{16,24},{20,28},{24,16},{28,20},{1,9},{5... | collective-permute-start | bytes 1548296 | tf_op jit(solution)/shard_map/ppermute | solution.py:28
  37.0 9.1 %collective-permute-start.8 = (bf16[2,2,96,960]{3,2,1,0:T(8,128)(2,1)}, bf16[2,2,96,960]{3,2,1,0:T(8,128)(2,1)}, u32[]{:S(2)}, u32[]{:S(2)}) collective-permute-start(bf16[2,2,96,960]{3,2,1,0:T(8,128)(2,1)} %pad_maximum_fusion.3), channel_id=1, source_target_pairs={{0,4},{4,0},{8,12},{12,8},{16,20},{20,16},{24,28},{28,24},{1,5},{5... | collective-permute-start | bytes 2211848 | tf_op jit(solution)/shard_map/ppermute | solution.py:28
  40.8 8.1 %collective-permute-start.11 = (bf16[2,2,96,1344]{3,2,0,1:T(8,128)(2,1)S(1)}, bf16[2,2,96,1344]{3,2,0,1:T(8,128)(2,1)}, u32[]{:S(2)}, u32[]{:S(2)}) collective-permute-start(bf16[2,2,96,1344]{3,2,0,1:T(8,128)(2,1)S(1)} %pad_maximum_fusion.2), channel_id=1, source_target_pairs={{0,4},{4,0},{8,12},{12,8},{16,20},{20,16},{24,28},{28,24},{1,5},{5... | collective-permute-start | bytes 3096584 | tf_op jit(solution)/shard_map/ppermute | solution.py:28
  73.7 109.6 %reduce-scatter.5.cloned.1.call-start = ((), (), s32[]{:S(2)}) async-start(), calls=%async_computation.5 | async-start | bytes 1966080 | tf_op jit(solution)/shard_map/reduce_scatter | solution.py:626
  115.1 10.6 %collective-permute-start.14 = (f32[2,8,24]{2,1,0:T(8,128)S(1)}, f32[2,8,24]{2,1,0:T(8,128)S(1)}, u32[]{:S(2)}, u32[]{:S(2)}) collective-permute-start(f32[2,8,24]{2,1,0:T(8,128)S(1)} %bitcast.140), channel_id=1, source_target_pairs={{0,3},{1,0},{2,1},{3,2},{4,7},{5,4},{6,5},{7,6},{8,11},{9,8},{10,9... | collective-permute-start | bytes 4616 | tf_op jit(solution)/shard_map/ppermute | solution.py:636
  116.5 9.3 %collective-permute-start.13 = (f32[2,8,24]{2,1,0:T(8,128)S(1)}, f32[2,8,24]{2,1,0:T(8,128)S(1)}, u32[]{:S(2)}, u32[]{:S(2)}) collective-permute-start(f32[2,8,24]{2,1,0:T(8,128)S(1)} %bitcast.139), channel_id=1, source_target_pairs={{0,2},{1,3},{2,0},{3,1},{4,6},{5,7},{6,4},{7,5},{8,10},{9,11},{10,... | collective-permute-start | bytes 4616 | tf_op jit(solution)/shard_map/ppermute | solution.py:636
  117.2 8.5 %collective-permute-start.12 = (f32[2,8,24]{2,1,0:T(8,128)S(1)}, f32[2,8,24]{2,1,0:T(8,128)S(1)}, u32[]{:S(2)}, u32[]{:S(2)}) collective-permute-start(f32[2,8,24]{2,1,0:T(8,128)S(1)} %bitcast.138), channel_id=1, source_target_pairs={{0,1},{1,2},{2,3},{3,0},{4,5},{5,6},{6,7},{7,4},{8,9},{9,10},{10,1... | collective-permute-start | bytes 4616 | tf_op jit(solution)/shard_map/ppermute | solution.py:636
  125.7 26.3 %collective-permute-start.19 = (bf16[4,96,1728]{2,1,0:T(8,128)(2,1)}, bf16[4,96,1728]{2,1,0:T(8,128)(2,1)S(1)}, u32[]{:S(2)}, u32[]{:S(2)}) collective-permute-start(bf16[4,96,1728]{2,1,0:T(8,128)(2,1)} %shard_map.196), channel_id=1, source_target_pairs={{0,4},{4,0},{8,12},{12,8},{16,20},{20,16},{24,28},{28,24},{1,5},{5... | collective-permute-start | bytes 3981320 | tf_op jit(solution)/shard_map/ppermute | solution.py:28
  138.1 7.7 %collective-permute-start.18 = (bf16[112,576]{1,0:T(8,128)(2,1)}, bf16[112,576]{1,0:T(8,128)(2,1)S(1)}, u32[]{:S(2)}, u32[]{:S(2)}) collective-permute-start(bf16[112,576]{1,0:T(8,128)(2,1)} %get-tuple-element.63), channel_id=1, source_target_pairs={{0,24},{4,28},{8,16},{12,20},{16,8},{20,12},{24,0},{28,4},{1,25},{... | collective-permute-start | bytes 387080 | tf_op jit(solution)/shard_map/ppermute | solution.py:28
  140.5 7.8 %collective-permute-start.17 = (bf16[112,576]{1,0:T(8,128)(2,1)}, bf16[112,576]{1,0:T(8,128)(2,1)S(1)}, u32[]{:S(2)}, u32[]{:S(2)}) collective-permute-start(bf16[112,576]{1,0:T(8,128)(2,1)} %get-tuple-element.62), channel_id=1, source_target_pairs={{0,16},{4,20},{8,24},{12,28},{16,0},{20,4},{24,8},{28,12},{1,17},{... | collective-permute-start | bytes 387080 | tf_op jit(solution)/shard_map/ppermute | solution.py:28
  141.1 7.3 %collective-permute-start.16 = (bf16[112,576]{1,0:T(8,128)(2,1)}, bf16[112,576]{1,0:T(8,128)(2,1)S(1)}, u32[]{:S(2)}, u32[]{:S(2)}) collective-permute-start(bf16[112,576]{1,0:T(8,128)(2,1)} %get-tuple-element.61), channel_id=1, source_target_pairs={{0,8},{4,12},{8,0},{12,4},{16,24},{20,28},{24,16},{28,20},{1,9},{5... | collective-permute-start | bytes 387080 | tf_op jit(solution)/shard_map/ppermute | solution.py:28
  159.9 12.1 %collective-permute-start.22 = (bf16[96,1728]{1,0:T(8,128)(2,1)}, bf16[96,1728]{1,0:T(8,128)(2,1)S(1)}, u32[]{:S(2)}, u32[]{:S(2)}) collective-permute-start(bf16[96,1728]{1,0:T(8,128)(2,1)} %get-tuple-element.68), channel_id=1, source_target_pairs={{0,24},{4,28},{8,16},{12,20},{16,8},{20,12},{24,0},{28,4},{1,25},{... | collective-permute-start | bytes 995336 | tf_op jit(solution)/shard_map/ppermute | solution.py:28
  161.6 16.9 %collective-permute-start.21 = (bf16[96,1728]{1,0:T(8,128)(2,1)}, bf16[96,1728]{1,0:T(8,128)(2,1)S(1)}, u32[]{:S(2)}, u32[]{:S(2)}) collective-permute-start(bf16[96,1728]{1,0:T(8,128)(2,1)} %get-tuple-element.67), channel_id=1, source_target_pairs={{0,16},{4,20},{8,24},{12,28},{16,0},{20,4},{24,8},{28,12},{1,17},{... | collective-permute-start | bytes 995336 | tf_op jit(solution)/shard_map/ppermute | solution.py:28
  162.8 15.7 %collective-permute-start.20 = (bf16[96,1728]{1,0:T(8,128)(2,1)}, bf16[96,1728]{1,0:T(8,128)(2,1)S(1)}, u32[]{:S(2)}, u32[]{:S(2)}) collective-permute-start(bf16[96,1728]{1,0:T(8,128)(2,1)} %get-tuple-element.66), channel_id=1, source_target_pairs={{0,8},{4,12},{8,0},{12,4},{16,24},{20,28},{24,16},{28,20},{1,9},{5... | collective-permute-start | bytes 995336 | tf_op jit(solution)/shard_map/ppermute | solution.py:28
  (13 other events, 107.3 us)
Sparse Core Ops, SparseCore 0:
  9.6 39.7 all-gather.2
  50.9 35.8 all-gather.4
  89.2 34.8 reduce-scatter.2
  126.2 35.3 reduce-scatter.4

commit v3 on v2

--- a/solution.py
+++ b/solution.py
@@ -13,7 +13,6 @@
 ROOT_HALF = 0.7071067811865476
 INV_ROOT_TAU = 0.3989422804014327
 NEG_BIG = -1e30
-SMALL_ROWS = 16
 F32 = jnp.float32
 BF16 = jnp.bfloat16
 
@@ -79,23 +78,22 @@
 
 
 def enter_kernel(
-    heads, head_dim, x_ref, vec_ref, in_bias_ref, qkv_bias_ref, first_ref, second_ref,
+    heads, head_dim, qkv_cols, x_ref, vec_ref, in_bias_ref, qkv_bias_ref, first_ref, second_ref,
     cos_ref, sin_ref, normed_t_ref, proj_t_ref, hidden_ref, slope_ref,
 ):
     width = heads * head_dim
-    hidden_units = hidden_ref.shape[1]
     unit, _ = normalize(x_ref[...])
     wide = unit * vec_ref[0:1] + vec_ref[1:2]
     normed = wide.astype(BF16)
     normed_t_ref[...] = jnp.transpose(normed)
-    projected = dot(normed, second_ref[:, hidden_units:], (1, 0)) + qkv_bias_ref[...]
+    projected = dot(normed, second_ref[:, qkv_cols], (1, 0)) + qkv_bias_ref[...]
     projected = jnp.transpose(projected)
     cosine, sine = cos_ref[...], sin_ref[...]
     for place in range(2 * heads):
         rows = slice(place * head_dim, (place + 1) * head_dim)
         proj_t_ref[rows] = rotate_rows(projected[rows], cosine, sine).astype(BF16)
     proj_t_ref[2 * width :] = projected[2 * width :].astype(BF16)
-    pre_act = dot(normed, first_ref[:, :hidden_units], (1, 0)) + in_bias_ref[...]
+    pre_act = dot(normed, first_ref[...], (1, 0)) + in_bias_ref[...]
     normal_cdf = 0.5 * (1.0 + lax.erf(pre_act * ROOT_HALF))
     normal_pdf = jnp.exp(-0.5 * pre_act * pre_act) * INV_ROOT_TAU
     hidden_ref[...] = (pre_act * normal_cdf).astype(BF16)
@@ -108,7 +106,7 @@
     return key_pos <= query_pos
 
 
-def forward_kernel(scale, block, q_ref, k_ref, v_ref, ctx_ref, lse_ref):
+def forward_kernel(scale, block, q_ref, k_ref, v_ref, ctx_ref, prob_ref):
     length = q_ref.shape[1]
     queries = q_ref[...] * jnp.asarray(scale, BF16)
     keys = jnp.transpose(k_ref[...])
@@ -116,54 +114,58 @@
     allowed = causal(block)
     for step in range(length // block):
         here = slice(step * block, (step + 1) * block)
+        before = slice(0, step * block)
         q_cols = queries[:, here]
         near = jnp.where(allowed, dot(keys[here], q_cols, (1, 0)), NEG_BIG)
         top = jnp.max(near, axis=0, keepdims=True)
         if step:
-            far = dot(keys[: step * block], q_cols, (1, 0))
+            far = dot(keys[before], q_cols, (1, 0))
             top = jnp.maximum(top, jnp.max(far, axis=0, keepdims=True))
         near = jnp.exp(near - top)
         total = jnp.sum(near, axis=0, keepdims=True)
-        context = dot(values[:, here], near.astype(BF16), (1, 0))
         if step:
             far = jnp.exp(far - top)
             total = total + jnp.sum(far, axis=0, keepdims=True)
-            context = context + dot(values[:, : step * block], far.astype(BF16), (1, 0))
-        ctx_ref[:, here] = (context / total).astype(BF16)
-        lse_ref[0, :, here] = jnp.broadcast_to(top + jnp.log(total), (8, block))
+        inverse = 1.0 / total
+        near = (near * inverse).astype(BF16)
+        prob_ref[0, 0, here, here] = near
+        context = dot(values[:, here], near, (1, 0))
+        if step:
+            far = (far * inverse).astype(BF16)
+            prob_ref[0, 0, before, here] = far
+            context = context + dot(values[:, before], far, (1, 0))
+        ctx_ref[:, here] = context.astype(BF16)
 
 
 def backward_kernel(
-    scale, block, q_ref, k_ref, v_ref, cos_ref, sin_ref, lse_ref, grad_ref,
+    scale, block, q_ref, k_ref, v_ref, cos_ref, sin_ref, prob_ref, grad_ref,
     dq_ref, dk_ref, dv_ref, sum_ref, keys_acc, values_acc,
 ):
     length = q_ref.shape[1]
     cosine, sine = cos_ref[...], sin_ref[...]
-    queries = q_ref[...] * jnp.asarray(scale, BF16)
-    query_rows = jnp.transpose(q_ref[...])
+    query_rows = jnp.transpose(q_ref[...] * jnp.asarray(scale, BF16))
     keys_t = k_ref[...]
-    keys = jnp.transpose(keys_t)
     values = jnp.transpose(v_ref[...])
     grad_t = grad_ref[...]
     grad_rows = jnp.transpose(grad_t)
-    allowed = causal(block)
-    keys_acc[...] = jnp.zeros_like(keys_acc)
-    values_acc[...] = jnp.zeros_like(values_acc)
     query_sum = 0.0
-    for step in range(length // block):
+    for step in reversed(range(length // block)):
         here = slice(step * block, (step + 1) * block)
         upto = slice(0, (step + 1) * block)
-        lse = lse_ref[0, 0:1, here]
-        scores = dot(keys[upto], queries[:, here], (1, 0))
-        probs = jnp.exp(scores - lse)
-        low = jnp.where(allowed, probs[step * block :], 0.0)
-        probs = jnp.concatenate([probs[: step * block], low], axis=0) if step else low
-        values_acc[upto, :] += dot(probs.astype(BF16), grad_rows[here], (1, 0))
+        probs = prob_ref[0, 0, upto, here]
+        value_part = dot(probs, grad_rows[here], (1, 0))
         prob_grad = dot(values[upto], grad_t[:, here], (1, 0))
+        probs = probs.astype(F32)
         row_dot = jnp.sum(probs * prob_grad, axis=0, keepdims=True)
-        score_grad = (probs * (prob_grad - row_dot) * scale).astype(BF16)
-        keys_acc[upto, :] += dot(score_grad, query_rows[here], (1, 0))
-        dq = dot(keys_t[:, upto], score_grad, (1, 0))
+        score_grad = (probs * (prob_grad - row_dot)).astype(BF16)
+        key_part = dot(score_grad, query_rows[here], (1, 0))
+        if (step + 1) * block == length:
+            values_acc[...] = value_part
+            keys_acc[...] = key_part
+        else:
+            values_acc[upto, :] += value_part
+            keys_acc[upto, :] += key_part
+        dq = dot(keys_t[:, upto], score_grad, (1, 0)) * scale
         dq = rotate_rows(dq, cosine[:, here], -sine[:, here])
         dq_ref[:, here] = dq.astype(BF16)
         query_sum = query_sum + jnp.sum(dq, axis=1, keepdims=True)
@@ -176,12 +178,11 @@
         sum_ref[0, 0, place] = jnp.broadcast_to(part, (part.shape[0], 128))
 
 
-def branch_kernel(ctx_t_ref, hidden_ref, first_ref, second_ref, branch_ref, ctx_ref):
-    hidden_units = hidden_ref.shape[1]
+def branch_kernel(out_cols, ctx_t_ref, hidden_ref, first_ref, second_ref, branch_ref, ctx_ref):
     context = jnp.transpose(ctx_t_ref[...])
     ctx_ref[...] = context
-    total = dot(context, first_ref[:, hidden_units:], (1, 1))
-    total = total + dot(hidden_ref[...], second_ref[:, :hidden_units], (1, 1))
+    total = dot(context, first_ref[:, out_cols], (1, 1))
+    total = total + dot(hidden_ref[...], second_ref[...], (1, 1))
     branch_ref[...] = total.astype(BF16)
 
 
@@ -190,15 +191,14 @@
 
 
 def return_kernel(
-    after_ref, cot_ref, slope_ref, first_ref, second_ref,
+    out_cols, after_ref, cot_ref, slope_ref, first_ref, second_ref,
     cot_t_ref, ctx_grad_t_ref, pre_low_ref, in_sum_ref, cot_sum_ref,
 ):
-    hidden_units = slope_ref.shape[1]
     cot = cot_ref[...]
     cot_t_ref[...] = jnp.transpose(cot)
-    ctx_grad = dot(cot, first_ref[:, hidden_units:], (1, 0))
+    ctx_grad = dot(cot, first_ref[:, out_cols], (1, 0))
     ctx_grad_t_ref[...] = jnp.transpose(ctx_grad).astype(BF16)
-    pre_grad = dot(cot, second_ref[:, :hidden_units], (1, 0)) * slope_ref[...]
+    pre_grad = dot(cot, second_ref[...], (1, 0)) * slope_ref[...]
     pre_low_ref[...] = pre_grad.astype(BF16)
 
     @pl.when(pl.program_id(0) == 0)
@@ -211,16 +211,15 @@
 
 
 def norm_kernel(
-    x_ref, dq_ref, dk_ref, dv_ref, pre_low_ref, first_ref, second_ref,
+    qkv_cols, x_ref, dq_ref, dk_ref, dv_ref, pre_low_ref, first_ref, second_ref,
     proj_low_ref, norm_grad_ref, gain_sum_ref, shift_sum_ref,
 ):
-    hidden_units = pre_low_ref.shape[1]
     proj_low = jnp.transpose(
         jnp.concatenate([dq_ref[...], dk_ref[...], dv_ref[...]], axis=0)
     )
     proj_low_ref[...] = proj_low
-    norm_grad = dot(proj_low, second_ref[:, hidden_units:], (1, 1))
-    norm_grad = norm_grad + dot(pre_low_ref[...], first_ref[:, :hidden_units], (1, 1))
+    norm_grad = dot(proj_low, second_ref[:, qkv_cols], (1, 1))
+    norm_grad = norm_grad + dot(pre_low_ref[...], first_ref[...], (1, 1))
     norm_grad_ref[...] = norm_grad.astype(BF16)
     unit, _ = normalize(x_ref[...])
 
@@ -239,35 +238,31 @@
     return jnp.concatenate([ref[pl.ds(start, part), :] for start in starts], axis=0)
 
 
-def put(outs, got_ref, rows, columns, value):
-    blocks = value.shape[0] // (rows.stop - rows.start)
-    value = value.reshape(blocks, rows.stop - rows.start, -1)
+def put(outs, got_ref, columns, value):
+    blocks, part = (outs[0].shape[0], outs[0].shape[1]) if got_ref is None else got_ref.shape[:2]
+    value = value.reshape(blocks, part, -1)
     if got_ref is None:
-        outs[0][:, rows, columns] = value.astype(BF16)
+        outs[0][:, :, columns] = value.astype(BF16)
         return
-    value = value + got_ref[:, rows, columns].astype(F32)
+    value = value + got_ref[:, :, columns].astype(F32)
     for k in range(blocks):
-        outs[k][rows, columns] = value[k].astype(outs[k].dtype)
+        outs[k][:, columns] = value[k].astype(outs[k].dtype)
 
 
 def early_kernel(blocks, part, at_ref, normed_t_ref, cot_t_ref, pre_low_ref, ctx_ref, hidden_ref, *refs):
     got_ref, outs = (None, refs) if len(refs) == 1 else (refs[0], refs[1:])
     units = hidden_ref.shape[1]
-    rows = slice(0, part)
     left = half_rows(normed_t_ref, at_ref, blocks, part)
-    put(outs, got_ref, rows, slice(0, units), dot(left, pre_low_ref[...], (1, 0)))
+    put(outs, got_ref, slice(0, units), dot(left, pre_low_ref[...], (1, 0)))
     left = half_rows(cot_t_ref, at_ref, blocks, part)
-    put(outs, got_ref, rows, slice(units, 2 * units), dot(left, hidden_ref[...], (1, 0)))
-    put(outs, got_ref, rows, slice(2 * units, None), dot(left, ctx_ref[...], (1, 0)))
-
-
-def late_kernel(blocks, part, at_ref, normed_t_ref, proj_low_ref, small_ref, *refs):
+    put(outs, got_ref, slice(units, 2 * units), dot(left, hidden_ref[...], (1, 0)))
+    put(outs, got_ref, slice(2 * units, None), dot(left, ctx_ref[...], (1, 0)))
+
+
+def late_kernel(blocks, part, at_ref, normed_t_ref, proj_low_ref, *refs):
     got_ref, outs = (None, refs) if len(refs) == 1 else (refs[0], refs[1:])
     left = half_rows(normed_t_ref, at_ref, blocks, part)
-    put(outs, got_ref, slice(0, part), slice(None), dot(left, proj_low_ref[...], (1, 0)))
-    members = [2 * lax.bitwise_xor(at_ref[1], k) + at_ref[0] for k in range(blocks)]
-    extra = jnp.concatenate([small_ref[member] for member in members], axis=0)
-    put(outs, got_ref, slice(part, part + SMALL_ROWS), slice(None), extra)
+    put(outs, got_ref, slice(None), dot(left, proj_low_ref[...], (1, 0)))
 
 
 def whole(x):
@@ -280,6 +275,15 @@
 
 def tokens_t(rows, block):
     return pl.BlockSpec((rows, block), lambda t: (0, t))
+
+
+def columns(x, start, count):
+    for wide in range(-(-count // 128) * 128, start + 1, 128):
+        if start % wide == 0:
+            return pl.BlockSpec((x.shape[0], wide), lambda *_: (0, start // wide)), slice(0, count)
+    if start == 0:
+        return pl.BlockSpec((x.shape[0], count), lambda *_: (0, 0)), slice(0, count)
+    return whole(x), slice(start, start + count)
 
 
 def cost(flops, nbytes, trans=0):
@@ -297,12 +301,14 @@
     block = min(256, rows)
     per_seq = cosine.shape[1] // block
     table = pl.BlockSpec((ROT // 2, block), lambda t: (0, lax.rem(t, per_seq)))
+    first_spec, _ = columns(first, 0, hidden_units)
+    second_spec, qkv_cols = columns(second, hidden_units, proj)
     return pl.pallas_call(
-        functools.partial(enter_kernel, heads, head_dim),
+        functools.partial(enter_kernel, heads, head_dim, qkv_cols),
         grid=(rows // block,),
         in_specs=[
             tokens(block, model), whole(vectors), whole(in_bias), whole(qkv_bias),
-            whole(first), whole(second), table, table,
+            first_spec, second_spec, table, table,
         ],
         out_specs=[
             tokens_t(model, block), tokens_t(proj, block),
@@ -327,23 +333,23 @@
     def part(which):
         return pl.BlockSpec((head_dim, length), lambda s, h: (which * heads + h, s))
 
-    lse_spec = pl.BlockSpec((1, 8, length), lambda s, h: (h, 0, s))
+    prob_spec = pl.BlockSpec((1, 1, length, length), lambda s, h: (s, h, 0, 0))
     work = seqs * heads * length * length
     return pl.pallas_call(
         functools.partial(forward_kernel, scale, block),
         grid=(seqs, heads),
         in_specs=[part(0), part(1), part(2)],
-        out_specs=[part(0), lse_spec],
+        out_specs=[part(0), prob_spec],
         out_shape=[
             struct(heads * head_dim, seqs * length),
-            struct(heads, 8, seqs * length, dtype=F32),
+            struct(seqs, heads, length, length),
         ],
         cost_estimate=cost(4 * work * head_dim, proj_t.size * 4, work),
         name="attend_forward",
     )(proj_t, proj_t, proj_t)
 
 
-def attend_back(proj_t, cosine, sine, lse, ctx_grad_t, seqs, heads, head_dim, length):
+def attend_back(proj_t, cosine, sine, probs, ctx_grad_t, seqs, heads, head_dim, length):
     block = min(256, length)
     scale = 1.0 / math.sqrt(head_dim)
 
@@ -351,20 +357,20 @@
         return pl.BlockSpec((head_dim, length), lambda s, h: (which * heads + h, s))
 
     table = pl.BlockSpec((ROT // 2, length), lambda s, h: (0, 0))
-    lse_spec = pl.BlockSpec((1, 8, length), lambda s, h: (h, 0, s))
+    prob_spec = pl.BlockSpec((1, 1, length, length), lambda s, h: (s, h, 0, 0))
     sum_spec = pl.BlockSpec((1, 1, 3, head_dim, 128), lambda s, h: (s, h, 0, 0, 0))
     flat = struct(heads * head_dim, seqs * length)
     work = seqs * heads * length * length
     return pl.pallas_call(
         functools.partial(backward_kernel, scale, block),
         grid=(seqs, heads),
-        in_specs=[part(0), part(1), part(2), table, table, lse_spec, part(0)],
+        in_specs=[part(0), part(1), part(2), table, table, prob_spec, part(0)],
         out_specs=[part(0), part(0), part(0), sum_spec],
         out_shape=[flat, flat, flat, struct(seqs, heads, 3, head_dim, 128, dtype=F32)],
         scratch_shapes=[pltpu.VMEM((length, head_dim), F32)] * 2,
         cost_estimate=cost(10 * work * head_dim, proj_t.size * 6, work),
         name="attend_backward",
-    )(proj_t, proj_t, proj_t, cosine, sine, lse, ctx_grad_t)
+    )(proj_t, proj_t, proj_t, cosine, sine, probs, ctx_grad_t)
 
 
 def branch_sum(ctx_t, hidden, first, second):
@@ -372,11 +378,13 @@
     hidden_units = hidden.shape[1]
     model = first.shape[0]
     block = min(256, rows)
+    first_spec, out_cols = columns(first, hidden_units, width)
+    second_spec, _ = columns(second, 0, hidden_units)
     return pl.pallas_call(
-        branch_kernel,
+        functools.partial(branch_kernel, out_cols),
         grid=(rows // block,),
         in_specs=[
-            tokens_t(width, block), tokens(block, hidden_units), whole(first), whole(second),
+            tokens_t(width, block), tokens(block, hidden_units), first_spec, second_spec,
         ],
         out_specs=[tokens(block, model), tokens(block, width)],
         out_shape=[struct(rows, model), struct(rows, width)],
@@ -389,11 +397,13 @@
     rows, model = cot.shape
     hidden_units = slopes.shape[1]
     block = min(256, rows)
+    first_spec, out_cols = columns(first, hidden_units, width)
+    second_spec, _ = columns(second, 0, hidden_units)
     return pl.pallas_call(
-        return_kernel,
+        functools.partial(return_kernel, out_cols),
         grid=(rows // block,),
         in_specs=[
-            pl.BlockSpec(memory_space=pl.ANY), tokens(block, model), tokens(block, hidden_units), whole(first), whole(second),
+            pl.BlockSpec(memory_space=pl.ANY), tokens(block, model), tokens(block, hidden_units), first_spec, second_spec,
         ],
         out_specs=[
             tokens_t(model, block), tokens_t(width, block), tokens(block, hidden_units),
@@ -414,12 +424,14 @@
     width = dq_t.shape[0]
     hidden_units = pre_low.shape[1]
     block = min(256, rows)
+    first_spec, _ = columns(first, 0, hidden_units)
+    second_spec, qkv_cols = columns(second, hidden_units, 3 * width)
     return pl.pallas_call(
-        norm_kernel,
+        functools.partial(norm_kernel, qkv_cols),
         grid=(rows // block,),
         in_specs=[
             tokens(block, model), tokens_t(width, block), tokens_t(width, block),
-            tokens_t(width, block), tokens(block, hidden_units), whole(first), whole(second),
+            tokens_t(width, block), tokens(block, hidden_units), first_spec, second_spec,
         ],
         out_specs=[
             tokens(block, 3 * width), tokens(block, model),
@@ -506,6 +518,23 @@
     return total
 
 
+def exchange_small(small, dp):
+    core, chip = bit_of("dp", 1), lax.axis_index("dp") // 2
+    count = dp // 2
+    small = small.reshape(count, 2, -1)
+    kept = lax.dynamic_index_in_dim(small, core, 1, keepdims=False)
+    sent = lax.dynamic_index_in_dim(small, 1 - core, 1, keepdims=False)
+    got = swap_core(sent, dp)
+    x = kept + got
+    if count > 4:
+        steps = [1 << b for b in range(count.bit_length() - 1)]
+        return scatter_bits(x, 0, steps[::-1], F32, dp, 2)
+    pieces = [
+        lax.dynamic_index_in_dim(x, chip ^ k, 0, keepdims=False) for k in range(count)
+    ]
+    return add_pieces(pieces, dp)
+
+
 def exchange(grad, dp):
     kept, sent = split_core(grad, dp)
     x = kept + swap_core(sent, dp).astype(F32)
@@ -579,7 +608,7 @@
         full_in, norm_rows, in_bias.reshape(1, -1), qkv_bias.reshape(1, -1), first, second,
         cosine, sine, heads, head_dim,
     )
-    ctx_t, lse = attend(proj_t, seqs, heads, head_dim, length)
+    ctx_t, probs = attend(proj_t, seqs, heads, head_dim, length)
     branch, context = branch_sum(ctx_t, hidden, first, second)
     summed = lax.psum_scatter(
         branch.reshape(seqs, length, model), "tensor", scatter_dimension=1, tiled=True
@@ -618,7 +647,7 @@
         )
         early = exchange(early, dp)
     dq_t, dk_t, dv_t, sums = attend_back(
-        proj_t, cosine, sine, lse, ctx_grad_t, seqs, heads, head_dim, length
+        proj_t, cosine, sine, probs, ctx_grad_t, seqs, heads, head_dim, length
     )
     proj_low, norm_grad, gain_sum, shift_sum = norm_sum(
         full_in, dq_t, dk_t, dv_t, pre_low, first, second
@@ -648,14 +677,13 @@
         ],
         axis=1,
     )
-    columns = 3 * width
-    small = jnp.pad(
-        small[:, None, :], ((0, 0), (0, SMALL_ROWS - 1), (0, columns - small.shape[1]))
+    small = exchange_small(
+        jnp.pad(small, ((0, 0), (0, -small.shape[1] % 128))), dp
     )
     if aligned:
-        operands = (normed_t, proj_low, small)
-        shape = (part + SMALL_ROWS, columns)
-        flops = rows * model * columns
+        operands = (normed_t, proj_low)
+        shape = (part, 3 * width)
+        flops = rows * model * shape[1]
         (late_sent,) = weight_half(
             late_kernel, (1 - core, chip), operands, None, blocks, part, shape,
             flops,
@@ -667,13 +695,11 @@
         )
         late = add_pieces(late_pieces, dp)
     else:
-        late = dot(normed_t, proj_low, (1, 0)).reshape(dp, part, columns)
-        late = exchange(jnp.concatenate([late, small], axis=1), dp)
+        late = exchange(dot(normed_t, proj_low, (1, 0)), dp)
     in_out = early[:, :hidden_units]
     down_out = early[:, hidden_units : 2 * hidden_units].T
     out_out = early[:, 2 * hidden_units :].T
-    qkv_out = late[:part].reshape(part, 3, width)
-    small = late[part]
+    qkv_out = late.reshape(part, 3, width)
     gain_out, shift_out, bias_out = (small[k * own : (k + 1) * own] for k in range(3))
     bias_grad = jnp.stack([bias_out, bias_out])
     at = 3 * own

time: 193 us -> 184 us (0.953)
  waiting for transfers between devices: 48.6 us -> 41.6 us
  starting transfers between devices: 24.3 us -> 27.4 us
  Pallas kernels: 73 us -> 70.3 us
  other arithmetic: 15 us -> 12.9 us
    ppermute x17 -> x21, waiting for transfers between devices: 35.5 us -> 29.2 us  [swap(): return lax.ppermute(x, axis_name, [(i, i ^ step) for i in range(size)])]
    ppermute x17 -> x21, starting transfers between devices: 14.4 us -> 18 us  [swap(): return lax.ppermute(x, axis_name, [(i, i ^ step) for i in range(size)])]
    pallas_call x4, Pallas kernels: 29.4 us -> 26.7 us  [the longest x1 7.86 us: enter(): pl.pallas_call(functools.partial(enter_kernel, heads, head_dim, qkv_cols)...]
    add x2 -> x3, other arithmetic: 2.33 us -> 0.2 us  [add_pieces(): total = total + got.astype(F32)]
    unnamed x25 -> x30, local copies, waits for them, and re-layouts: 5.55 us -> 5.51 us
  transfers between devices with their start and end apart: 27 -> 31, of which waited for: 13 -> 10; matrix products, arithmetic and copies ran while one was open for 16% -> 15% of each run, Pallas kernels for 37% -> 37%
where the time goes in v3:
time: 184 us; the launch traced here: 183 us
  Pallas kernels  70.3 us (38%)
  waiting for transfers between devices  41.6 us (23%)
  starting transfers between devices  27.4 us (15%)
  local copies, waits for them, and re-layouts  16.5 us (9%)
  between operations  14.3 us (8%)
  other arithmetic  12.9 us (7%)
    ppermute x21, waiting for transfers between devices, swap(): return lax.ppermute(x, axis_name, [(i, i ^ step) for i in range(size)])  29.2 us
    pallas_call x4, Pallas kernels, weight_half(): pl.pallas_call(functools.partial(kernel, blocks, part), grid_spec=pltpu.P...  21.6 us
    ppermute x21, starting transfers between devices, swap(): return lax.ppermute(x, axis_name, [(i, i ^ step) for i in range(size)])  18 us
    all_gather x1, waiting for transfers between devices, body(): lax.all_gather(cotangent, 'tensor', axis=1, tiled=True).reshape(rows, model)  11.7 us
    pallas_call x1, Pallas kernels, attend_back(): pl.pallas_call(functools.partial(backward_kernel, scale, block), grid=(se...  11.1 us
    pallas_call x1, Pallas kernels, attend(): pl.pallas_call(functools.partial(forward_kernel, scale, block), grid=(seq...  8.36 us
    pallas_call x1, Pallas kernels, enter(): pl.pallas_call(functools.partial(enter_kernel, heads, head_dim, qkv_cols)...  7.86 us
    pallas_call x1, Pallas kernels, norm_sum(): pl.pallas_call(functools.partial(norm_kernel, qkv_cols), grid=(rows // bl...  7.23 us
  transfers between devices with their start and end apart: 31, of which 10 were waited for; matrix products, arithmetic and copies ran while one was open for 15% of the time, Pallas kernels for 37%

profile of v3, /device:TPU:0, one launch (start us, length us, event | category | flops | bytes accessed | tf_op | source)
XLA Modules:
  0.0 183.0 jit_solution(11348244172966877224)
XLA Ops:
  9.4 5.1 %collective-permute-start.2 = (f32[3,24]{1,0:T(4,128)S(1)}, f32[3,24]{1,0:T(4,128)S(1)}, u32[]{:S(2)}, u32[]{:S(2)}) collective-permute-start(f32[3,24]{1,0:T(4,128)S(1)} %get-tuple-element.139), channel_id=1, source_target_pairs={{0,3},{1,0},{2,1},{3,2},{4,7},{5,4},{6,5},{7,6},{8,11},{9,8},{10,9... | collective-permute-start | bytes 872 | tf_op jit(solution)/shard_map/ppermute | solution.py:568
  20.2 1.6 collective-permute-start.9
  23.6 3.1 %collective-permute-done.3 = f32[8,128]{1,0:T(8,128)S(1)} collective-permute-done((f32[8,128]{1,0:T(8,128)S(1)}, f32[8,128]{1,0:T(8,128)S(1)}, u32[]{:S(2)}, u32[]{:S(2)}) %collective-permute-start.3) | collective-permute-done | bytes 4128 | tf_op jit(solution)/shard_map/ppermute | solution.py:27
  30.5 5.5 %collective-permute-done.7 = bf16[2,96,960]{2,1,0:T(8,128)(2,1)S(1)} collective-permute-done((bf16[2,96,960]{2,1,0:T(8,128)(2,1)S(1)}, bf16[2,96,960]{2,1,0:T(8,128)(2,1)S(1)}, u32[]{:S(2)}, u32[]{:S(2)}) %collective-permute-start.7) | collective-permute-done | bytes 368672 | tf_op jit(solution)/shard_map/ppermute | solution.py:27
  37.0 3.4 %collective-permute-done.10 = bf16[2,96,1344]{2,1,0:T(8,128)(2,1)S(1)} collective-permute-done((bf16[2,96,1344]{2,1,0:T(8,128)(2,1)S(1)}, bf16[2,96,1344]{2,1,0:T(8,128)(2,1)S(1)}, u32[]{:S(2)}, u32[]{:S(2)}) %collective-permute-start.10) | collective-permute-done | bytes 516128 | tf_op jit(solution)/shard_map/ppermute | solution.py:27
  52.1 7.9 %enter.1 = (bf16[768,1024]{1,0:T(8,128)(2,1)}, bf16[576,1024]{1,0:T(8,128)(2,1)}, bf16[1024,768]{1,0:T(8,128)(2,1)}, f32[1024,768]{1,0:T(8,128)}) custom-call(bf16[1024,768]{1,0:T(8,128)(2,1)} %bitcast.121, f32[3,768]{1,0:T(4,128)} %reshape.183.vec_ref, f32[1,768]{1,0:T(1,128)} %reshape_reshape.16.in_bias_ref, f32[1,576]{1,0:T(1,128)} %reshape_reshape.17.qkv_bias_ref, ...), custom_call_target="tpu_custom_call" | custom-call | flops 2113929216 | bytes 12976128 | tf_op jit(solution)/shard_map/enter/pallas_call | solution.py:306
  60.0 8.4 %attend_forward.1 = (bf16[192,1024]{1,0:T(8,128)(2,1)}, bf16[1,3,1024,1024]{3,2,1,0:T(8,128)(2,1)}) custom-call(bf16[576,1024]{1,0:T(8,128)(2,1)} %get-tuple-element.40.q_ref.k_ref.v_ref, bf16[576,1024]{1,0:T(8,128)(2,1)} %get-tuple-element.40.q_ref.k_ref.v_ref, bf16[576,1024]{1,0:T(8,128)(2,1)} %get-tuple-element.40.q_ref.k_ref.v_ref), custom_call_target="tpu_custom_call" | custom-call | flops 805306368 | bytes 2359296 | tf_op jit(solution)/shard_map/attend_forward/pallas_call | solution.py:338
  68.4 5.5 %branch.1 = (bf16[1024,768]{1,0:T(8,128)(2,1)}, bf16[1024,192]{1,0:T(8,128)(2,1)}) custom-call(bf16[192,1024]{1,0:T(8,128)(2,1)} %get-tuple-element.41.ctx_t_ref, bf16[1024,768]{1,0:T(8,128)(2,1)} %get-tuple-element.42.hidden_ref, bf16[768,960]{1,0:T(8,128)(2,1)} %bitcast.116, bf16[768,1344]{1,0:T(8,128)(2,1)} %bitcast.112), custom_call_target="tpu_custom_call" | custom-call | flops 1509949440 | bytes 6291456 | tf_op jit(solution)/shard_map/branch/pallas_call | solution.py:383
  75.2 11.7 %all-gather.5.cloned.1.call-done = bf16[1,1024,768]{2,1,0:T(8,128)(2,1)} async-done(((bf16[1,256,768]{2,1,0:T(8,128)(2,1)}), bf16[1,1024,768]{2,1,0:T(8,128)(2,1)}) %all-gather.5.cloned.1.call-update) | async-done | bytes 1572880 | tf_op jit(solution)/shard_map/all_gather | solution.py:562
  86.9 6.2 %return_grads.1 = (bf16[768,1024]{1,0:T(8,128)(2,1)}, bf16[192,1024]{1,0:T(8,128)(2,1)}, bf16[1024,768]{1,0:T(8,128)(2,1)}, f32[8,768]{1,0:T(8,128)}, f32[8,768]{1,0:T(8,128)}) custom-call(bf16[1024,192]{1,0:T(8,128)(2,1)} %get-tuple-element.45.after_ref.ctx_ref, bf16[1024,768]{1,0:T(8,128)(2,1)} %bitcast.123, f32[1024,768]{1,0:T(8,128)} %get-tuple-element.46.slope_ref, ...), custom_call_target="tpu_custom_call" | custom-call | flops 1509949440 | bytes 7864320 | tf_op jit(solution)/shard_map/return_grads/pallas_call | solution.py:402
  93.1 11.1 %attend_backward.1 = (bf16[192,1024]{1,0:T(8,128)(2,1)}, bf16[192,1024]{1,0:T(8,128)(2,1)}, bf16[192,1024]{1,0:T(8,128)(2,1)}, f32[1,3,3,64,128]{4,3,2,1,0:T(8,128)}) custom-call(bf16[576,1024]{1,0:T(8,128)(2,1)} %get-tuple-element.40.q_ref.k_ref.v_ref, bf16[576,1024]{1,0:T(8,128)(2,1)} %get-tuple-element.40.q_ref.k_ref.v_ref, ...), custom_call_target="tpu_custom_call" | custom-call | flops 2013265920 | bytes 3538944 | tf_op jit(solution)/shard_map/attend_backward/pallas_call | solution.py:364
  104.2 7.2 %norm_grads.1 = (bf16[1024,576]{1,0:T(8,128)(2,1)}, bf16[1024,768]{1,0:T(8,128)(2,1)}, f32[8,768]{1,0:T(8,128)}, f32[8,768]{1,0:T(8,128)}) custom-call(bf16[1024,768]{1,0:T(8,128)(2,1)} %bitcast.122, bf16[192,1024]{1,0:T(8,128)(2,1)} %get-tuple-element.48.dq_ref, bf16[192,1024]{1,0:T(8,128)(2,1)} %get-tuple-element.49.dk_ref, ...), custom_call_target="tpu_custom_call" | custom-call | flops 2113929216 | bytes 6291456 | tf_op jit(solution)/shard_map/norm_grads/pallas_call | solution.py:429
  115.7 6.5 %shard_map.196 = bf16[4,96,1728]{2,1,0:T(8,128)(2,1)} custom-call(s32[2]{0:T(128)} %pad_add_fusion.1.at_ref, bf16[768,1024]{1,0:T(8,128)(2,1)} %get-tuple-element.58.normed_t_ref, bf16[768,1024]{1,0:T(8,128)(2,1)} %get-tuple-element.64.cot_t_ref, bf16[1024,768]{1,0:T(8,128)(2,1)} %get-tuple-element.51.pre_low_ref, ...), custom_call_target="tpu_custom_call" | custom-call | flops 1358954496 | bytes 3145728 | tf_op jit(solution)/shard_map/pallas_call | solution.py:480
  124.2 1.8 collective-permute-done.15
  126.0 2.5 %collective-permute-start.18 = (f32[256]{0:T(256)S(1)}, f32[256]{0:T(256)S(1)}, u32[]{:S(2)}, u32[]{:S(2)}) collective-permute-start(f32[256]{0:T(256)S(1)} %bitcast.155), channel_id=1, source_target_pairs={{0,24},{4,28},{8,16},{12,20},{16,8},{20,12},{24,0},{28,4},{1,25},{... | collective-permute-start | bytes 3080 | tf_op jit(solution)/shard_map/ppermute | solution.py:27
  129.6 4.2 %shard_map.194 = bf16[4,96,576]{2,1,0:T(8,128)(2,1)} custom-call(s32[2]{0:T(128)} %pad_add_fusion.1.at_ref, bf16[768,1024]{1,0:T(8,128)(2,1)} %get-tuple-element.58.normed_t_ref, bf16[1024,576]{1,0:T(8,128)(2,1)} %get-tuple-element.59.proj_low_ref), custom_call_target="tpu_custom_call" | custom-call | flops 452984832 | bytes 3145728 | tf_op jit(solution)/shard_map/pallas_call | solution.py:480
  136.7 4.1 %shard_map.195 = (f32[96,576]{1,0:T(8,128)}, bf16[96,576]{1,0:T(8,128)(2,1)}, bf16[96,576]{1,0:T(8,128)(2,1)}, bf16[96,576]{1,0:T(8,128)(2,1)}) custom-call(s32[2]{0:T(128)} %pad_add_fusion.at_ref, bf16[768,1024]{1,0:T(8,128)(2,1)} %get-tuple-element.58.normed_t_ref, bf16[1024,576]{1,0:T(8,128)(2,1)} %get-tuple-element.59.proj_low_ref, ...), custom_call_target="tpu_custom_call" | custom-call | flops 452984832 | bytes 3145728 | tf_op jit(solution)/shard_map/pallas_call | solution.py:480
  140.8 2.4 %collective-permute-start.22 = (bf16[96,576]{1,0:T(8,128)(2,1)}, bf16[96,576]{1,0:T(8,128)(2,1)S(1)}, u32[]{:S(2)}, u32[]{:S(2)}) collective-permute-start(bf16[96,576]{1,0:T(8,128)(2,1)} %get-tuple-element.63), channel_id=1, source_target_pairs={{0,24},{4,28},{8,16},{12,20},{16,8},{20,12},{24,0},{28,4},{1,25},{... | collective-permute-start | bytes 331784 | tf_op jit(solution)/shard_map/ppermute | solution.py:27
  145.4 6.8 %shard_map.197 = (f32[96,1728]{1,0:T(8,128)}, bf16[96,1728]{1,0:T(8,128)(2,1)}, bf16[96,1728]{1,0:T(8,128)(2,1)}, bf16[96,1728]{1,0:T(8,128)(2,1)}) custom-call(s32[2]{0:T(128)} %pad_add_fusion.at_ref, bf16[768,1024]{1,0:T(8,128)(2,1)} %get-tuple-element.58.normed_t_ref, bf16[768,1024]{1,0:T(8,128)(2,1)} %get-tuple-element.64.cot_t_ref, ...), custom_call_target="tpu_custom_call" | custom-call | flops 1358954496 | bytes 3145728 | tf_op jit(solution)/shard_map/pallas_call | solution.py:480
  152.1 2.4 %collective-permute-start.26 = (bf16[96,1728]{1,0:T(8,128)(2,1)}, bf16[96,1728]{1,0:T(8,128)(2,1)S(1)}, u32[]{:S(2)}, u32[]{:S(2)}) collective-permute-start(bf16[96,1728]{1,0:T(8,128)(2,1)} %get-tuple-element.68), channel_id=1, source_target_pairs={{0,24},{4,28},{8,16},{12,20},{16,8},{20,12},{24,0},{28,4},{1,25},{... | collective-permute-start | bytes 995336 | tf_op jit(solution)/shard_map/ppermute | solution.py:27
  157.3 6.9 %collective-permute-done.26 = bf16[96,1728]{1,0:T(8,128)(2,1)S(1)} collective-permute-done((bf16[96,1728]{1,0:T(8,128)(2,1)}, bf16[96,1728]{1,0:T(8,128)(2,1)S(1)}, u32[]{:S(2)}, u32[]{:S(2)}) %collective-permute-start.26) | collective-permute-done | bytes 331808 | tf_op jit(solution)/shard_map/ppermute | solution.py:27
  164.2 6.1 %collective-permute-done.25 = bf16[96,1728]{1,0:T(8,128)(2,1)S(1)} collective-permute-done((bf16[96,1728]{1,0:T(8,128)(2,1)}, bf16[96,1728]{1,0:T(8,128)(2,1)S(1)}, u32[]{:S(2)}, u32[]{:S(2)}) %collective-permute-start.25) | collective-permute-done | bytes 331808 | tf_op jit(solution)/shard_map/ppermute | solution.py:27
  172.1 1.9 %add_convert_fusion = bf16[1,256,768]{2,1,0:T(8,128)(2,1)} fusion(bf16[1,256,768]{2,1,0:T(8,128)(2,1)} %reduce-scatter.3.cloned.1.call-done, bf16[1,256,768]{2,1,0:T(8,128)(2,1)S(1)} %copy-done, f32[768]{0:T(1024)S(1)} %add.180), kind=kLoop, calls=%fused_computation.7 | loop fusion | flops 983040 | bytes 1182720 | tf_op jit(solution)/shard_map/convert_element_type | solution.py:616
  174.0 2.5 %finish.1 = bf16[1,256,768]{2,1,0:T(8,128)(2,1)} custom-call(bf16[1,256,768]{2,1,0:T(8,128)(2,1)} %x_ref.1, bf16[1,256,768]{2,1,0:T(8,128)(2,1)} %cot_ref.1, bf16[1,256,768]{2,1,0:T(8,128)(2,1)} %reduce-scatter.5.cloned.1.call-done.own_ref, f32[1,768]{1,0:T(1,128)} %slice.75.gain_ref), custom_call_target="tpu_custom_call" | custom-call | flops 3932160 | bytes 1572864 | tf_op jit(solution)/shard_map/finish/pallas_call | solution.py:463
  (174 shorter events, 44.0 us)
Async XLA Ops:
  7.2 44.9 %all-gather.3.cloned.1.call-start = ((), (), s32[]{:S(2)}) async-start(), calls=%async_computation.2 | async-start | bytes 1966080 | tf_op jit(solution)/shard_map/all_gather | solution.py:561
  8.0 78.9 %all-gather.5.cloned.1.call-start = ((), (), s32[]{:S(2)}) async-start(), calls=%async_computation.4 | async-start | bytes 1966080 | tf_op jit(solution)/shard_map/all_gather | solution.py:562
  9.4 12.7 %collective-permute-start.2 = (f32[3,24]{1,0:T(4,128)S(1)}, f32[3,24]{1,0:T(4,128)S(1)}, u32[]{:S(2)}, u32[]{:S(2)}) collective-permute-start(f32[3,24]{1,0:T(4,128)S(1)} %get-tuple-element.139), channel_id=1, source_target_pairs={{0,3},{1,0},{2,1},{3,2},{4,7},{5,4},{6,5},{7,6},{8,11},{9,8},{10,9... | collective-permute-start | bytes 872 | tf_op jit(solution)/shard_map/ppermute | solution.py:568
  14.6 7.6 %collective-permute-start.1 = (f32[3,24]{1,0:T(4,128)S(1)}, f32[3,24]{1,0:T(4,128)S(1)}, u32[]{:S(2)}, u32[]{:S(2)}) collective-permute-start(f32[3,24]{1,0:T(4,128)S(1)} %get-tuple-element.139), channel_id=1, source_target_pairs={{0,2},{1,3},{2,0},{3,1},{4,6},{5,7},{6,4},{7,5},{8,10},{9,11},{10,... | collective-permute-start | bytes 872 | tf_op jit(solution)/shard_map/ppermute | solution.py:568
  14.6 7.6 %collective-permute-start = (f32[3,24]{1,0:T(4,128)S(1)}, f32[3,24]{1,0:T(4,128)S(1)}, u32[]{:S(2)}, u32[]{:S(2)}) collective-permute-start(f32[3,24]{1,0:T(4,128)S(1)} %get-tuple-element.139), channel_id=1, source_target_pairs={{0,1},{1,2},{2,3},{3,0},{4,5},{5,6},{6,7},{7,4},{8,9},{9,10},{10,1... | collective-permute-start | bytes 872 | tf_op jit(solution)/shard_map/ppermute | solution.py:568
  17.4 9.8 %collective-permute-start.6 = (bf16[96,960]{1,0:T(8,128)(2,1)S(1)}, bf16[96,960]{1,0:T(8,128)(2,1)S(1)}, u32[]{:S(2)}, u32[]{:S(2)}) collective-permute-start(bf16[96,960]{1,0:T(8,128)(2,1)S(1)} %pad_maximum_fusion.7), channel_id=1, source_target_pairs={{0,8},{4,12},{8,0},{12,4},{16,24},{20,28},{24,16},{28,20},{1,9},{5... | collective-permute-start | bytes 552968 | tf_op jit(solution)/shard_map/ppermute | solution.py:27
  20.2 8.7 %collective-permute-start.9 = (bf16[96,1344]{1,0:T(8,128)(2,1)S(1)}, bf16[96,1344]{1,0:T(8,128)(2,1)S(1)}, u32[]{:S(2)}, u32[]{:S(2)}) collective-permute-start(bf16[96,1344]{1,0:T(8,128)(2,1)S(1)} %pad_maximum_fusion.6), channel_id=1, source_target_pairs={{0,16},{4,20},{8,24},{12,28},{16,0},{20,4},{24,8},{28,12},{1,17},{... | collective-permute-start | bytes 774152 | tf_op jit(solution)/shard_map/ppermute | solution.py:27
  21.8 150.3 %reduce-scatter.3.cloned.1.call-start = ((), (), s32[]{:S(2)}) async-start(), calls=%async_computation.3 | async-start | bytes 1966080 | tf_op jit(solution)/shard_map/reduce_scatter | solution.py:613
  27.4 8.6 %collective-permute-start.7 = (bf16[2,96,960]{2,1,0:T(8,128)(2,1)S(1)}, bf16[2,96,960]{2,1,0:T(8,128)(2,1)S(1)}, u32[]{:S(2)}, u32[]{:S(2)}) collective-permute-start(bf16[2,96,960]{2,1,0:T(8,128)(2,1)S(1)} %pad_maximum_fusion.5), channel_id=1, source_target_pairs={{0,16},{4,20},{8,24},{12,28},{16,0},{20,4},{24,8},{28,12},{1,17},{... | collective-permute-start | bytes 1105928 | tf_op jit(solution)/shard_map/ppermute | solution.py:27
  29.1 11.4 %collective-permute-start.10 = (bf16[2,96,1344]{2,1,0:T(8,128)(2,1)S(1)}, bf16[2,96,1344]{2,1,0:T(8,128)(2,1)S(1)}, u32[]{:S(2)}, u32[]{:S(2)}) collective-permute-start(bf16[2,96,1344]{2,1,0:T(8,128)(2,1)S(1)} %pad_maximum_fusion.4), channel_id=1, source_target_pairs={{0,8},{4,12},{8,0},{12,4},{16,24},{20,28},{24,16},{28,20},{1,9},{5... | collective-permute-start | bytes 1548296 | tf_op jit(solution)/shard_map/ppermute | solution.py:27
  37.0 9.1 %collective-permute-start.8 = (bf16[2,2,96,960]{3,2,1,0:T(8,128)(2,1)}, bf16[2,2,96,960]{3,2,1,0:T(8,128)(2,1)}, u32[]{:S(2)}, u32[]{:S(2)}) collective-permute-start(bf16[2,2,96,960]{3,2,1,0:T(8,128)(2,1)} %pad_maximum_fusion.3), channel_id=1, source_target_pairs={{0,4},{4,0},{8,12},{12,8},{16,20},{20,16},{24,28},{28,24},{1,5},{5... | collective-permute-start | bytes 2211848 | tf_op jit(solution)/shard_map/ppermute | solution.py:27
  40.8 8.2 %collective-permute-start.11 = (bf16[2,2,96,1344]{3,2,0,1:T(8,128)(2,1)S(1)}, bf16[2,2,96,1344]{3,2,0,1:T(8,128)(2,1)}, u32[]{:S(2)}, u32[]{:S(2)}) collective-permute-start(bf16[2,2,96,1344]{3,2,0,1:T(8,128)(2,1)S(1)} %pad_maximum_fusion.2), channel_id=1, source_target_pairs={{0,4},{4,0},{8,12},{12,8},{16,20},{20,16},{24,28},{28,24},{1,5},{5... | collective-permute-start | bytes 3096584 | tf_op jit(solution)/shard_map/ppermute | solution.py:27
  73.8 100.2 %reduce-scatter.5.cloned.1.call-start = ((), (), s32[]{:S(2)}) async-start(), calls=%async_computation.5 | async-start | bytes 1966080 | tf_op jit(solution)/shard_map/reduce_scatter | solution.py:655
  112.3 10.3 %collective-permute-start.14 = (f32[2,8,24]{2,1,0:T(8,128)S(1)}, f32[2,8,24]{2,1,0:T(8,128)S(1)}, u32[]{:S(2)}, u32[]{:S(2)}) collective-permute-start(f32[2,8,24]{2,1,0:T(8,128)S(1)} %bitcast.147), channel_id=1, source_target_pairs={{0,3},{1,0},{2,1},{3,2},{4,7},{5,4},{6,5},{7,6},{8,11},{9,8},{10,9... | collective-permute-start | bytes 4616 | tf_op jit(solution)/shard_map/ppermute | solution.py:665
  113.4 9.3 %collective-permute-start.13 = (f32[2,8,24]{2,1,0:T(8,128)S(1)}, f32[2,8,24]{2,1,0:T(8,128)S(1)}, u32[]{:S(2)}, u32[]{:S(2)}) collective-permute-start(f32[2,8,24]{2,1,0:T(8,128)S(1)} %bitcast.146), channel_id=1, source_target_pairs={{0,2},{1,3},{2,0},{3,1},{4,6},{5,7},{6,4},{7,5},{8,10},{9,11},{10,... | collective-permute-start | bytes 4616 | tf_op jit(solution)/shard_map/ppermute | solution.py:665
  114.3 8.4 %collective-permute-start.12 = (f32[2,8,24]{2,1,0:T(8,128)S(1)}, f32[2,8,24]{2,1,0:T(8,128)S(1)}, u32[]{:S(2)}, u32[]{:S(2)}) collective-permute-start(f32[2,8,24]{2,1,0:T(8,128)S(1)} %bitcast.145), channel_id=1, source_target_pairs={{0,1},{1,2},{2,3},{3,0},{4,5},{5,6},{6,7},{7,4},{8,9},{9,10},{10,1... | collective-permute-start | bytes 4616 | tf_op jit(solution)/shard_map/ppermute | solution.py:665
  122.6 21.6 %collective-permute-start.23 = (bf16[4,96,1728]{2,1,0:T(8,128)(2,1)}, bf16[4,96,1728]{2,1,0:T(8,128)(2,1)S(1)}, u32[]{:S(2)}, u32[]{:S(2)}) collective-permute-start(bf16[4,96,1728]{2,1,0:T(8,128)(2,1)} %shard_map.196), channel_id=1, source_target_pairs={{0,4},{4,0},{8,12},{12,8},{16,20},{20,16},{24,28},{28,24},{1,5},{5... | collective-permute-start | bytes 3981320 | tf_op jit(solution)/shard_map/ppermute | solution.py:27
  126.0 7.8 %collective-permute-start.18 = (f32[256]{0:T(256)S(1)}, f32[256]{0:T(256)S(1)}, u32[]{:S(2)}, u32[]{:S(2)}) collective-permute-start(f32[256]{0:T(256)S(1)} %bitcast.155), channel_id=1, source_target_pairs={{0,24},{4,28},{8,16},{12,20},{16,8},{20,12},{24,0},{28,4},{1,25},{... | collective-permute-start | bytes 3080 | tf_op jit(solution)/shard_map/ppermute | solution.py:27
  140.8 14.3 %collective-permute-start.22 = (bf16[96,576]{1,0:T(8,128)(2,1)}, bf16[96,576]{1,0:T(8,128)(2,1)S(1)}, u32[]{:S(2)}, u32[]{:S(2)}) collective-permute-start(bf16[96,576]{1,0:T(8,128)(2,1)} %get-tuple-element.63), channel_id=1, source_target_pairs={{0,24},{4,28},{8,16},{12,20},{16,8},{20,12},{24,0},{28,4},{1,25},{... | collective-permute-start | bytes 331784 | tf_op jit(solution)/shard_map/ppermute | solution.py:27
  143.2 13.0 %collective-permute-start.21 = (bf16[96,576]{1,0:T(8,128)(2,1)}, bf16[96,576]{1,0:T(8,128)(2,1)S(1)}, u32[]{:S(2)}, u32[]{:S(2)}) collective-permute-start(bf16[96,576]{1,0:T(8,128)(2,1)} %get-tuple-element.62), channel_id=1, source_target_pairs={{0,16},{4,20},{8,24},{12,28},{16,0},{20,4},{24,8},{28,12},{1,17},{... | collective-permute-start | bytes 331784 | tf_op jit(solution)/shard_map/ppermute | solution.py:27
  143.7 12.5 %collective-permute-start.20 = (bf16[96,576]{1,0:T(8,128)(2,1)}, bf16[96,576]{1,0:T(8,128)(2,1)S(1)}, u32[]{:S(2)}, u32[]{:S(2)}) collective-permute-start(bf16[96,576]{1,0:T(8,128)(2,1)} %get-tuple-element.61), channel_id=1, source_target_pairs={{0,8},{4,12},{8,0},{12,4},{16,24},{20,28},{24,16},{28,20},{1,9},{5... | collective-permute-start | bytes 331784 | tf_op jit(solution)/shard_map/ppermute | solution.py:27
  152.1 12.1 %collective-permute-start.26 = (bf16[96,1728]{1,0:T(8,128)(2,1)}, bf16[96,1728]{1,0:T(8,128)(2,1)S(1)}, u32[]{:S(2)}, u32[]{:S(2)}) collective-permute-start(bf16[96,1728]{1,0:T(8,128)(2,1)} %get-tuple-element.68), channel_id=1, source_target_pairs={{0,24},{4,28},{8,16},{12,20},{16,8},{20,12},{24,0},{28,4},{1,25},{... | collective-permute-start | bytes 995336 | tf_op jit(solution)/shard_map/ppermute | solution.py:27
  154.6 15.7 %collective-permute-start.25 = (bf16[96,1728]{1,0:T(8,128)(2,1)}, bf16[96,1728]{1,0:T(8,128)(2,1)S(1)}, u32[]{:S(2)}, u32[]{:S(2)}) collective-permute-start(bf16[96,1728]{1,0:T(8,128)(2,1)} %get-tuple-element.67), channel_id=1, source_target_pairs={{0,16},{4,20},{8,24},{12,28},{16,0},{20,4},{24,8},{28,12},{1,17},{... | collective-permute-start | bytes 995336 | tf_op jit(solution)/shard_map/ppermute | solution.py:27
  155.1 15.3 %collective-permute-start.24 = (bf16[96,1728]{1,0:T(8,128)(2,1)}, bf16[96,1728]{1,0:T(8,128)(2,1)S(1)}, u32[]{:S(2)}, u32[]{:S(2)}) collective-permute-start(bf16[96,1728]{1,0:T(8,128)(2,1)} %get-tuple-element.66), channel_id=1, source_target_pairs={{0,8},{4,12},{8,0},{12,4},{16,24},{20,28},{24,16},{28,20},{1,9},{5... | collective-permute-start | bytes 995336 | tf_op jit(solution)/shard_map/ppermute | solution.py:27
  (19 other events, 152.0 us)
Sparse Core Ops, SparseCore 0:
  9.6 39.7 all-gather.2
  50.9 35.8 all-gather.4
  89.2 34.8 reduce-scatter.2
  126.2 34.2 reduce-scatter.4

commit v4 on v3

--- a/solution.py
+++ b/solution.py
@@ -79,10 +79,11 @@
 
 def enter_kernel(
     heads, head_dim, qkv_cols, x_ref, vec_ref, in_bias_ref, qkv_bias_ref, first_ref, second_ref,
-    cos_ref, sin_ref, normed_t_ref, proj_t_ref, hidden_ref, slope_ref,
+    cos_ref, sin_ref, unit_ref, normed_t_ref, proj_t_ref, hidden_ref, slope_ref,
 ):
     width = heads * head_dim
     unit, _ = normalize(x_ref[...])
+    unit_ref[...] = unit.astype(BF16)
     wide = unit * vec_ref[0:1] + vec_ref[1:2]
     normed = wide.astype(BF16)
     normed_t_ref[...] = jnp.transpose(normed)
@@ -191,7 +192,7 @@
 
 
 def return_kernel(
-    out_cols, after_ref, cot_ref, slope_ref, first_ref, second_ref,
+    out_cols, after_ref, places_ref, cot_ref, slope_ref, first_ref, second_ref,
     cot_t_ref, ctx_grad_t_ref, pre_low_ref, in_sum_ref, cot_sum_ref,
 ):
     cot = cot_ref[...]
@@ -211,7 +212,7 @@
 
 
 def norm_kernel(
-    qkv_cols, x_ref, dq_ref, dk_ref, dv_ref, pre_low_ref, first_ref, second_ref,
+    qkv_cols, unit_ref, dq_ref, dk_ref, dv_ref, pre_low_ref, first_ref, second_ref,
     proj_low_ref, norm_grad_ref, gain_sum_ref, shift_sum_ref,
 ):
     proj_low = jnp.transpose(
@@ -221,7 +222,7 @@
     norm_grad = dot(proj_low, second_ref[:, qkv_cols], (1, 1))
     norm_grad = norm_grad + dot(pre_low_ref[...], first_ref[...], (1, 1))
     norm_grad_ref[...] = norm_grad.astype(BF16)
-    unit, _ = normalize(x_ref[...])
+    unit = unit_ref[...].astype(F32)
 
     @pl.when(pl.program_id(0) == 0)
     def _():
@@ -232,9 +233,9 @@
     shift_sum_ref[...] += row_sums(norm_grad)
 
 
-def half_rows(ref, at_ref, blocks, part):
-    chips = [lax.bitwise_xor(at_ref[1], k) for k in range(blocks)]
-    starts = [pl.multiple_of((2 * chip + at_ref[0]) * part, part) for chip in chips]
+def half_rows(ref, places_ref, row, blocks, part):
+    chips = [lax.bitwise_xor(places_ref[1], k) for k in range(blocks)]
+    starts = [pl.multiple_of((2 * chip + places_ref[2 * row]) * part, part) for chip in chips]
     return jnp.concatenate([ref[pl.ds(start, part), :] for start in starts], axis=0)
 
 
@@ -249,19 +250,19 @@
         outs[k][:, columns] = value[k].astype(outs[k].dtype)
 
 
-def early_kernel(blocks, part, at_ref, normed_t_ref, cot_t_ref, pre_low_ref, ctx_ref, hidden_ref, *refs):
+def early_kernel(blocks, part, row, at_ref, normed_t_ref, cot_t_ref, pre_low_ref, ctx_ref, hidden_ref, *refs):
     got_ref, outs = (None, refs) if len(refs) == 1 else (refs[0], refs[1:])
     units = hidden_ref.shape[1]
-    left = half_rows(normed_t_ref, at_ref, blocks, part)
+    left = half_rows(normed_t_ref, at_ref, row, blocks, part)
     put(outs, got_ref, slice(0, units), dot(left, pre_low_ref[...], (1, 0)))
-    left = half_rows(cot_t_ref, at_ref, blocks, part)
+    left = half_rows(cot_t_ref, at_ref, row, blocks, part)
     put(outs, got_ref, slice(units, 2 * units), dot(left, hidden_ref[...], (1, 0)))
     put(outs, got_ref, slice(2 * units, None), dot(left, ctx_ref[...], (1, 0)))
 
 
-def late_kernel(blocks, part, at_ref, normed_t_ref, proj_low_ref, *refs):
+def late_kernel(blocks, part, row, at_ref, normed_t_ref, proj_low_ref, *refs):
     got_ref, outs = (None, refs) if len(refs) == 1 else (refs[0], refs[1:])
-    left = half_rows(normed_t_ref, at_ref, blocks, part)
+    left = half_rows(normed_t_ref, at_ref, row, blocks, part)
     put(outs, got_ref, slice(None), dot(left, proj_low_ref[...], (1, 0)))
 
 
@@ -311,11 +312,11 @@
             first_spec, second_spec, table, table,
         ],
         out_specs=[
-            tokens_t(model, block), tokens_t(proj, block),
+            tokens(block, model), tokens_t(model, block), tokens_t(proj, block),
             tokens(block, hidden_units), tokens(block, hidden_units),
         ],
         out_shape=[
-            struct(model, rows), struct(proj, rows),
+            struct(rows, model), struct(model, rows), struct(proj, rows),
             struct(rows, hidden_units), struct(rows, hidden_units, dtype=F32),
         ],
         cost_estimate=cost(
@@ -393,7 +394,7 @@
     )(ctx_t, hidden, first, second)
 
 
-def return_grads(after, cot, slopes, first, second, width):
+def return_grads(after, places, cot, slopes, first, second, width):
     rows, model = cot.shape
     hidden_units = slopes.shape[1]
     block = min(256, rows)
@@ -403,7 +404,8 @@
         functools.partial(return_kernel, out_cols),
         grid=(rows // block,),
         in_specs=[
-            pl.BlockSpec(memory_space=pl.ANY), tokens(block, model), tokens(block, hidden_units), first_spec, second_spec,
+            pl.BlockSpec(memory_space=pl.ANY), pl.BlockSpec(memory_space=pl.ANY),
+            tokens(block, model), tokens(block, hidden_units), first_spec, second_spec,
         ],
         out_specs=[
             tokens_t(model, block), tokens_t(width, block), tokens(block, hidden_units),
@@ -416,7 +418,7 @@
         ],
         cost_estimate=cost(2 * rows * model * (width + hidden_units), 10 * rows * model),
         name="return_grads",
-    )(after, cot, slopes, first, second)
+    )(after, places, cot, slopes, first, second)
 
 
 def norm_sum(x, dq_t, dk_t, dv_t, pre_low, first, second):
@@ -471,14 +473,14 @@
     )(x, cot, own, gain)
 
 
-def weight_half(kernel, at, operands, got, blocks, part, shape, flops):
+def weight_half(kernel, places, row, operands, got, blocks, part, shape, flops):
     if got is None:
         outs = [struct(blocks, *shape)]
     else:
         operands = operands + (got,)
         outs = [struct(*shape, dtype=F32)] + [struct(*shape)] * (blocks - 1)
     return pl.pallas_call(
-        functools.partial(kernel, blocks, part),
+        functools.partial(kernel, blocks, part, row),
         grid_spec=pltpu.PrefetchScalarGridSpec(
             num_scalar_prefetch=1,
             grid=(1,),
@@ -487,7 +489,7 @@
         ),
         out_shape=outs,
         cost_estimate=cost(flops, 4 * operands[0].size),
-    )(jnp.stack(at).astype(jnp.int32), *operands)
+    )(places, *operands)
 
 
 def rotary_tables(length):
@@ -604,7 +606,7 @@
     second = second.reshape(model, -1)
 
     cosine, sine = rotary_tables(length)
-    normed_t, proj_t, hidden, slopes = enter(
+    unit, normed_t, proj_t, hidden, slopes = enter(
         full_in, norm_rows, in_bias.reshape(1, -1), qkv_bias.reshape(1, -1), first, second,
         cosine, sine, heads, head_dim,
     )
@@ -615,24 +617,24 @@
     )
     outputs = (inputs.astype(F32) + summed.astype(F32) + out_shift).astype(BF16)
 
+    core, chip = bit_of("dp", 1), lax.axis_index("dp") // 2
+    places = jnp.stack([1 - core, chip, core, chip]).astype(jnp.int32)
     cot_t, ctx_grad_t, pre_low, in_sum, cot_sum = return_grads(
-        context, full_cot, slopes, first, second, width
+        context, places, full_cot, slopes, first, second, width
     )
     part = model // dp
-    core = bit_of("dp", 1)
     aligned = 2 <= dp <= 8 and part % 16 == 0
-    chip = lax.axis_index("dp") // 2
     blocks = dp // 2
     if aligned:
         operands = (normed_t, cot_t, pre_low, context, hidden)
         shape = (part, 2 * hidden_units + width)
         flops = rows * model * shape[1]
         (early_sent,) = weight_half(
-            early_kernel, (1 - core, chip), operands, None, blocks, part, shape, flops
+            early_kernel, places, 0, operands, None, blocks, part, shape, flops
         )
         early_got = swap_core(early_sent, dp)
         early_pieces = weight_half(
-            early_kernel, (core, chip), operands, early_got, blocks, part,
+            early_kernel, places, 1, operands, early_got, blocks, part,
             shape, flops,
         )
         early = add_pieces(early_pieces, dp)
@@ -650,7 +652,7 @@
         proj_t, cosine, sine, probs, ctx_grad_t, seqs, heads, head_dim, length
     )
     proj_low, norm_grad, gain_sum, shift_sum = norm_sum(
-        full_in, dq_t, dk_t, dv_t, pre_low, first, second
+        unit, dq_t, dk_t, dv_t, pre_low, first, second
     )
     own_grad = lax.psum_scatter(
         norm_grad.reshape(seqs, length, model), "tensor", scatter_dimension=1, tiled=True
@@ -685,12 +687,12 @@
         shape = (part, 3 * width)
         flops = rows * model * shape[1]
         (late_sent,) = weight_half(
-            late_kernel, (1 - core, chip), operands, None, blocks, part, shape,
+            late_kernel, places, 0, operands, None, blocks, part, shape,
             flops,
         )
         late_got = swap_core(late_sent, dp)
         late_pieces = weight_half(
-            late_kernel, (core, chip), operands, late_got, blocks, part, shape,
+            late_kernel, places, 1, operands, late_got, blocks, part, shape,
             flops,
         )
         late = add_pieces(late_pieces, dp)

time: 184 us -> 184 us (level)
  no operation moved by 1% of the time
where the time goes in v4:
time: 184 us; the launch traced here: 183 us
  Pallas kernels  70.4 us (38%)
  waiting for transfers between devices  42.1 us (23%)
  starting transfers between devices  27.4 us (15%)
  local copies, waits for them, and re-layouts  16.5 us (9%)
  between operations  14.3 us (8%)
  other arithmetic  12.3 us (7%)
    ppermute x21, waiting for transfers between devices, swap(): return lax.ppermute(x, axis_name, [(i, i ^ step) for i in range(size)])  29.1 us
    pallas_call x4, Pallas kernels, weight_half(): pl.pallas_call(functools.partial(kernel, blocks, part, row), grid_spec=pl...  21.6 us
    ppermute x21, starting transfers between devices, swap(): return lax.ppermute(x, axis_name, [(i, i ^ step) for i in range(size)])  18 us
    all_gather x1, waiting for transfers between devices, body(): lax.all_gather(cotangent, 'tensor', axis=1, tiled=True).reshape(rows, model)  12.2 us
    pallas_call x1, Pallas kernels, attend_back(): pl.pallas_call(functools.partial(backward_kernel, scale, block), grid=(se...  11.1 us
    pallas_call x1, Pallas kernels, attend(): pl.pallas_call(functools.partial(forward_kernel, scale, block), grid=(seq...  8.37 us
    pallas_call x1, Pallas kernels, enter(): pl.pallas_call(functools.partial(enter_kernel, heads, head_dim, qkv_cols)...  7.94 us
    pallas_call x1, Pallas kernels, norm_sum(): pl.pallas_call(functools.partial(norm_kernel, qkv_cols), grid=(rows // bl...  7.18 us
  transfers between devices with their start and end apart: 31, of which 10 were waited for; matrix products, arithmetic and copies ran while one was open for 15% of the time, Pallas kernels for 37%

profile of v4, /device:TPU:0, one launch (start us, length us, event | category | flops | bytes accessed | tf_op | source)
XLA Modules:
  0.0 183.0 jit_solution(15122773469920503195)
XLA Ops:
  9.4 5.1 %collective-permute-start.2 = (f32[3,24]{1,0:T(4,128)S(1)}, f32[3,24]{1,0:T(4,128)S(1)}, u32[]{:S(2)}, u32[]{:S(2)}) collective-permute-start(f32[3,24]{1,0:T(4,128)S(1)} %get-tuple-element.141), channel_id=1, source_target_pairs={{0,3},{1,0},{2,1},{3,2},{4,7},{5,4},{6,5},{7,6},{8,11},{9,8},{10,9... | collective-permute-start | bytes 872 | tf_op jit(solution)/shard_map/ppermute | solution.py:570
  20.2 1.6 collective-permute-start.9
  23.6 3.1 %collective-permute-done.3 = f32[8,128]{1,0:T(8,128)S(1)} collective-permute-done((f32[8,128]{1,0:T(8,128)S(1)}, f32[8,128]{1,0:T(8,128)S(1)}, u32[]{:S(2)}, u32[]{:S(2)}) %collective-permute-start.3) | collective-permute-done | bytes 4128 | tf_op jit(solution)/shard_map/ppermute | solution.py:27
  30.5 5.5 %collective-permute-done.7 = bf16[2,96,960]{2,1,0:T(8,128)(2,1)S(1)} collective-permute-done((bf16[2,96,960]{2,1,0:T(8,128)(2,1)S(1)}, bf16[2,96,960]{2,1,0:T(8,128)(2,1)S(1)}, u32[]{:S(2)}, u32[]{:S(2)}) %collective-permute-start.7) | collective-permute-done | bytes 368672 | tf_op jit(solution)/shard_map/ppermute | solution.py:27
  37.0 3.5 %collective-permute-done.10 = bf16[2,96,1344]{2,1,0:T(8,128)(2,1)S(1)} collective-permute-done((bf16[2,96,1344]{2,1,0:T(8,128)(2,1)S(1)}, bf16[2,96,1344]{2,1,0:T(8,128)(2,1)S(1)}, u32[]{:S(2)}, u32[]{:S(2)}) %collective-permute-start.10) | collective-permute-done | bytes 516128 | tf_op jit(solution)/shard_map/ppermute | solution.py:27
  52.1 7.9 %enter.1 = (bf16[1024,768]{1,0:T(8,128)(2,1)}, bf16[768,1024]{1,0:T(8,128)(2,1)}, bf16[576,1024]{1,0:T(8,128)(2,1)}, bf16[1024,768]{1,0:T(8,128)(2,1)}, f32[1024,768]{1,0:T(8,128)}) custom-call(bf16[1024,768]{1,0:T(8,128)(2,1)} %bitcast.156, f32[3,768]{1,0:T(4,128)} %reshape.183.vec_ref, f32[1,768]{1,0:T(1,128)} %reshape_reshape.16.in_bias_ref, ...), custom_call_target="tpu_custom_call" | custom-call | flops 2113929216 | bytes 12976128 | tf_op jit(solution)/shard_map/enter/pallas_call | solution.py:307
  60.1 8.4 %attend_forward.1 = (bf16[192,1024]{1,0:T(8,128)(2,1)}, bf16[1,3,1024,1024]{3,2,1,0:T(8,128)(2,1)}) custom-call(bf16[576,1024]{1,0:T(8,128)(2,1)} %get-tuple-element.41.q_ref.k_ref.v_ref, bf16[576,1024]{1,0:T(8,128)(2,1)} %get-tuple-element.41.q_ref.k_ref.v_ref, bf16[576,1024]{1,0:T(8,128)(2,1)} %get-tuple-element.41.q_ref.k_ref.v_ref), custom_call_target="tpu_custom_call" | custom-call | flops 805306368 | bytes 2359296 | tf_op jit(solution)/shard_map/attend_forward/pallas_call | solution.py:339
  68.4 5.5 %branch.1 = (bf16[1024,768]{1,0:T(8,128)(2,1)}, bf16[1024,192]{1,0:T(8,128)(2,1)}) custom-call(bf16[192,1024]{1,0:T(8,128)(2,1)} %get-tuple-element.42.ctx_t_ref, bf16[1024,768]{1,0:T(8,128)(2,1)} %get-tuple-element.43.hidden_ref, bf16[768,960]{1,0:T(8,128)(2,1)} %bitcast.116, bf16[768,1344]{1,0:T(8,128)(2,1)} %bitcast.112), custom_call_target="tpu_custom_call" | custom-call | flops 1509949440 | bytes 6291456 | tf_op jit(solution)/shard_map/branch/pallas_call | solution.py:384
  74.6 12.2 %all-gather.5.cloned.1.call-done = bf16[1,1024,768]{2,1,0:T(8,128)(2,1)} async-done(((bf16[1,256,768]{2,1,0:T(8,128)(2,1)}), bf16[1,1024,768]{2,1,0:T(8,128)(2,1)}) %all-gather.5.cloned.1.call-update) | async-done | bytes 1572880 | tf_op jit(solution)/shard_map/all_gather | solution.py:564
  86.8 6.2 %return_grads.1 = (bf16[768,1024]{1,0:T(8,128)(2,1)}, bf16[192,1024]{1,0:T(8,128)(2,1)}, bf16[1024,768]{1,0:T(8,128)(2,1)}, f32[8,768]{1,0:T(8,128)}, f32[8,768]{1,0:T(8,128)}) custom-call(bf16[1024,192]{1,0:T(8,128)(2,1)} %get-tuple-element.47.after_ref.ctx_ref, s32[4]{0:T(128)} %pad_add_fusion.places_ref.at_ref, bf16[1024,768]{1,0:T(8,128)(2,1)} %bitcast.119, ...), custom_call_target="tpu_custom_call" | custom-call | flops 1509949440 | bytes 7864320 | tf_op jit(solution)/shard_map/return_grads/pallas_call | solution.py:403
  93.0 11.1 %attend_backward.1 = (bf16[192,1024]{1,0:T(8,128)(2,1)}, bf16[192,1024]{1,0:T(8,128)(2,1)}, bf16[192,1024]{1,0:T(8,128)(2,1)}, f32[1,3,3,64,128]{4,3,2,1,0:T(8,128)}) custom-call(bf16[576,1024]{1,0:T(8,128)(2,1)} %get-tuple-element.41.q_ref.k_ref.v_ref, bf16[576,1024]{1,0:T(8,128)(2,1)} %get-tuple-element.41.q_ref.k_ref.v_ref, ...), custom_call_target="tpu_custom_call" | custom-call | flops 2013265920 | bytes 3538944 | tf_op jit(solution)/shard_map/attend_backward/pallas_call | solution.py:365
  104.2 7.2 %norm_grads.1 = (bf16[1024,576]{1,0:T(8,128)(2,1)}, bf16[1024,768]{1,0:T(8,128)(2,1)}, f32[8,768]{1,0:T(8,128)}, f32[8,768]{1,0:T(8,128)}) custom-call(bf16[1024,768]{1,0:T(8,128)(2,1)} %get-tuple-element.45.unit_ref, bf16[192,1024]{1,0:T(8,128)(2,1)} %get-tuple-element.50.dq_ref, bf16[192,1024]{1,0:T(8,128)(2,1)} %get-tuple-element.51.dk_ref, ...), custom_call_target="tpu_custom_call" | custom-call | flops 2113929216 | bytes 6291456 | tf_op jit(solution)/shard_map/norm_grads/pallas_call | solution.py:431
  115.7 6.5 %shard_map.196 = bf16[4,96,1728]{2,1,0:T(8,128)(2,1)} custom-call(s32[4]{0:T(128)} %pad_add_fusion.places_ref.at_ref, bf16[768,1024]{1,0:T(8,128)(2,1)} %get-tuple-element.60.normed_t_ref, bf16[768,1024]{1,0:T(8,128)(2,1)} %get-tuple-element.66.cot_t_ref, bf16[1024,768]{1,0:T(8,128)(2,1)} %get-tuple-element.53.pre_low_ref, ...), custom_call_target="tpu_custom_call" | custom-call | flops 1358954496 | bytes 3145728 | tf_op jit(solution)/shard_map/pallas_call | solution.py:482
  124.1 1.8 collective-permute-done.15
  126.0 2.4 %collective-permute-start.18 = (f32[256]{0:T(256)S(1)}, f32[256]{0:T(256)S(1)}, u32[]{:S(2)}, u32[]{:S(2)}) collective-permute-start(f32[256]{0:T(256)S(1)} %bitcast.153), channel_id=1, source_target_pairs={{0,24},{4,28},{8,16},{12,20},{16,8},{20,12},{24,0},{28,4},{1,25},{... | collective-permute-start | bytes 3080 | tf_op jit(solution)/shard_map/ppermute | solution.py:27
  129.5 4.3 %shard_map.194 = bf16[4,96,576]{2,1,0:T(8,128)(2,1)} custom-call(s32[4]{0:T(128)} %pad_add_fusion.places_ref.at_ref, bf16[768,1024]{1,0:T(8,128)(2,1)} %get-tuple-element.60.normed_t_ref, bf16[1024,576]{1,0:T(8,128)(2,1)} %get-tuple-element.61.proj_low_ref), custom_call_target="tpu_custom_call" | custom-call | flops 452984832 | bytes 3145728 | tf_op jit(solution)/shard_map/pallas_call | solution.py:482
  136.7 4.1 %shard_map.195 = (f32[96,576]{1,0:T(8,128)}, bf16[96,576]{1,0:T(8,128)(2,1)}, bf16[96,576]{1,0:T(8,128)(2,1)}, bf16[96,576]{1,0:T(8,128)(2,1)}) custom-call(s32[4]{0:T(128)} %pad_add_fusion.places_ref.at_ref, bf16[768,1024]{1,0:T(8,128)(2,1)} %get-tuple-element.60.normed_t_ref, bf16[1024,576]{1,0:T(8,128)(2,1)} %get-tuple-element.61.proj_low_ref, ...), custom_call_target="tpu_custom_call" | custom-call | flops 452984832 | bytes 3145728 | tf_op jit(solution)/shard_map/pallas_call | solution.py:482
  140.7 2.4 %collective-permute-start.22 = (bf16[96,576]{1,0:T(8,128)(2,1)}, bf16[96,576]{1,0:T(8,128)(2,1)S(1)}, u32[]{:S(2)}, u32[]{:S(2)}) collective-permute-start(bf16[96,576]{1,0:T(8,128)(2,1)} %get-tuple-element.65), channel_id=1, source_target_pairs={{0,24},{4,28},{8,16},{12,20},{16,8},{20,12},{24,0},{28,4},{1,25},{... | collective-permute-start | bytes 331784 | tf_op jit(solution)/shard_map/ppermute | solution.py:27
  145.3 6.8 %shard_map.197 = (f32[96,1728]{1,0:T(8,128)}, bf16[96,1728]{1,0:T(8,128)(2,1)}, bf16[96,1728]{1,0:T(8,128)(2,1)}, bf16[96,1728]{1,0:T(8,128)(2,1)}) custom-call(s32[4]{0:T(128)} %pad_add_fusion.places_ref.at_ref, bf16[768,1024]{1,0:T(8,128)(2,1)} %get-tuple-element.60.normed_t_ref, bf16[768,1024]{1,0:T(8,128)(2,1)} %get-tuple-element.66.cot_t_ref, ...), custom_call_target="tpu_custom_call" | custom-call | flops 1358954496 | bytes 3145728 | tf_op jit(solution)/shard_map/pallas_call | solution.py:482
  152.1 2.4 %collective-permute-start.26 = (bf16[96,1728]{1,0:T(8,128)(2,1)}, bf16[96,1728]{1,0:T(8,128)(2,1)S(1)}, u32[]{:S(2)}, u32[]{:S(2)}) collective-permute-start(bf16[96,1728]{1,0:T(8,128)(2,1)} %get-tuple-element.70), channel_id=1, source_target_pairs={{0,24},{4,28},{8,16},{12,20},{16,8},{20,12},{24,0},{28,4},{1,25},{... | collective-permute-start | bytes 995336 | tf_op jit(solution)/shard_map/ppermute | solution.py:27
  157.3 6.9 %collective-permute-done.26 = bf16[96,1728]{1,0:T(8,128)(2,1)S(1)} collective-permute-done((bf16[96,1728]{1,0:T(8,128)(2,1)}, bf16[96,1728]{1,0:T(8,128)(2,1)S(1)}, u32[]{:S(2)}, u32[]{:S(2)}) %collective-permute-start.26) | collective-permute-done | bytes 331808 | tf_op jit(solution)/shard_map/ppermute | solution.py:27
  164.2 6.0 %collective-permute-done.25 = bf16[96,1728]{1,0:T(8,128)(2,1)S(1)} collective-permute-done((bf16[96,1728]{1,0:T(8,128)(2,1)}, bf16[96,1728]{1,0:T(8,128)(2,1)S(1)}, u32[]{:S(2)}, u32[]{:S(2)}) %collective-permute-start.25) | collective-permute-done | bytes 331808 | tf_op jit(solution)/shard_map/ppermute | solution.py:27
  172.1 1.9 %add_convert_fusion = bf16[1,256,768]{2,1,0:T(8,128)(2,1)} fusion(bf16[1,256,768]{2,1,0:T(8,128)(2,1)} %reduce-scatter.3.cloned.1.call-done, bf16[1,256,768]{2,1,0:T(8,128)(2,1)S(1)} %copy-done, f32[768]{0:T(1024)S(1)} %add.180), kind=kLoop, calls=%fused_computation.7 | loop fusion | flops 983040 | bytes 1182720 | tf_op jit(solution)/shard_map/convert_element_type | solution.py:618
  173.9 2.5 %finish.1 = bf16[1,256,768]{2,1,0:T(8,128)(2,1)} custom-call(bf16[1,256,768]{2,1,0:T(8,128)(2,1)} %x_ref.1, bf16[1,256,768]{2,1,0:T(8,128)(2,1)} %cot_ref.1, bf16[1,256,768]{2,1,0:T(8,128)(2,1)} %reduce-scatter.5.cloned.1.call-done.own_ref, f32[1,768]{1,0:T(1,128)} %slice.75.gain_ref), custom_call_target="tpu_custom_call" | custom-call | flops 3932160 | bytes 1572864 | tf_op jit(solution)/shard_map/finish/pallas_call | solution.py:465
  (173 shorter events, 43.5 us)
Async XLA Ops:
  7.2 44.9 %all-gather.3.cloned.1.call-start = ((), (), s32[]{:S(2)}) async-start(), calls=%async_computation.2 | async-start | bytes 1966080 | tf_op jit(solution)/shard_map/all_gather | solution.py:563
  8.0 78.9 %all-gather.5.cloned.1.call-start = ((), (), s32[]{:S(2)}) async-start(), calls=%async_computation.4 | async-start | bytes 1966080 | tf_op jit(solution)/shard_map/all_gather | solution.py:564
  9.4 12.7 %collective-permute-start.2 = (f32[3,24]{1,0:T(4,128)S(1)}, f32[3,24]{1,0:T(4,128)S(1)}, u32[]{:S(2)}, u32[]{:S(2)}) collective-permute-start(f32[3,24]{1,0:T(4,128)S(1)} %get-tuple-element.141), channel_id=1, source_target_pairs={{0,3},{1,0},{2,1},{3,2},{4,7},{5,4},{6,5},{7,6},{8,11},{9,8},{10,9... | collective-permute-start | bytes 872 | tf_op jit(solution)/shard_map/ppermute | solution.py:570
  14.6 7.6 %collective-permute-start.1 = (f32[3,24]{1,0:T(4,128)S(1)}, f32[3,24]{1,0:T(4,128)S(1)}, u32[]{:S(2)}, u32[]{:S(2)}) collective-permute-start(f32[3,24]{1,0:T(4,128)S(1)} %get-tuple-element.141), channel_id=1, source_target_pairs={{0,2},{1,3},{2,0},{3,1},{4,6},{5,7},{6,4},{7,5},{8,10},{9,11},{10,... | collective-permute-start | bytes 872 | tf_op jit(solution)/shard_map/ppermute | solution.py:570
  14.6 7.6 %collective-permute-start = (f32[3,24]{1,0:T(4,128)S(1)}, f32[3,24]{1,0:T(4,128)S(1)}, u32[]{:S(2)}, u32[]{:S(2)}) collective-permute-start(f32[3,24]{1,0:T(4,128)S(1)} %get-tuple-element.141), channel_id=1, source_target_pairs={{0,1},{1,2},{2,3},{3,0},{4,5},{5,6},{6,7},{7,4},{8,9},{9,10},{10,1... | collective-permute-start | bytes 872 | tf_op jit(solution)/shard_map/ppermute | solution.py:570
  17.4 9.8 %collective-permute-start.6 = (bf16[96,960]{1,0:T(8,128)(2,1)S(1)}, bf16[96,960]{1,0:T(8,128)(2,1)S(1)}, u32[]{:S(2)}, u32[]{:S(2)}) collective-permute-start(bf16[96,960]{1,0:T(8,128)(2,1)S(1)} %pad_maximum_fusion.7), channel_id=1, source_target_pairs={{0,8},{4,12},{8,0},{12,4},{16,24},{20,28},{24,16},{28,20},{1,9},{5... | collective-permute-start | bytes 552968 | tf_op jit(solution)/shard_map/ppermute | solution.py:27
  20.2 8.7 %collective-permute-start.9 = (bf16[96,1344]{1,0:T(8,128)(2,1)S(1)}, bf16[96,1344]{1,0:T(8,128)(2,1)S(1)}, u32[]{:S(2)}, u32[]{:S(2)}) collective-permute-start(bf16[96,1344]{1,0:T(8,128)(2,1)S(1)} %pad_maximum_fusion.6), channel_id=1, source_target_pairs={{0,16},{4,20},{8,24},{12,28},{16,0},{20,4},{24,8},{28,12},{1,17},{... | collective-permute-start | bytes 774152 | tf_op jit(solution)/shard_map/ppermute | solution.py:27
  21.8 150.2 %reduce-scatter.3.cloned.1.call-start = ((), (), s32[]{:S(2)}) async-start(), calls=%async_computation.3 | async-start | bytes 1966080 | tf_op jit(solution)/shard_map/reduce_scatter | solution.py:615
  27.4 8.6 %collective-permute-start.7 = (bf16[2,96,960]{2,1,0:T(8,128)(2,1)S(1)}, bf16[2,96,960]{2,1,0:T(8,128)(2,1)S(1)}, u32[]{:S(2)}, u32[]{:S(2)}) collective-permute-start(bf16[2,96,960]{2,1,0:T(8,128)(2,1)S(1)} %pad_maximum_fusion.5), channel_id=1, source_target_pairs={{0,16},{4,20},{8,24},{12,28},{16,0},{20,4},{24,8},{28,12},{1,17},{... | collective-permute-start | bytes 1105928 | tf_op jit(solution)/shard_map/ppermute | solution.py:27
  29.1 11.4 %collective-permute-start.10 = (bf16[2,96,1344]{2,1,0:T(8,128)(2,1)S(1)}, bf16[2,96,1344]{2,1,0:T(8,128)(2,1)S(1)}, u32[]{:S(2)}, u32[]{:S(2)}) collective-permute-start(bf16[2,96,1344]{2,1,0:T(8,128)(2,1)S(1)} %pad_maximum_fusion.4), channel_id=1, source_target_pairs={{0,8},{4,12},{8,0},{12,4},{16,24},{20,28},{24,16},{28,20},{1,9},{5... | collective-permute-start | bytes 1548296 | tf_op jit(solution)/shard_map/ppermute | solution.py:27
  37.0 9.1 %collective-permute-start.8 = (bf16[2,2,96,960]{3,2,1,0:T(8,128)(2,1)}, bf16[2,2,96,960]{3,2,1,0:T(8,128)(2,1)}, u32[]{:S(2)}, u32[]{:S(2)}) collective-permute-start(bf16[2,2,96,960]{3,2,1,0:T(8,128)(2,1)} %pad_maximum_fusion.3), channel_id=1, source_target_pairs={{0,4},{4,0},{8,12},{12,8},{16,20},{20,16},{24,28},{28,24},{1,5},{5... | collective-permute-start | bytes 2211848 | tf_op jit(solution)/shard_map/ppermute | solution.py:27
  40.8 8.1 %collective-permute-start.11 = (bf16[2,2,96,1344]{3,2,0,1:T(8,128)(2,1)S(1)}, bf16[2,2,96,1344]{3,2,0,1:T(8,128)(2,1)}, u32[]{:S(2)}, u32[]{:S(2)}) collective-permute-start(bf16[2,2,96,1344]{3,2,0,1:T(8,128)(2,1)S(1)} %pad_maximum_fusion.2), channel_id=1, source_target_pairs={{0,4},{4,0},{8,12},{12,8},{16,20},{20,16},{24,28},{28,24},{1,5},{5... | collective-permute-start | bytes 3096584 | tf_op jit(solution)/shard_map/ppermute | solution.py:27
  73.9 100.0 %reduce-scatter.5.cloned.1.call-start = ((), (), s32[]{:S(2)}) async-start(), calls=%async_computation.5 | async-start | bytes 1966080 | tf_op jit(solution)/shard_map/reduce_scatter | solution.py:657
  112.3 10.4 %collective-permute-start.14 = (f32[2,8,24]{2,1,0:T(8,128)S(1)}, f32[2,8,24]{2,1,0:T(8,128)S(1)}, u32[]{:S(2)}, u32[]{:S(2)}) collective-permute-start(f32[2,8,24]{2,1,0:T(8,128)S(1)} %bitcast.145), channel_id=1, source_target_pairs={{0,3},{1,0},{2,1},{3,2},{4,7},{5,4},{6,5},{7,6},{8,11},{9,8},{10,9... | collective-permute-start | bytes 4616 | tf_op jit(solution)/shard_map/ppermute | solution.py:667
  113.4 9.3 %collective-permute-start.13 = (f32[2,8,24]{2,1,0:T(8,128)S(1)}, f32[2,8,24]{2,1,0:T(8,128)S(1)}, u32[]{:S(2)}, u32[]{:S(2)}) collective-permute-start(f32[2,8,24]{2,1,0:T(8,128)S(1)} %bitcast.144), channel_id=1, source_target_pairs={{0,2},{1,3},{2,0},{3,1},{4,6},{5,7},{6,4},{7,5},{8,10},{9,11},{10,... | collective-permute-start | bytes 4616 | tf_op jit(solution)/shard_map/ppermute | solution.py:667
  114.3 8.4 %collective-permute-start.12 = (f32[2,8,24]{2,1,0:T(8,128)S(1)}, f32[2,8,24]{2,1,0:T(8,128)S(1)}, u32[]{:S(2)}, u32[]{:S(2)}) collective-permute-start(f32[2,8,24]{2,1,0:T(8,128)S(1)} %bitcast.143), channel_id=1, source_target_pairs={{0,1},{1,2},{2,3},{3,0},{4,5},{5,6},{6,7},{7,4},{8,9},{9,10},{10,1... | collective-permute-start | bytes 4616 | tf_op jit(solution)/shard_map/ppermute | solution.py:667
  122.6 21.7 %collective-permute-start.23 = (bf16[4,96,1728]{2,1,0:T(8,128)(2,1)}, bf16[4,96,1728]{2,1,0:T(8,128)(2,1)S(1)}, u32[]{:S(2)}, u32[]{:S(2)}) collective-permute-start(bf16[4,96,1728]{2,1,0:T(8,128)(2,1)} %shard_map.196), channel_id=1, source_target_pairs={{0,4},{4,0},{8,12},{12,8},{16,20},{20,16},{24,28},{28,24},{1,5},{5... | collective-permute-start | bytes 3981320 | tf_op jit(solution)/shard_map/ppermute | solution.py:27
  126.0 7.8 %collective-permute-start.18 = (f32[256]{0:T(256)S(1)}, f32[256]{0:T(256)S(1)}, u32[]{:S(2)}, u32[]{:S(2)}) collective-permute-start(f32[256]{0:T(256)S(1)} %bitcast.153), channel_id=1, source_target_pairs={{0,24},{4,28},{8,16},{12,20},{16,8},{20,12},{24,0},{28,4},{1,25},{... | collective-permute-start | bytes 3080 | tf_op jit(solution)/shard_map/ppermute | solution.py:27
  140.7 14.3 %collective-permute-start.22 = (bf16[96,576]{1,0:T(8,128)(2,1)}, bf16[96,576]{1,0:T(8,128)(2,1)S(1)}, u32[]{:S(2)}, u32[]{:S(2)}) collective-permute-start(bf16[96,576]{1,0:T(8,128)(2,1)} %get-tuple-element.65), channel_id=1, source_target_pairs={{0,24},{4,28},{8,16},{12,20},{16,8},{20,12},{24,0},{28,4},{1,25},{... | collective-permute-start | bytes 331784 | tf_op jit(solution)/shard_map/ppermute | solution.py:27
  143.1 13.0 %collective-permute-start.21 = (bf16[96,576]{1,0:T(8,128)(2,1)}, bf16[96,576]{1,0:T(8,128)(2,1)S(1)}, u32[]{:S(2)}, u32[]{:S(2)}) collective-permute-start(bf16[96,576]{1,0:T(8,128)(2,1)} %get-tuple-element.64), channel_id=1, source_target_pairs={{0,16},{4,20},{8,24},{12,28},{16,0},{20,4},{24,8},{28,12},{1,17},{... | collective-permute-start | bytes 331784 | tf_op jit(solution)/shard_map/ppermute | solution.py:27
  143.7 12.5 %collective-permute-start.20 = (bf16[96,576]{1,0:T(8,128)(2,1)}, bf16[96,576]{1,0:T(8,128)(2,1)S(1)}, u32[]{:S(2)}, u32[]{:S(2)}) collective-permute-start(bf16[96,576]{1,0:T(8,128)(2,1)} %get-tuple-element.63), channel_id=1, source_target_pairs={{0,8},{4,12},{8,0},{12,4},{16,24},{20,28},{24,16},{28,20},{1,9},{5... | collective-permute-start | bytes 331784 | tf_op jit(solution)/shard_map/ppermute | solution.py:27
  152.1 12.1 %collective-permute-start.26 = (bf16[96,1728]{1,0:T(8,128)(2,1)}, bf16[96,1728]{1,0:T(8,128)(2,1)S(1)}, u32[]{:S(2)}, u32[]{:S(2)}) collective-permute-start(bf16[96,1728]{1,0:T(8,128)(2,1)} %get-tuple-element.70), channel_id=1, source_target_pairs={{0,24},{4,28},{8,16},{12,20},{16,8},{20,12},{24,0},{28,4},{1,25},{... | collective-permute-start | bytes 995336 | tf_op jit(solution)/shard_map/ppermute | solution.py:27
  154.5 15.7 %collective-permute-start.25 = (bf16[96,1728]{1,0:T(8,128)(2,1)}, bf16[96,1728]{1,0:T(8,128)(2,1)S(1)}, u32[]{:S(2)}, u32[]{:S(2)}) collective-permute-start(bf16[96,1728]{1,0:T(8,128)(2,1)} %get-tuple-element.69), channel_id=1, source_target_pairs={{0,16},{4,20},{8,24},{12,28},{16,0},{20,4},{24,8},{28,12},{1,17},{... | collective-permute-start | bytes 995336 | tf_op jit(solution)/shard_map/ppermute | solution.py:27
  155.1 15.3 %collective-permute-start.24 = (bf16[96,1728]{1,0:T(8,128)(2,1)}, bf16[96,1728]{1,0:T(8,128)(2,1)S(1)}, u32[]{:S(2)}, u32[]{:S(2)}) collective-permute-start(bf16[96,1728]{1,0:T(8,128)(2,1)} %get-tuple-element.68), channel_id=1, source_target_pairs={{0,8},{4,12},{8,0},{12,4},{16,24},{20,28},{24,16},{28,20},{1,9},{5... | collective-permute-start | bytes 995336 | tf_op jit(solution)/shard_map/ppermute | solution.py:27
  (19 other events, 152.0 us)
Sparse Core Ops, SparseCore 0:
  9.6 39.7 all-gather.2
  50.9 35.8 all-gather.4
  89.1 34.8 reduce-scatter.2
  126.2 34.2 reduce-scatter.4

commit v5 on v4

--- a/solution.py
+++ b/solution.py
@@ -449,9 +449,9 @@
     )(x, dq_t, dk_t, dv_t, pre_low, first, second)
 
 
-def finish_kernel(x_ref, cot_ref, own_ref, gain_ref, grad_ref):
+def finish_kernel(x_ref, cot_ref, own_ref, vec_ref, grad_ref):
     unit, inv_sigma = normalize(x_ref[0])
-    unit_grad = own_ref[0].astype(F32) * gain_ref[...]
+    unit_grad = own_ref[0].astype(F32) * vec_ref[0:1]
     grad = cot_ref[0].astype(F32) + inv_sigma * (
         unit_grad
         - jnp.mean(unit_grad, axis=-1, keepdims=True)
@@ -460,17 +460,17 @@
     grad_ref[0] = grad.astype(BF16)
 
 
-def finish(x, cot, own, gain):
+def finish(x, cot, own, vectors):
     rows = pl.BlockSpec((1, x.shape[1] // 2, x.shape[2]), lambda s, t: (s, t, 0))
     return pl.pallas_call(
         finish_kernel,
         grid=(x.shape[0], 2),
-        in_specs=[rows, rows, rows, pl.BlockSpec(gain.shape, lambda *_: (0, 0))],
+        in_specs=[rows, rows, rows, whole(vectors)],
         out_specs=rows,
         out_shape=struct(*x.shape),
         cost_estimate=cost(20 * x.size, 8 * x.size),
         name="finish",
-    )(x, cot, own, gain)
+    )(x, cot, own, vectors)
 
 
 def weight_half(kernel, places, row, operands, got, blocks, part, shape, flops):
@@ -580,7 +580,7 @@
     small = jnp.pad(small, (0, padded - used)).reshape(-1, 128)
     small = gather_bits(small, dp, 0, ways[0]).reshape(dp, padded)
     norm_rows = small[:, : 3 * share].reshape(dp, 3, share).transpose(1, 0, 2).reshape(3, model)
-    gain, out_shift = norm_rows[0], norm_rows[2]
+    out_shift = norm_rows[2]
     at = 3 * share
     qkv_count = b_qkv.size
     qkv_bias = (
@@ -709,7 +709,7 @@
     at += qkv_count
     in_bias_out = small[at : at + b_in.size].reshape(b_in.shape)
 
-    input_grad = finish(inputs, cotangent, own_grad, gain.reshape(1, model))
+    input_grad = finish(inputs, cotangent, own_grad, norm_rows)
     return (
         outputs,
         input_grad,

time: 184 us -> 191 us (1.038)
  waiting for transfers between devices: 42.1 us -> 50.4 us
    reduce_scatter x1, waiting for transfers between devices: 0.01 us -> 7.65 us  [body(): lax.psum_scatter(branch.reshape(seqs, length, model), 'tensor', scatter_d...]
    unnamed x30 -> x34, local copies, waits for them, and re-layouts: 5.51 us -> 6.14 us
  transfers between devices with their start and end apart: 31 -> 31, of which waited for: 10 -> 10; matrix products, arithmetic and copies ran while one was open for 15% -> 12% of each run, Pallas kernels for 37% -> 24%
where the time goes in v5:
time: 191 us; the launch traced here: 190 us
  Pallas kernels  69.7 us (36%)
  waiting for transfers between devices  50.4 us (26%)
  starting transfers between devices  27.8 us (15%)
  local copies, waits for them, and re-layouts  16.5 us (9%)
  between operations  14.5 us (8%)
  other arithmetic  11.6 us (6%)
    ppermute x21, waiting for transfers between devices, swap(): return lax.ppermute(x, axis_name, [(i, i ^ step) for i in range(size)])  28.3 us
    pallas_call x4, Pallas kernels, weight_half(): pl.pallas_call(functools.partial(kernel, blocks, part, row), grid_spec=pl...  21.4 us
    ppermute x21, starting transfers between devices, swap(): return lax.ppermute(x, axis_name, [(i, i ^ step) for i in range(size)])  18.1 us
    all_gather x1, waiting for transfers between devices, body(): lax.all_gather(cotangent, 'tensor', axis=1, tiled=True).reshape(rows, model)  13.7 us
    pallas_call x1, Pallas kernels, attend_back(): pl.pallas_call(functools.partial(backward_kernel, scale, block), grid=(se...  10.9 us
    pallas_call x1, Pallas kernels, attend(): pl.pallas_call(functools.partial(forward_kernel, scale, block), grid=(seq...  8.36 us
    pallas_call x1, Pallas kernels, enter(): pl.pallas_call(functools.partial(enter_kernel, heads, head_dim, qkv_cols)...  7.96 us
    reduce_scatter x1, waiting for transfers between devices, body(): lax.psum_scatter(branch.reshape(seqs, length, model), 'tensor', scatter_d...  7.65 us
  transfers between devices with their start and end apart: 31, of which 10 were waited for; matrix products, arithmetic and copies ran while one was open for 12% of the time, Pallas kernels for 24%

profile of v5, /device:TPU:0, one launch (start us, length us, event | category | flops | bytes accessed | tf_op | source)
XLA Modules:
  0.0 190.4 jit_solution(15811121104918177187)
XLA Ops:
  9.4 5.1 %collective-permute-start.2 = (f32[3,24]{1,0:T(4,128)S(1)}, f32[3,24]{1,0:T(4,128)S(1)}, u32[]{:S(2)}, u32[]{:S(2)}) collective-permute-start(f32[3,24]{1,0:T(4,128)S(1)} %get-tuple-element.139), channel_id=1, source_target_pairs={{0,3},{1,0},{2,1},{3,2},{4,7},{5,4},{6,5},{7,6},{8,11},{9,8},{10,9... | collective-permute-start | bytes 872 | tf_op jit(solution)/shard_map/ppermute | solution.py:570
  25.1 4.2 %collective-permute-done.9 = bf16[96,1344]{1,0:T(8,128)(2,1)S(1)} collective-permute-done((bf16[96,1344]{1,0:T(8,128)(2,1)S(1)}, bf16[96,1344]{1,0:T(8,128)(2,1)S(1)}, u32[]{:S(2)}, u32[]{:S(2)}) %collective-permute-start.9) | collective-permute-done | bytes 258080 | tf_op jit(solution)/shard_map/ppermute | solution.py:27
  29.7 2.1 %collective-permute-start.4 = (f32[2,8,128]{2,1,0:T(8,128)S(1)}, f32[2,8,128]{2,1,0:T(8,128)S(1)}, u32[]{:S(2)}, u32[]{:S(2)}) collective-permute-start(f32[2,8,128]{2,1,0:T(8,128)S(1)} %pad_maximum_fusion.11), channel_id=1, source_target_pairs={{0,16},{4,20},{8,24},{12,28},{16,0},{20,4},{24,8},{28,12},{1,17},{... | collective-permute-start | bytes 24584 | tf_op jit(solution)/shard_map/ppermute | solution.py:27
  31.8 4.1 %collective-permute-done.7 = bf16[2,96,960]{2,1,0:T(8,128)(2,1)S(1)} collective-permute-done((bf16[2,96,960]{2,1,0:T(8,128)(2,1)S(1)}, bf16[2,96,960]{2,1,0:T(8,128)(2,1)S(1)}, u32[]{:S(2)}, u32[]{:S(2)}) %collective-permute-start.7) | collective-permute-done | bytes 368672 | tf_op jit(solution)/shard_map/ppermute | solution.py:27
  37.0 2.8 %collective-permute-done.10 = bf16[2,96,1344]{2,1,0:T(8,128)(2,1)S(1)} collective-permute-done((bf16[2,96,1344]{2,1,0:T(8,128)(2,1)S(1)}, bf16[2,96,1344]{2,1,0:T(8,128)(2,1)S(1)}, u32[]{:S(2)}, u32[]{:S(2)}) %collective-permute-start.10) | collective-permute-done | bytes 516128 | tf_op jit(solution)/shard_map/ppermute | solution.py:27
  51.4 8.0 %enter.1 = (bf16[1024,768]{1,0:T(8,128)(2,1)}, bf16[768,1024]{1,0:T(8,128)(2,1)}, bf16[576,1024]{1,0:T(8,128)(2,1)}, bf16[1024,768]{1,0:T(8,128)(2,1)}, f32[1024,768]{1,0:T(8,128)}) custom-call(bf16[1024,768]{1,0:T(8,128)(2,1)} %bitcast.156, f32[3,768]{1,0:T(4,128)} %reshape.182.vec_ref, f32[1,768]{1,0:T(1,128)} %reshape_reshape.16.in_bias_ref, ...), custom_call_target="tpu_custom_call" | custom-call | flops 2113929216 | bytes 12976128 | tf_op jit(solution)/shard_map/enter/pallas_call | solution.py:307
  59.4 8.4 %attend_forward.1 = (bf16[192,1024]{1,0:T(8,128)(2,1)}, bf16[1,3,1024,1024]{3,2,1,0:T(8,128)(2,1)}) custom-call(bf16[576,1024]{1,0:T(8,128)(2,1)} %get-tuple-element.41.q_ref.k_ref.v_ref, bf16[576,1024]{1,0:T(8,128)(2,1)} %get-tuple-element.41.q_ref.k_ref.v_ref, bf16[576,1024]{1,0:T(8,128)(2,1)} %get-tuple-element.41.q_ref.k_ref.v_ref), custom_call_target="tpu_custom_call" | custom-call | flops 805306368 | bytes 2359296 | tf_op jit(solution)/shard_map/attend_forward/pallas_call | solution.py:339
  67.8 5.4 %branch.1 = (bf16[1024,768]{1,0:T(8,128)(2,1)}, bf16[1024,192]{1,0:T(8,128)(2,1)}) custom-call(bf16[192,1024]{1,0:T(8,128)(2,1)} %get-tuple-element.42.ctx_t_ref, bf16[1024,768]{1,0:T(8,128)(2,1)} %get-tuple-element.43.hidden_ref, bf16[768,960]{1,0:T(8,128)(2,1)} %bitcast.116, bf16[768,1344]{1,0:T(8,128)(2,1)} %bitcast.112), custom_call_target="tpu_custom_call" | custom-call | flops 1509949440 | bytes 6291456 | tf_op jit(solution)/shard_map/branch/pallas_call | solution.py:384
  73.2 13.7 %all-gather.5.cloned.1.call-done = bf16[1,1024,768]{2,1,0:T(8,128)(2,1)} async-done(((bf16[1,256,768]{2,1,0:T(8,128)(2,1)}), bf16[1,1024,768]{2,1,0:T(8,128)(2,1)}) %all-gather.5.cloned.1.call-update) | async-done | bytes 1572880 | tf_op jit(solution)/shard_map/all_gather | solution.py:564
  86.9 6.2 %return_grads.1 = (bf16[768,1024]{1,0:T(8,128)(2,1)}, bf16[192,1024]{1,0:T(8,128)(2,1)}, bf16[1024,768]{1,0:T(8,128)(2,1)}, f32[8,768]{1,0:T(8,128)}, f32[8,768]{1,0:T(8,128)}) custom-call(bf16[1024,192]{1,0:T(8,128)(2,1)} %get-tuple-element.47.after_ref.ctx_ref, s32[4]{0:T(128)} %pad_add_fusion.places_ref.at_ref, bf16[1024,768]{1,0:T(8,128)(2,1)} %bitcast.119, ...), custom_call_target="tpu_custom_call" | custom-call | flops 1509949440 | bytes 7864320 | tf_op jit(solution)/shard_map/return_grads/pallas_call | solution.py:403
  93.1 10.9 %attend_backward.1 = (bf16[192,1024]{1,0:T(8,128)(2,1)}, bf16[192,1024]{1,0:T(8,128)(2,1)}, bf16[192,1024]{1,0:T(8,128)(2,1)}, f32[1,3,3,64,128]{4,3,2,1,0:T(8,128)}) custom-call(bf16[576,1024]{1,0:T(8,128)(2,1)} %get-tuple-element.41.q_ref.k_ref.v_ref, bf16[576,1024]{1,0:T(8,128)(2,1)} %get-tuple-element.41.q_ref.k_ref.v_ref, ...), custom_call_target="tpu_custom_call" | custom-call | flops 2013265920 | bytes 3538944 | tf_op jit(solution)/shard_map/attend_backward/pallas_call | solution.py:365
  103.9 7.1 %norm_grads.1 = (bf16[1024,576]{1,0:T(8,128)(2,1)}, bf16[1024,768]{1,0:T(8,128)(2,1)}, f32[8,768]{1,0:T(8,128)}, f32[8,768]{1,0:T(8,128)}) custom-call(bf16[1024,768]{1,0:T(8,128)(2,1)} %get-tuple-element.45.unit_ref, bf16[192,1024]{1,0:T(8,128)(2,1)} %get-tuple-element.50.dq_ref, bf16[192,1024]{1,0:T(8,128)(2,1)} %get-tuple-element.51.dk_ref, ...), custom_call_target="tpu_custom_call" | custom-call | flops 2113929216 | bytes 6291456 | tf_op jit(solution)/shard_map/norm_grads/pallas_call | solution.py:431
  115.4 6.5 %shard_map.196 = bf16[4,96,1728]{2,1,0:T(8,128)(2,1)} custom-call(s32[4]{0:T(128)} %pad_add_fusion.places_ref.at_ref, bf16[768,1024]{1,0:T(8,128)(2,1)} %get-tuple-element.60.normed_t_ref, bf16[768,1024]{1,0:T(8,128)(2,1)} %get-tuple-element.66.cot_t_ref, bf16[1024,768]{1,0:T(8,128)(2,1)} %get-tuple-element.53.pre_low_ref, ...), custom_call_target="tpu_custom_call" | custom-call | flops 1358954496 | bytes 3145728 | tf_op jit(solution)/shard_map/pallas_call | solution.py:482
  123.4 2.5 %collective-permute-done.15 = f32[4,256]{1,0:T(4,128)S(1)} collective-permute-done((f32[4,256]{1,0:T(4,128)S(1)}, f32[4,256]{1,0:T(4,128)S(1)}, u32[]{:S(2)}, u32[]{:S(2)}) %collective-permute-start.15) | collective-permute-done | bytes 4128 | tf_op jit(solution)/shard_map/ppermute | solution.py:27
  125.9 2.5 %collective-permute-start.18 = (f32[256]{0:T(256)S(1)}, f32[256]{0:T(256)S(1)}, u32[]{:S(2)}, u32[]{:S(2)}) collective-permute-start(f32[256]{0:T(256)S(1)} %bitcast.153), channel_id=1, source_target_pairs={{0,24},{4,28},{8,16},{12,20},{16,8},{20,12},{24,0},{28,4},{1,25},{... | collective-permute-start | bytes 3080 | tf_op jit(solution)/shard_map/ppermute | solution.py:27
  129.5 4.1 %shard_map.194 = bf16[4,96,576]{2,1,0:T(8,128)(2,1)} custom-call(s32[4]{0:T(128)} %pad_add_fusion.places_ref.at_ref, bf16[768,1024]{1,0:T(8,128)(2,1)} %get-tuple-element.60.normed_t_ref, bf16[1024,576]{1,0:T(8,128)(2,1)} %get-tuple-element.61.proj_low_ref), custom_call_target="tpu_custom_call" | custom-call | flops 452984832 | bytes 3145728 | tf_op jit(solution)/shard_map/pallas_call | solution.py:482
  136.4 4.1 %shard_map.195 = (f32[96,576]{1,0:T(8,128)}, bf16[96,576]{1,0:T(8,128)(2,1)}, bf16[96,576]{1,0:T(8,128)(2,1)}, bf16[96,576]{1,0:T(8,128)(2,1)}) custom-call(s32[4]{0:T(128)} %pad_add_fusion.places_ref.at_ref, bf16[768,1024]{1,0:T(8,128)(2,1)} %get-tuple-element.60.normed_t_ref, bf16[1024,576]{1,0:T(8,128)(2,1)} %get-tuple-element.61.proj_low_ref, ...), custom_call_target="tpu_custom_call" | custom-call | flops 452984832 | bytes 3145728 | tf_op jit(solution)/shard_map/pallas_call | solution.py:482
  140.5 2.4 %collective-permute-start.22 = (bf16[96,576]{1,0:T(8,128)(2,1)}, bf16[96,576]{1,0:T(8,128)(2,1)S(1)}, u32[]{:S(2)}, u32[]{:S(2)}) collective-permute-start(bf16[96,576]{1,0:T(8,128)(2,1)} %get-tuple-element.65), channel_id=1, source_target_pairs={{0,24},{4,28},{8,16},{12,20},{16,8},{20,12},{24,0},{28,4},{1,25},{... | collective-permute-start | bytes 331784 | tf_op jit(solution)/shard_map/ppermute | solution.py:27
  145.1 6.7 %shard_map.197 = (f32[96,1728]{1,0:T(8,128)}, bf16[96,1728]{1,0:T(8,128)(2,1)}, bf16[96,1728]{1,0:T(8,128)(2,1)}, bf16[96,1728]{1,0:T(8,128)(2,1)}) custom-call(s32[4]{0:T(128)} %pad_add_fusion.places_ref.at_ref, bf16[768,1024]{1,0:T(8,128)(2,1)} %get-tuple-element.60.normed_t_ref, bf16[768,1024]{1,0:T(8,128)(2,1)} %get-tuple-element.66.cot_t_ref, ...), custom_call_target="tpu_custom_call" | custom-call | flops 1358954496 | bytes 3145728 | tf_op jit(solution)/shard_map/pallas_call | solution.py:482
  151.9 2.4 %collective-permute-start.26 = (bf16[96,1728]{1,0:T(8,128)(2,1)}, bf16[96,1728]{1,0:T(8,128)(2,1)S(1)}, u32[]{:S(2)}, u32[]{:S(2)}) collective-permute-start(bf16[96,1728]{1,0:T(8,128)(2,1)} %get-tuple-element.70), channel_id=1, source_target_pairs={{0,24},{4,28},{8,16},{12,20},{16,8},{20,12},{24,0},{28,4},{1,25},{... | collective-permute-start | bytes 995336 | tf_op jit(solution)/shard_map/ppermute | solution.py:27
  157.0 6.9 %collective-permute-done.26 = bf16[96,1728]{1,0:T(8,128)(2,1)S(1)} collective-permute-done((bf16[96,1728]{1,0:T(8,128)(2,1)}, bf16[96,1728]{1,0:T(8,128)(2,1)S(1)}, u32[]{:S(2)}, u32[]{:S(2)}) %collective-permute-start.26) | collective-permute-done | bytes 331808 | tf_op jit(solution)/shard_map/ppermute | solution.py:27
  163.9 6.1 %collective-permute-done.25 = bf16[96,1728]{1,0:T(8,128)(2,1)S(1)} collective-permute-done((bf16[96,1728]{1,0:T(8,128)(2,1)}, bf16[96,1728]{1,0:T(8,128)(2,1)S(1)}, u32[]{:S(2)}, u32[]{:S(2)}) %collective-permute-start.25) | collective-permute-done | bytes 331808 | tf_op jit(solution)/shard_map/ppermute | solution.py:27
  171.9 2.5 %finish.1 = bf16[1,256,768]{2,1,0:T(8,128)(2,1)} custom-call(bf16[1,256,768]{2,1,0:T(8,128)(2,1)} %x_ref.1, bf16[1,256,768]{2,1,0:T(8,128)(2,1)} %cot_ref.1, bf16[1,256,768]{2,1,0:T(8,128)(2,1)} %reduce-scatter.5.cloned.1.call-done.own_ref, f32[3,768]{1,0:T(4,128)} %reshape.182.vec_ref), custom_call_target="tpu_custom_call" | custom-call | flops 3932160 | bytes 1572864 | tf_op jit(solution)/shard_map/finish/pallas_call | solution.py:465
  174.4 7.7 %reduce-scatter.3.cloned.1.call-done = bf16[1,256,768]{2,1,0:T(8,128)(2,1)} async-done(((bf16[1,1024,768]{2,1,0:T(8,128)(2,1)}), bf16[1,256,768]{2,1,0:T(8,128)(2,1)}) %reduce-scatter.3.cloned.1.call-update) | async-done | bytes 393232 | tf_op jit(solution)/shard_map/reduce_scatter | solution.py:615
  (176 shorter events, 43.7 us)
Async XLA Ops:
  7.2 44.2 %all-gather.3.cloned.1.call-start = ((), (), s32[]{:S(2)}) async-start(), calls=%async_computation.2 | async-start | bytes 1966080 | tf_op jit(solution)/shard_map/all_gather | solution.py:563
  8.0 78.9 %all-gather.5.cloned.1.call-start = ((), (), s32[]{:S(2)}) async-start(), calls=%async_computation.4 | async-start | bytes 1966080 | tf_op jit(solution)/shard_map/all_gather | solution.py:564
  9.4 13.6 %collective-permute-start.2 = (f32[3,24]{1,0:T(4,128)S(1)}, f32[3,24]{1,0:T(4,128)S(1)}, u32[]{:S(2)}, u32[]{:S(2)}) collective-permute-start(f32[3,24]{1,0:T(4,128)S(1)} %get-tuple-element.139), channel_id=1, source_target_pairs={{0,3},{1,0},{2,1},{3,2},{4,7},{5,4},{6,5},{7,6},{8,11},{9,8},{10,9... | collective-permute-start | bytes 872 | tf_op jit(solution)/shard_map/ppermute | solution.py:570
  14.6 8.5 %collective-permute-start.1 = (f32[3,24]{1,0:T(4,128)S(1)}, f32[3,24]{1,0:T(4,128)S(1)}, u32[]{:S(2)}, u32[]{:S(2)}) collective-permute-start(f32[3,24]{1,0:T(4,128)S(1)} %get-tuple-element.139), channel_id=1, source_target_pairs={{0,2},{1,3},{2,0},{3,1},{4,6},{5,7},{6,4},{7,5},{8,10},{9,11},{10,... | collective-permute-start | bytes 872 | tf_op jit(solution)/shard_map/ppermute | solution.py:570
  14.6 8.5 %collective-permute-start = (f32[3,24]{1,0:T(4,128)S(1)}, f32[3,24]{1,0:T(4,128)S(1)}, u32[]{:S(2)}, u32[]{:S(2)}) collective-permute-start(f32[3,24]{1,0:T(4,128)S(1)} %get-tuple-element.139), channel_id=1, source_target_pairs={{0,1},{1,2},{2,3},{3,0},{4,5},{5,6},{6,7},{7,4},{8,9},{9,10},{10,1... | collective-permute-start | bytes 872 | tf_op jit(solution)/shard_map/ppermute | solution.py:570
  20.2 9.2 %collective-permute-start.9 = (bf16[96,1344]{1,0:T(8,128)(2,1)S(1)}, bf16[96,1344]{1,0:T(8,128)(2,1)S(1)}, u32[]{:S(2)}, u32[]{:S(2)}) collective-permute-start(bf16[96,1344]{1,0:T(8,128)(2,1)S(1)} %pad_maximum_fusion.6), channel_id=1, source_target_pairs={{0,16},{4,20},{8,24},{12,28},{16,0},{20,4},{24,8},{28,12},{1,17},{... | collective-permute-start | bytes 774152 | tf_op jit(solution)/shard_map/ppermute | solution.py:27
  21.8 150.0 %reduce-scatter.5.cloned.1.call-start = ((), (), s32[]{:S(2)}) async-start(), calls=%async_computation.5 | async-start | bytes 1966080 | tf_op jit(solution)/shard_map/reduce_scatter | solution.py:657
  24.6 11.3 %collective-permute-start.7 = (bf16[2,96,960]{2,1,0:T(8,128)(2,1)S(1)}, bf16[2,96,960]{2,1,0:T(8,128)(2,1)S(1)}, u32[]{:S(2)}, u32[]{:S(2)}) collective-permute-start(bf16[2,96,960]{2,1,0:T(8,128)(2,1)S(1)} %pad_maximum_fusion.5), channel_id=1, source_target_pairs={{0,16},{4,20},{8,24},{12,28},{16,0},{20,4},{24,8},{28,12},{1,17},{... | collective-permute-start | bytes 1105928 | tf_op jit(solution)/shard_map/ppermute | solution.py:27
  29.6 10.2 %collective-permute-start.10 = (bf16[2,96,1344]{2,1,0:T(8,128)(2,1)S(1)}, bf16[2,96,1344]{2,1,0:T(8,128)(2,1)S(1)}, u32[]{:S(2)}, u32[]{:S(2)}) collective-permute-start(bf16[2,96,1344]{2,1,0:T(8,128)(2,1)S(1)} %pad_maximum_fusion.4), channel_id=1, source_target_pairs={{0,8},{4,12},{8,0},{12,4},{16,24},{20,28},{24,16},{28,20},{1,9},{5... | collective-permute-start | bytes 1548296 | tf_op jit(solution)/shard_map/ppermute | solution.py:27
  29.7 10.4 %collective-permute-start.4 = (f32[2,8,128]{2,1,0:T(8,128)S(1)}, f32[2,8,128]{2,1,0:T(8,128)S(1)}, u32[]{:S(2)}, u32[]{:S(2)}) collective-permute-start(f32[2,8,128]{2,1,0:T(8,128)S(1)} %pad_maximum_fusion.11), channel_id=1, source_target_pairs={{0,16},{4,20},{8,24},{12,28},{16,0},{20,4},{24,8},{28,12},{1,17},{... | collective-permute-start | bytes 24584 | tf_op jit(solution)/shard_map/ppermute | solution.py:27
  37.0 8.5 %collective-permute-start.8 = (bf16[2,2,96,960]{3,2,1,0:T(8,128)(2,1)}, bf16[2,2,96,960]{3,2,1,0:T(8,128)(2,1)}, u32[]{:S(2)}, u32[]{:S(2)}) collective-permute-start(bf16[2,2,96,960]{3,2,1,0:T(8,128)(2,1)} %pad_maximum_fusion.3), channel_id=1, source_target_pairs={{0,4},{4,0},{8,12},{12,8},{16,20},{20,16},{24,28},{28,24},{1,5},{5... | collective-permute-start | bytes 2211848 | tf_op jit(solution)/shard_map/ppermute | solution.py:27
  40.0 8.2 %collective-permute-start.11 = (bf16[2,2,96,1344]{3,2,0,1:T(8,128)(2,1)S(1)}, bf16[2,2,96,1344]{3,2,0,1:T(8,128)(2,1)}, u32[]{:S(2)}, u32[]{:S(2)}) collective-permute-start(bf16[2,2,96,1344]{3,2,0,1:T(8,128)(2,1)S(1)} %pad_maximum_fusion.2), channel_id=1, source_target_pairs={{0,4},{4,0},{8,12},{12,8},{16,20},{20,16},{24,28},{28,24},{1,5},{5... | collective-permute-start | bytes 3096584 | tf_op jit(solution)/shard_map/ppermute | solution.py:27
  111.0 71.0 %reduce-scatter.3.cloned.1.call-start = ((), (), s32[]{:S(2)}) async-start(), calls=%async_computation.3 | async-start | bytes 1966080 | tf_op jit(solution)/shard_map/reduce_scatter | solution.py:615
  111.9 10.6 %collective-permute-start.14 = (f32[2,8,24]{2,1,0:T(8,128)S(1)}, f32[2,8,24]{2,1,0:T(8,128)S(1)}, u32[]{:S(2)}, u32[]{:S(2)}) collective-permute-start(f32[2,8,24]{2,1,0:T(8,128)S(1)} %bitcast.145), channel_id=1, source_target_pairs={{0,3},{1,0},{2,1},{3,2},{4,7},{5,4},{6,5},{7,6},{8,11},{9,8},{10,9... | collective-permute-start | bytes 4616 | tf_op jit(solution)/shard_map/ppermute | solution.py:667
  113.3 9.3 %collective-permute-start.13 = (f32[2,8,24]{2,1,0:T(8,128)S(1)}, f32[2,8,24]{2,1,0:T(8,128)S(1)}, u32[]{:S(2)}, u32[]{:S(2)}) collective-permute-start(f32[2,8,24]{2,1,0:T(8,128)S(1)} %bitcast.144), channel_id=1, source_target_pairs={{0,2},{1,3},{2,0},{3,1},{4,6},{5,7},{6,4},{7,5},{8,10},{9,11},{10,... | collective-permute-start | bytes 4616 | tf_op jit(solution)/shard_map/ppermute | solution.py:667
  114.0 8.6 %collective-permute-start.12 = (f32[2,8,24]{2,1,0:T(8,128)S(1)}, f32[2,8,24]{2,1,0:T(8,128)S(1)}, u32[]{:S(2)}, u32[]{:S(2)}) collective-permute-start(f32[2,8,24]{2,1,0:T(8,128)S(1)} %bitcast.143), channel_id=1, source_target_pairs={{0,1},{1,2},{2,3},{3,0},{4,5},{5,6},{6,7},{7,4},{8,9},{9,10},{10,1... | collective-permute-start | bytes 4616 | tf_op jit(solution)/shard_map/ppermute | solution.py:667
  122.5 21.5 %collective-permute-start.23 = (bf16[4,96,1728]{2,1,0:T(8,128)(2,1)}, bf16[4,96,1728]{2,1,0:T(8,128)(2,1)S(1)}, u32[]{:S(2)}, u32[]{:S(2)}) collective-permute-start(bf16[4,96,1728]{2,1,0:T(8,128)(2,1)} %shard_map.196), channel_id=1, source_target_pairs={{0,4},{4,0},{8,12},{12,8},{16,20},{20,16},{24,28},{28,24},{1,5},{5... | collective-permute-start | bytes 3981320 | tf_op jit(solution)/shard_map/ppermute | solution.py:27
  125.9 7.6 %collective-permute-start.18 = (f32[256]{0:T(256)S(1)}, f32[256]{0:T(256)S(1)}, u32[]{:S(2)}, u32[]{:S(2)}) collective-permute-start(f32[256]{0:T(256)S(1)} %bitcast.153), channel_id=1, source_target_pairs={{0,24},{4,28},{8,16},{12,20},{16,8},{20,12},{24,0},{28,4},{1,25},{... | collective-permute-start | bytes 3080 | tf_op jit(solution)/shard_map/ppermute | solution.py:27
  140.5 14.3 %collective-permute-start.22 = (bf16[96,576]{1,0:T(8,128)(2,1)}, bf16[96,576]{1,0:T(8,128)(2,1)S(1)}, u32[]{:S(2)}, u32[]{:S(2)}) collective-permute-start(bf16[96,576]{1,0:T(8,128)(2,1)} %get-tuple-element.65), channel_id=1, source_target_pairs={{0,24},{4,28},{8,16},{12,20},{16,8},{20,12},{24,0},{28,4},{1,25},{... | collective-permute-start | bytes 331784 | tf_op jit(solution)/shard_map/ppermute | solution.py:27
  142.9 13.0 %collective-permute-start.21 = (bf16[96,576]{1,0:T(8,128)(2,1)}, bf16[96,576]{1,0:T(8,128)(2,1)S(1)}, u32[]{:S(2)}, u32[]{:S(2)}) collective-permute-start(bf16[96,576]{1,0:T(8,128)(2,1)} %get-tuple-element.64), channel_id=1, source_target_pairs={{0,16},{4,20},{8,24},{12,28},{16,0},{20,4},{24,8},{28,12},{1,17},{... | collective-permute-start | bytes 331784 | tf_op jit(solution)/shard_map/ppermute | solution.py:27
  143.5 12.4 %collective-permute-start.20 = (bf16[96,576]{1,0:T(8,128)(2,1)}, bf16[96,576]{1,0:T(8,128)(2,1)S(1)}, u32[]{:S(2)}, u32[]{:S(2)}) collective-permute-start(bf16[96,576]{1,0:T(8,128)(2,1)} %get-tuple-element.63), channel_id=1, source_target_pairs={{0,8},{4,12},{8,0},{12,4},{16,24},{20,28},{24,16},{28,20},{1,9},{5... | collective-permute-start | bytes 331784 | tf_op jit(solution)/shard_map/ppermute | solution.py:27
  151.9 12.1 %collective-permute-start.26 = (bf16[96,1728]{1,0:T(8,128)(2,1)}, bf16[96,1728]{1,0:T(8,128)(2,1)S(1)}, u32[]{:S(2)}, u32[]{:S(2)}) collective-permute-start(bf16[96,1728]{1,0:T(8,128)(2,1)} %get-tuple-element.70), channel_id=1, source_target_pairs={{0,24},{4,28},{8,16},{12,20},{16,8},{20,12},{24,0},{28,4},{1,25},{... | collective-permute-start | bytes 995336 | tf_op jit(solution)/shard_map/ppermute | solution.py:27
  154.3 15.7 %collective-permute-start.25 = (bf16[96,1728]{1,0:T(8,128)(2,1)}, bf16[96,1728]{1,0:T(8,128)(2,1)S(1)}, u32[]{:S(2)}, u32[]{:S(2)}) collective-permute-start(bf16[96,1728]{1,0:T(8,128)(2,1)} %get-tuple-element.69), channel_id=1, source_target_pairs={{0,16},{4,20},{8,24},{12,28},{16,0},{20,4},{24,8},{28,12},{1,17},{... | collective-permute-start | bytes 995336 | tf_op jit(solution)/shard_map/ppermute | solution.py:27
  154.8 15.3 %collective-permute-start.24 = (bf16[96,1728]{1,0:T(8,128)(2,1)}, bf16[96,1728]{1,0:T(8,128)(2,1)S(1)}, u32[]{:S(2)}, u32[]{:S(2)}) collective-permute-start(bf16[96,1728]{1,0:T(8,128)(2,1)} %get-tuple-element.68), channel_id=1, source_target_pairs={{0,8},{4,12},{8,0},{12,4},{16,24},{20,28},{24,16},{28,20},{1,9},{5... | collective-permute-start | bytes 995336 | tf_op jit(solution)/shard_map/ppermute | solution.py:27
  (21 other events, 156.7 us)
Sparse Core Ops, SparseCore 0:
  9.6 39.7 all-gather.2
  50.9 35.8 all-gather.4
  111.2 34.2 reduce-scatter.4
  147.7 34.2 reduce-scatter.2
